TPU v7x, 768 devices: a whole 4x8x12 slice. The times are simulated.
768 devices in a mesh: fsdp: 192 (over z, y, core), row: 4 (over x).
Axes of the slice: x: 4, y: 8, z: 12, core: 2. Of those that a mesh axis runs over, the one named last changes fastest.
Arguments:
- factor: float32 [3072, 3072], P('fsdp', 'row'), may hold values from -1 to 17, as said below
- gradient: bfloat16 [3072, 3840], P('row', 'fsdp'), may hold values from -0.125 to 0.125
- sketch_ids: int32 [3072, 256], P('row'), may hold values from -3 to 3
Outputs:
- factor_new: float32 [3072, 3072], P('fsdp', 'row')
- range_basis: float32 [3072, 256], P('fsdp')
- projected_core: float32 [256, 256], replicated
Inputs may be any that keep to these rules, and one draw needn't show every extreme that they name: `factor`: symmetric.
All inputs are finite; a program needn't handle non-finite values.
Results may differ from a plain program's by a relative error of at most 0.0003.
Values may be sent and summed in bfloat16 or wider, within the bound.
No kernel may reach another device: no remote copies, remote signals or barrier semaphores. Data moves between devices by JAX's collectives and lax.ppermute only.
A program may use at most 64 MiB of HBM per device.

v0:
```python
import jax
import jax.numpy as jnp
from jax import lax
from jax.sharding import PartitionSpec as P

B = 3072


decay_rate = 0.9


def from_root(block, axis, owner):
    block = jnp.where(lax.axis_index(axis) == owner, block, jnp.zeros_like(block))
    return lax.psum(block, axis)


def shards(factor, gradient, sketch_ids):
    highest = lax.Precision.HIGHEST
    rows_here = factor.shape[0]
    cols_here = factor.shape[1]
    row_pos = lax.axis_index("row")
    fsdp_pos = lax.axis_index("fsdp")
    contract_last = (((1,), (1,)), ((), ()))
    block_rows = lax.all_gather(gradient, "fsdp", axis=1, tiled=True)
    owner = fsdp_pos * rows_here // cols_here
    local_start = jnp.clip(fsdp_pos * rows_here - row_pos * cols_here, 0, cols_here - rows_here)
    own_slice = lax.dynamic_slice_in_dim(block_rows, local_start, rows_here, 0)
    own_slice = from_root(own_slice, "row", owner)
    outer_sum = lax.dot_general(
        own_slice, block_rows, contract_last, preferred_element_type=jnp.float32
    )
    factor_new = decay_rate * factor + outer_sum
    sketch = sketch_ids.astype(jnp.float32)
    ranged = lax.psum(jnp.dot(factor_new, sketch, precision=highest), "row")
    gram_matrix = lax.psum(jnp.dot(ranged.T, ranged, precision=highest), "fsdp") / B
    lower_factor = jnp.linalg.cholesky(gram_matrix)
    range_basis = jax.scipy.linalg.solve_triangular(lower_factor, ranged.T, lower=True).T
    gathered_piece = lax.all_gather(range_basis, "fsdp", axis=0, tiled=True)
    local_cols = jnp.arange(gathered_piece.shape[0], dtype=jnp.int32) - row_pos * cols_here
    inside = ((local_cols >= 0) & (local_cols < cols_here)).astype(jnp.float32)
    picked = jnp.take(factor_new, jnp.clip(local_cols, 0, cols_here - 1), axis=1) * inside[None, :]
    applied = jnp.dot(picked, gathered_piece, precision=highest)
    core_term = jnp.dot(range_basis.T, applied, precision=highest)
    projected_core = lax.psum(core_term, ("fsdp", "row")) / B
    return (factor_new, range_basis, projected_core)


def solution(mesh):
    return jax.shard_map(
        shards,
        mesh=mesh,
        in_specs=(P("fsdp", "row"), P("row", "fsdp"), P("row", None)),
        out_specs=(P("fsdp", "row"), P("fsdp", None), P()),
        check_vma=False,
    )
```

profile of v0, /device:TPU:1, one launch (start us, length us, event | category | flops | bytes accessed | tf_op | source)
XLA Modules:
  0.0 1182.0 jit_solution(6455109773613980412)
XLA Ops:
  8.0 137.6 %all-gather.6.cloned.1.call-done = bf16[192,20,768]{2,1,0:T(8,128)(2,1)} async-done(((bf16[1,20,768]{2,1,0:T(8,128)(2,1)}), bf16[192,20,768]{2,1,0:T(8,128)(2,1)}) %all-gather.6.cloned.1.call-update) | async-done | bytes 5898256 | tf_op jit(solution)/shard_map/all_gather | solution.py:24
  145.6 9.7 reshape.85
  155.3 3.0 select_bitcast_fusion
  158.3 56.9 %all-reduce.5.cloned.1.call-done = bf16[16,3840]{0,1:T(8,128)(2,1)} async-done(((bf16[16,3840]{0,1:T(8,128)(2,1)}), bf16[16,3840]{0,1:T(8,128)(2,1)}) %all-reduce.5.cloned.1.call-update) | async-done | bytes 122896 | tf_op jit(solution)/shard_map/psum | solution.py:14
  215.3 3.9 convolution_add_fusion
  219.6 12.7 %psum.29 = f32[16,256]{1,0:T(8,128)S(1)} all-reduce(f32[16,256]{1,0:T(8,128)S(1)} %fusion.5), channel_id=1, replica_groups=mesh['fsdp'=192,'row'=4] {'row'}, use_global_device_ids=true, to_apply=%region_1.2 | all-reduce | flops 4096 | bytes 32768 | tf_op jit(solution)/shard_map/psum | solution.py:34
  232.3 1.1 fusion.28
  233.7 291.4 %all-reduce.7.cloned.1.call-done = f32[256,256]{0,1:T(8,128)} async-done(((f32[256,256]{0,1:T(8,128)}), f32[256,256]{0,1:T(8,128)}) %all-reduce.7.cloned.1.call-update) | async-done | bytes 262160 | tf_op jit(solution)/shard_map/psum | solution.py:35
  525.1 1.0 broadcast_multiply_fusion.1
  526.2 1.0 fusion.8
  527.2 11.7 cholesky.50
  539.0 9.8 custom-call.15
  549.3 11.7 cholesky.105
  563.1 4.1 while.1
  563.9 1.4 bitcast_dynamic-update-slice_fusion.2
  565.9 1.4 bitcast_dynamic-update-slice_fusion.2
  567.3 19.7 %custom-call.16 = f32[2,128,128]{1,2,0:T(8,128)S(1)} custom-call(f32[2,128,128]{2,1,0:T(8,128)S(1)} %get-tuple-element.10), custom_call_target="InvertDiagBlocksLowerTriangular" | custom-call | tf_op jit(solution)/shard_map/jit(_solve_triangular)/triangular_solve | solution.py:37
  588.5 8.1 gather_fusion
  596.6 110.3 %all-gather.4.cloned.1.call-done = f32[3072,256]{1,0:T(8,128)} async-done(((f32[16,256]{1,0:T(8,128)}), f32[3072,256]{1,0:T(8,128)}) %all-gather.4.cloned.1.call-update) | async-done | bytes 3145744 | tf_op jit(solution)/shard_map/all_gather | solution.py:38
  706.9 5.9 fusion
  712.8 1.1 fusion.15
  713.9 459.8 %all-reduce.9.cloned.1.call-done = f32[256,256]{0,1:T(8,128)} async-done(((f32[256,256]{0,1:T(8,128)}), f32[256,256]{0,1:T(8,128)}) %all-reduce.9.cloned.1.call-update) | async-done | bytes 262160 | tf_op jit(solution)/shard_map/psum | solution.py:44
  1173.7 1.0 broadcast_multiply_fusion
  1174.7 0.8 copy.20
  (41 shorter events, 5.6 us)
Async XLA Ops:
  7.2 138.4 %all-gather.6.cloned.1.call-start = ((), (), s32[]{:S(2)}) async-start(), calls=%async_computation.4 | async-start | bytes 7114752 | tf_op jit(solution)/shard_map/all_gather | solution.py:24
  7.9 207.4 %all-reduce.5.cloned.1.call-start = ((), (), s32[]{:S(2)}) async-start(), calls=%async_computation | async-start | bytes 1966080 | tf_op jit(solution)/shard_map/psum | solution.py:14
  8.0 207.3 %copy-start.2 = (f32[16,768]{1,0:T(8,128)S(1)}, f32[16,768]{1,0:T(8,128)}, u32[]{:S(2)}) copy-start(f32[16,768]{1,0:T(8,128)} %param.3) | copy-start | bytes 147460
  158.3 60.9 %copy-start = (s32[768,256]{1,0:T(8,128)S(1)}, s32[768,256]{1,0:T(8,128)}, u32[]{:S(2)}) copy-start(s32[768,256]{1,0:T(8,128)} %param.5) | copy-start | bytes 2359300
  158.3 366.8 %all-reduce.7.cloned.1.call-start = ((), (), s32[]{:S(2)}) async-start(), calls=%async_computation.1 | async-start | bytes 524288 | tf_op jit(solution)/shard_map/psum | solution.py:35
  219.2 369.3 %copy-start.1 = (f32[16,768]{1,0:T(8,128)}, f32[16,768]{1,0:T(8,128)S(1)}, u32[]{:S(2)}) copy-start(f32[16,768]{1,0:T(8,128)S(1)} %convolution_add_fusion) | copy-start | bytes 147460
  233.4 473.4 %all-gather.4.cloned.1.call-start = ((), (), s32[]{:S(2)}) async-start(), calls=%async_computation.2 | async-start | bytes 3162112 | tf_op jit(solution)/shard_map/all_gather | solution.py:38
  588.2 585.5 %all-reduce.9.cloned.1.call-start = ((), (), s32[]{:S(2)}) async-start(), calls=%async_computation.3 | async-start | bytes 524288 | tf_op jit(solution)/shard_map/psum | solution.py:44
Sparse Core Ops, SparseCore 0:
  11.8 133.7 all-gather.5
  158.4 56.8 all-reduce.4
  233.5 291.5 all-reduce.6
  588.3 118.5 all-gather.3
  714.0 459.5 all-reduce.8
where the time goes:
time: 1180 us
  waiting for transfers between devices  1060 us (90%)
  other arithmetic  60.3 us (5%)
  local copies, waits for them, and re-layouts  23 us (2%)
  between operations  15.3 us (1%)
  matrix products  13.5 us (1%)
  blocking collectives  12.7 us (1%)
    psum x1, waiting for transfers between devices, shards(): projected_core = lax.psum(core_term, ('fsdp', 'row')) / B  460 us
    psum x1, waiting for transfers between devices, shards(): lax.psum(jnp.dot(ranged.T, ranged, precision=highest), 'fsdp') / B  291 us
    all_gather x1, waiting for transfers between devices, shards(): block_rows = lax.all_gather(gradient, 'fsdp', axis=1, tiled=True)  138 us
    all_gather x1, waiting for transfers between devices, shards(): gathered_piece = lax.all_gather(range_basis, 'fsdp', axis=0, tiled=True)  110 us
    psum x1, waiting for transfers between devices, from_root(): return lax.psum(block, axis)  56.9 us
    another operation x6, other arithmetic, shards(): lower_factor = jnp.linalg.cholesky(gram_matrix)  34 us
  transfers between devices with their start and end apart: 5, of which 5 were waited for; matrix products, arithmetic and copies ran while one was open for 1% of the time, Pallas kernels for 0%

commit v1 on v0

v1 whole, which is shorter than its diff:
```python
import jax
import jax.numpy as jnp
from jax import lax
from jax.sharding import Mesh, PartitionSpec as P

B = 3072
decay_rate = 0.9
NZ, NY, NC, NX = 12, 8, 2, 4
ALL = ("z", "y", "c", "x")
F32 = jnp.float32
HI = lax.Precision.HIGHEST


def dot(a, b, ca, cb):
    return lax.dot_general(a, b, (((ca,), (cb,)), ((), ())), precision=HI, preferred_element_type=F32)


def spread(v, axis, n):
    return lax.all_to_all(jnp.broadcast_to(v[None], (n,) + v.shape), axis, 0, 0)


def swap_core(v):
    return lax.ppermute(v, "c", [(0, 1), (1, 0)])


def scatter_core(v, core):
    half = v.shape[0] // 2
    mine = lax.dynamic_slice_in_dim(v, core * half, half, 0)
    other = lax.dynamic_slice_in_dim(v, (1 - core) * half, half, 0)
    return mine + swap_core(other)


def scatter(v, axis, n):
    return jnp.sum(lax.all_to_all(v.reshape(n, v.shape[0] // n, v.shape[1]), axis, 0, 0), axis=0)


def join(v):
    return v.reshape(v.shape[0] * v.shape[1], v.shape[2])


def shards(factor, gradient, sketch_ids):
    rows, cols = factor.shape
    z, y, c, x = (lax.axis_index(a) for a in ALL)
    owner = z // (NZ // NX)
    offset = rows * (((z % (NZ // NX)) * NY + y) * NC + c)
    mine = (x == owner).astype(F32)

    strip = jnp.pad(gradient.T, ((0, 4), (0, 0)))
    plane = lax.all_gather(strip, ("z", "y"), axis=0, tiled=False)

    grad32 = gradient.astype(F32)
    sketch = sketch_ids.astype(F32)
    small = jnp.concatenate([dot(grad32, sketch, 0, 0), decay_rate * dot(factor, sketch, 1, 0)], axis=0)
    small = jnp.sum(spread(small, "x", NX), axis=0)
    inner, decayed = small[:gradient.shape[1]], small[gradient.shape[1]:]
    place = (lax.broadcasted_iota(jnp.int32, (cols, rows), 0) == offset + lax.broadcasted_iota(jnp.int32, (cols, rows), 1)).astype(F32)
    partial = dot(jnp.concatenate([grad32, mine * place], axis=1), jnp.concatenate([inner, decayed], axis=0), 1, 0)
    piece = scatter(scatter(scatter_core(partial, c), "y", NY), "z", NZ)
    piece = join(spread(join(spread(piece, "z", NZ)), "y", NY))
    ranged = lax.all_gather(piece, "c", axis=0, tiled=True)

    here = mine * lax.dynamic_slice_in_dim(ranged, offset, rows, 0)
    gram = dot(lax.dynamic_slice_in_dim(ranged, c * 128, 128, 1), ranged, 0, 0)
    part = jnp.concatenate([gram, dot(grad32, ranged, 0, 0), here], axis=0)
    part = jnp.sum(spread(part, "x", NX), axis=0)
    gram, weighted, own_rows = part[:128], part[128:128 + gradient.shape[1]], part[128 + gradient.shape[1]:]
    gram_matrix = lax.all_gather(gram, "c", axis=0, tiled=True) / B

    core = decay_rate * dot(own_rows, dot(factor, ranged, 1, 0), 0, 0)
    core = core + (x == 0).astype(F32) * dot(weighted, weighted, 0, 0)
    core = scatter(scatter_core(core, c), ("y", "x"), NY * NX)
    core = jnp.sum(spread(core, "z", NZ), axis=0)
    core = join(spread(core, ("y", "x"), NY * NX))
    core = lax.all_gather(core, "c", axis=0, tiled=True)

    lower_factor = jnp.linalg.cholesky(gram_matrix)
    inverse = jax.scipy.linalg.solve_triangular(lower_factor, jnp.eye(256, dtype=F32), lower=True)
    range_basis = dot(own_rows, inverse, 1, 1)
    projected_core = dot(dot(inverse, core, 1, 0), inverse, 1, 1) / B

    plane, _ = lax.optimization_barrier((plane, inverse))
    plane = plane.reshape(-1, cols)
    plane = lax.all_gather(plane, "c", axis=0, tiled=True)
    picked = lax.dot_general(place.astype(jnp.bfloat16), plane, (((0,), (1,)), ((), ())), preferred_element_type=F32).astype(jnp.bfloat16)
    picked = picked * mine.astype(jnp.bfloat16)
    total = picked
    for k in range(1, NX):
        pairs = []
        for d in range(NZ * NY * NC):
            src = (d // (NY * NC)) // (NZ // NX)
            pairs.append((d * NX + src, d * NX + (src + k) % NX))
        total = total + lax.ppermute(picked, ALL, pairs)
    outer_sum = lax.dot_general(total, plane, (((1,), (0,)), ((), ())), preferred_element_type=F32)
    factor_new = decay_rate * factor + outer_sum
    return (factor_new, range_basis, projected_core)


def solution(mesh):
    fine = Mesh(mesh.devices.reshape(NZ, NY, NC, NX), ALL)
    f = ("z", "y", "c")
    return jax.shard_map(
        shards,
        mesh=fine,
        in_specs=(P(f, "x"), P("x", f), P("x", None)),
        out_specs=(P(f, "x"), P(f, None), P()),
        check_vma=False,
    )
```

time: 1180 us -> 352 us (0.30)
  waiting for transfers between devices: 1060 us -> 146 us
  starting transfers between devices: 0.38 us -> 53.6 us
  blocking collectives: 12.7 us -> 48.9 us
  local copies, waits for them, and re-layouts: 23 us -> 10.9 us
    psum x3 -> x0, waiting for transfers between devices: 808 us -> none  [the longest x1 460 us: shards(): projected_core = lax.psum(core_term, ('fsdp', 'row')) / B]
    all_gather x2, waiting for transfers between devices: 248 us -> 98.9 us  [the longest x1 98.9 us: shards(): plane = lax.all_gather(strip, ('z', 'y'), axis=0, tiled=False)]
    all_to_all x0 -> x7, waiting for transfers between devices: none -> 42.3 us  [the longest x5 42.2 us: spread(): return lax.all_to_all(jnp.broadcast_to(v[None], (n,) + v.shape), axis, 0, 0)]
    all_to_all x0 -> x7, starting transfers between devices: none -> 33.7 us  [the longest x5 26.1 us: spread(): return lax.all_to_all(jnp.broadcast_to(v[None], (n,) + v.shape), axis, 0, 0)]
    all_to_all x0 -> x2, blocking collectives: none -> 27.3 us  [the longest x1 15.4 us: scatter(): lax.all_to_all(v.reshape(n, v.shape[0] // n, v.shape[1]), axis, 0, 0)]
    all_gather x0 -> x3, blocking collectives: none -> 21.6 us  [the longest x1 13.3 us: shards(): ranged = lax.all_gather(piece, 'c', axis=0, tiled=True)]
    ppermute x0 -> x5, starting transfers between devices: none -> 19.8 us  [the longest x2 14.3 us: swap_core(): return lax.ppermute(v, 'c', [(0, 1), (1, 0)])]
    psum x1 -> x0, blocking collectives: 12.7 us -> none  [shards(): ranged = lax.psum(jnp.dot(factor_new, sketch, precision=highest), 'row')]
  transfers between devices with their start and end apart: 5 -> 14, of which waited for: 5 -> 9; matrix products, arithmetic and copies ran while one was open for 1% -> 21% of each run, Pallas kernels for 0% -> 0%
where the time goes in v1:
time: 352 us; the launch traced here: 350 us
  waiting for transfers between devices  146 us (41%)
  other arithmetic  55.6 us (16%)
  starting transfers between devices  53.6 us (15%)
  blocking collectives  48.9 us (14%)
  matrix products  19.2 us (5%)
  between operations  15.8 us (4%)
  local copies, waits for them, and re-layouts  10.9 us (3%)
    all_gather x1, waiting for transfers between devices, shards(): plane = lax.all_gather(strip, ('z', 'y'), axis=0, tiled=False)  98.9 us
    all_to_all x5, waiting for transfers between devices, spread(): return lax.all_to_all(jnp.broadcast_to(v[None], (n,) + v.shape), axis, 0, 0)  42.2 us
    another operation x6, other arithmetic, shards(): lower_factor = jnp.linalg.cholesky(gram_matrix)  33.9 us
    all_to_all x5, starting transfers between devices, spread(): return lax.all_to_all(jnp.broadcast_to(v[None], (n,) + v.shape), axis, 0, 0)  26.1 us
    another operation x3, other arithmetic, shards(): jax.scipy.linalg.solve_triangular(lower_factor, jnp.eye(256, dtype=F32),...  19.7 us
    all_to_all x1, blocking collectives, scatter(): lax.all_to_all(v.reshape(n, v.shape[0] // n, v.shape[1]), axis, 0, 0)  15.4 us
    ppermute x2, starting transfers between devices, swap_core(): return lax.ppermute(v, 'c', [(0, 1), (1, 0)])  14.3 us
    all_gather x1, blocking collectives, shards(): ranged = lax.all_gather(piece, 'c', axis=0, tiled=True)  13.3 us
  transfers between devices with their start and end apart: 14, of which 9 were waited for; matrix products, arithmetic and copies ran while one was open for 21% of the time, Pallas kernels for 0%

profile of v1, /device:TPU:1, one launch (start us, length us, event | category | flops | bytes accessed | tf_op | source)
XLA Modules:
  0.0 349.9 jit_solution(10030239470533725279)
XLA Ops:
  12.5 4.8 %all-to-all-start = ((f32[4,36,256]{2,1,0:T(8,128)}), f32[4,36,256]{2,1,0:T(8,128)S(1)}, u32[]{:S(2)}, u32[]{:S(2)}) async-start(f32[4,36,256]{2,1,0:T(8,128)} %broadcast_in_dim.15), calls=%async_computation | async-start | bytes 327680 | tf_op jit(solution)/shard_map/all_to_all | solution.py:19
  18.2 4.1 %all-to-all-done = f32[4,36,256]{2,1,0:T(8,128)S(1)} async-done(((f32[4,36,256]{2,1,0:T(8,128)}), f32[4,36,256]{2,1,0:T(8,128)S(1)}, u32[]{:S(2)}, u32[]{:S(2)}) %all-to-all-start) | async-done | bytes 147488 | tf_op jit(solution)/shard_map/all_to_all | solution.py:19
  23.3 12.1 %collective-permute-start = (f32[384,256]{1,0:T(8,128)S(1)}, f32[384,256]{1,0:T(8,128)S(1)}, u32[]{:S(2)}, u32[]{:S(2)}) collective-permute-start(f32[384,256]{1,0:T(8,128)S(1)} %constant_dynamic-slice_fusion.2), channel_id=1, source_target_pairs={{0,4},{4,0},{1,5},{5,1},{2,6},{6,2},{3,7},{7,3},{8,12},{12,8},{9,1... | collective-permute-start | bytes 1179656 | tf_op jit(solution)/shard_map/ppermute | solution.py:23
  41.0 98.9 %all-gather.6.cloned.1.call-done = bf16[2304,768]{1,0:T(8,128)(2,1)} async-done(((bf16[24,768]{1,0:T(8,128)(2,1)}), bf16[2304,768]{1,0:T(8,128)(2,1)}) %all-gather.6.cloned.1.call-update) | async-done | bytes 3538960 | tf_op jit(solution)/shard_map/all_gather | solution.py:49
  140.0 15.4 %all_to_all.45 = f32[12,4,256]{2,1,0:T(4,128)S(1)} all-to-all(f32[12,4,256]{2,1,0:T(4,128)S(1)} %reshape.50), channel_id=1, replica_groups=mesh['z'=12,'y'=8,'c'=2,'x'=4] {'z'}, dimensions={0} | all-to-all | bytes 98304 | tf_op jit(solution)/shard_map/all_to_all | solution.py:34
  155.4 12.0 %all_to_all.46 = f32[12,4,256]{2,1,0:T(4,128)S(1)} all-to-all(f32[12,4,256]{2,1,0:T(4,128)S(1)} %broadcast_in_dim.16), channel_id=1, replica_groups=mesh['z'=12,'y'=8,'c'=2,'x'=4] {'z'}, dimensions={0} | all-to-all | bytes 98304 | tf_op jit(solution)/shard_map/all_to_all | solution.py:19
  168.2 4.7 %all-to-all-start.4 = ((f32[8,48,256]{2,1,0:T(8,128)}), f32[8,48,256]{2,1,0:T(8,128)S(1)}, u32[]{:S(2)}, u32[]{:S(2)}) async-start(f32[8,48,256]{2,1,0:T(8,128)} %broadcast_in_dim.18), calls=%async_computation.4 | async-start | bytes 786432 | tf_op jit(solution)/shard_map/all_to_all | solution.py:19
  172.9 10.7 %all-to-all-done.4 = f32[8,48,256]{2,1,0:T(8,128)S(1)} async-done(((f32[8,48,256]{2,1,0:T(8,128)}), f32[8,48,256]{2,1,0:T(8,128)S(1)}, u32[]{:S(2)}, u32[]{:S(2)}) %all-to-all-start.4) | async-done | bytes 393248 | tf_op jit(solution)/shard_map/all_to_all | solution.py:19
  183.7 13.3 %all_gather.20 = f32[768,256]{1,0:T(8,128)S(1)} all-gather(f32[384,256]{1,0:T(8,128)S(1)} %bitcast.51), channel_id=1, replica_groups=mesh['z'=12,'y'=8,'c'=2,'x'=4] {'c'}, dimensions={0}, use_global_device_ids=true | all-gather | bytes 1179648 | tf_op jit(solution)/shard_map/all_gather | solution.py:60
  199.2 4.0 %all-to-all-start.5 = ((f32[4,164,256]{2,1,0:T(8,128)}), f32[4,164,256]{2,1,0:T(8,128)S(1)}, u32[]{:S(2)}, u32[]{:S(2)}) async-start(f32[4,164,256]{2,1,0:T(8,128)} %broadcast_in_dim.19), calls=%async_computation.5 | async-start | bytes 1376256 | tf_op jit(solution)/shard_map/all_to_all | solution.py:19
  203.7 10.2 %all-to-all-done.5 = f32[4,164,256]{2,1,0:T(8,128)S(1)} async-done(((f32[4,164,256]{2,1,0:T(8,128)}), f32[4,164,256]{2,1,0:T(8,128)S(1)}, u32[]{:S(2)}, u32[]{:S(2)}) %all-to-all-start.5) | async-done | bytes 671776 | tf_op jit(solution)/shard_map/all_to_all | solution.py:19
  217.5 11.7 %cholesky.50 = f32[128,128]{1,0:T(8,128)S(1)} custom-call(f32[128,128]{1,0:T(8,128)S(1)} %cholesky.118), custom_call_target="Cholesky" | custom-call | tf_op jit(solution)/shard_map/jit(cholesky)/cholesky | solution.py:76
  229.3 9.8 %custom-call.15 = f32[1,128,128]{1,2,0:T(8,128)S(1)} custom-call(f32[1,128,128]{2,1,0:T(8,128)S(1)} %get-tuple-element.35), custom_call_target="InvertDiagBlocksLowerTriangular" | custom-call | tf_op jit(solution)/shard_map/jit(cholesky)/cholesky | solution.py:76
  239.6 11.7 %cholesky.105 = f32[128,128]{1,0:T(8,128)S(1)} custom-call(f32[128,128]{1,0:T(8,128)S(1)} %convolution_subtract_fusion.1), custom_call_target="Cholesky" | custom-call | tf_op jit(solution)/shard_map/jit(cholesky)/cholesky | solution.py:76
  257.2 4.1 %all-to-all-start.6 = ((f32[32,4,256]{2,1,0:T(4,128)}), f32[32,4,256]{2,1,0:T(4,128)S(1)}, u32[]{:S(2)}, u32[]{:S(2)}) async-start(f32[32,4,256]{2,1,0:T(4,128)} %reshape.53), calls=%async_computation.6 | async-start | bytes 262144 | tf_op jit(solution)/shard_map/all_to_all | solution.py:34
  261.4 3.8 %while.1 = (s32[]{:T(128)}, f32[256,256]{1,0:T(8,128)S(1)}, s32[2,2]{1,0:T(2,128)S(1)}, f32[2,128,128]{2,1,0:T(8,128)S(1)}, s32[]{:T(128)}) while((s32[]{:T(128)}, f32[256,256]{1,0:T(8,128)S(1)}, s32[2,2]{1,0:T(2,128)S(1)}, f32[2,128,128]{2,1,0:T(8,128)S(1)}, s32[]{:T(128)}) %tuple.33), condition=%wide.while_cond, body=%wide.while_body.sunk | while | flops 2 | bytes 131189 | solution.py:77
  265.2 19.7 %custom-call.16 = f32[2,128,128]{1,2,0:T(8,128)S(1)} custom-call(f32[2,128,128]{2,1,0:T(8,128)S(1)} %get-tuple-element.12), custom_call_target="InvertDiagBlocksLowerTriangular" | custom-call | tf_op jit(solution)/shard_map/jit(_solve_triangular)/triangular_solve | solution.py:77
  285.8 3.5 all-to-all-start.7
  289.6 9.1 %all-to-all-done.7 = f32[12,4,256]{2,1,0:T(4,128)S(1)} async-done(((f32[12,4,256]{2,1,0:T(4,128)}), f32[12,4,256]{2,1,0:T(4,128)S(1)}, u32[]{:S(2)}, u32[]{:S(2)}) %all-to-all-start.7) | async-done | bytes 49184 | tf_op jit(solution)/shard_map/all_to_all | solution.py:19
  299.4 9.1 %all-to-all-start.8 = ((f32[32,4,256]{2,1,0:T(4,128)}), f32[32,4,256]{2,1,0:T(4,128)S(1)}, u32[]{:S(2)}, u32[]{:S(2)}) async-start(f32[32,4,256]{2,1,0:T(4,128)} %broadcast_in_dim.21), calls=%async_computation.8 | async-start | bytes 262144 | tf_op jit(solution)/shard_map/all_to_all | solution.py:19
  309.7 8.1 %all-to-all-done.8 = f32[32,4,256]{2,1,0:T(4,128)S(1)} async-done(((f32[32,4,256]{2,1,0:T(4,128)}), f32[32,4,256]{2,1,0:T(4,128)S(1)}, u32[]{:S(2)}, u32[]{:S(2)}) %all-to-all-start.8) | async-done | bytes 131104 | tf_op jit(solution)/shard_map/all_to_all | solution.py:19
  317.9 5.0 %all_gather.23 = f32[256,256]{1,0:T(8,128)S(1)} all-gather(f32[128,256]{1,0:T(8,128)S(1)} %reshape.54), channel_id=1, replica_groups=mesh['z'=12,'y'=8,'c'=2,'x'=4] {'c'}, dimensions={0}, use_global_device_ids=true | all-gather | bytes 393216 | tf_op jit(solution)/shard_map/all_gather | solution.py:74
  323.2 4.9 %fusion = bf16[16,4608]{1,0:T(8,128)(2,1)S(1)} fusion(bf16[4608,768]{1,0:T(8,128)(2,1)} %all-gather.4.cloned.1.call-done, bf16[]{:T(256)S(6)} %convert_element_type.33, s32[16]{0:T(128)S(1)} %iota_add_fusion), kind=kOutput, calls=%fused_computation.3 | convolution fusion | flops 113430528 | bytes 7225410 | tf_op jit(solution)/shard_map/dot_general | solution.py:84
  338.4 4.7 %convolution_add_fusion = f32[16,768]{1,0:T(8,128)} fusion(bf16[4608,768]{1,0:T(8,128)(2,1)} %all-gather.4.cloned.1.call-done, bf16[16,4608]{1,0:T(8,128)(2,1)S(1)} %collective-permute-done.3, bf16[16,4608]{1,0:T(8,128)(2,1)S(1)} %collective-permute-done.2, bf16[16,4608]{1,0:T(8,128)(2,1)S(1)} %fusion, bf16[16,4608]{1,0:T(8,128)(2,1)S(1)} %collective-permute-done.1, ...), kind=kOutput, calls=%fused_computation.10 | convolution fusion | flops 113491968 | bytes 7766016 | tf_op jit(solution)/shard_map/dot_general | solution.py:93
  (87 shorter events, 42.6 us)
Async XLA Ops:
  7.2 189.8 %copy-start = (bf16[768,20]{0,1:T(8,128)(2,1)S(1)}, bf16[768,20]{0,1:T(8,128)(2,1)}, u32[]{:S(2)}) copy-start(bf16[768,20]{0,1:T(8,128)(2,1)} %param.4) | copy-start | bytes 92164
  7.2 132.7 %all-gather.6.cloned.1.call-start = ((), (), s32[]{:S(2)}) async-start(), calls=%async_computation.10 | async-start | bytes 3575808 | tf_op jit(solution)/shard_map/all_gather | solution.py:49
  12.5 9.8 %all-to-all-start = ((f32[4,36,256]{2,1,0:T(8,128)}), f32[4,36,256]{2,1,0:T(8,128)S(1)}, u32[]{:S(2)}, u32[]{:S(2)}) async-start(f32[4,36,256]{2,1,0:T(8,128)} %broadcast_in_dim.15), calls=%async_computation | async-start | bytes 327680 | tf_op jit(solution)/shard_map/all_to_all | solution.py:19
  23.2 180.0 %copy-start.1 = (f32[16,768]{1,0:T(8,128)S(1)}, f32[16,768]{1,0:T(8,128)}, u32[]{:S(2)}) copy-start(f32[16,768]{1,0:T(8,128)} %param.3) | copy-start | bytes 147460
  23.3 13.4 %collective-permute-start = (f32[384,256]{1,0:T(8,128)S(1)}, f32[384,256]{1,0:T(8,128)S(1)}, u32[]{:S(2)}, u32[]{:S(2)}) collective-permute-start(f32[384,256]{1,0:T(8,128)S(1)} %constant_dynamic-slice_fusion.2), channel_id=1, source_target_pairs={{0,4},{4,0},{1,5},{5,1},{2,6},{6,2},{3,7},{7,3},{8,12},{12,8},{9,1... | collective-permute-start | bytes 1179656 | tf_op jit(solution)/shard_map/ppermute | solution.py:23
  37.5 102.4 %all-to-all-start.1 = ((f32[8,48,256]{2,1,0:T(8,128)}), f32[8,48,256]{2,1,0:T(8,128)S(1)}, u32[]{:S(2)}, u32[]{:S(2)}) async-start(f32[8,48,256]{2,1,0:T(8,128)} %bitcast.2), calls=%async_computation.1 | async-start | bytes 786432 | tf_op jit(solution)/shard_map/all_to_all | solution.py:34
  40.9 282.3 %all-gather.4.cloned.1.call-start = ((), (), s32[]{:S(2)}) async-start(), calls=%async_computation.9 | async-start | bytes 10616832 | tf_op jit(solution)/shard_map/all_gather | solution.py:83
  168.2 15.5 %all-to-all-start.4 = ((f32[8,48,256]{2,1,0:T(8,128)}), f32[8,48,256]{2,1,0:T(8,128)S(1)}, u32[]{:S(2)}, u32[]{:S(2)}) async-start(f32[8,48,256]{2,1,0:T(8,128)} %broadcast_in_dim.18), calls=%async_computation.4 | async-start | bytes 786432 | tf_op jit(solution)/shard_map/all_to_all | solution.py:19
  199.2 14.7 %all-to-all-start.5 = ((f32[4,164,256]{2,1,0:T(8,128)}), f32[4,164,256]{2,1,0:T(8,128)S(1)}, u32[]{:S(2)}, u32[]{:S(2)}) async-start(f32[4,164,256]{2,1,0:T(8,128)} %broadcast_in_dim.19), calls=%async_computation.5 | async-start | bytes 1376256 | tf_op jit(solution)/shard_map/all_to_all | solution.py:19
  252.2 4.3 %collective-permute-start.4 = (f32[128,256]{1,0:T(8,128)S(1)}, f32[128,256]{1,0:T(8,128)S(1)}, u32[]{:S(2)}, u32[]{:S(2)}) collective-permute-start(f32[128,256]{1,0:T(8,128)S(1)} %constant_dynamic-slice_fusion.1), channel_id=1, source_target_pairs={{0,4},{4,0},{1,5},{5,1},{2,6},{6,2},{3,7},{7,3},{8,12},{12,8},{9,1... | collective-permute-start | bytes 393224 | tf_op jit(solution)/shard_map/ppermute | solution.py:23
  257.2 27.9 %all-to-all-start.6 = ((f32[32,4,256]{2,1,0:T(4,128)}), f32[32,4,256]{2,1,0:T(4,128)S(1)}, u32[]{:S(2)}, u32[]{:S(2)}) async-start(f32[32,4,256]{2,1,0:T(4,128)} %reshape.53), calls=%async_computation.6 | async-start | bytes 262144 | tf_op jit(solution)/shard_map/all_to_all | solution.py:34
  285.8 12.9 %all-to-all-start.7 = ((f32[12,4,256]{2,1,0:T(4,128)}), f32[12,4,256]{2,1,0:T(4,128)S(1)}, u32[]{:S(2)}, u32[]{:S(2)}) async-start(f32[12,4,256]{2,1,0:T(4,128)} %broadcast_in_dim.20), calls=%async_computation.7 | async-start | bytes 98304 | tf_op jit(solution)/shard_map/all_to_all | solution.py:19
  299.4 18.4 %all-to-all-start.8 = ((f32[32,4,256]{2,1,0:T(4,128)}), f32[32,4,256]{2,1,0:T(4,128)S(1)}, u32[]{:S(2)}, u32[]{:S(2)}) async-start(f32[32,4,256]{2,1,0:T(4,128)} %broadcast_in_dim.21), calls=%async_computation.8 | async-start | bytes 262144 | tf_op jit(solution)/shard_map/all_to_all | solution.py:19
  328.2 6.8 %collective-permute-start.3 = (bf16[16,4608]{1,0:T(8,128)(2,1)S(1)}, bf16[16,4608]{1,0:T(8,128)(2,1)S(1)}, u32[]{:S(2)}, u32[]{:S(2)}) collective-permute-start(bf16[16,4608]{1,0:T(8,128)(2,1)S(1)} %fusion), channel_id=1, source_target_pairs={{0,3},{4,7},{8,11},{12,15},{16,19},{20,23},{24,27},{28,31},{32,35}... | collective-permute-start | bytes 442376 | tf_op jit(solution)/shard_map/ppermute | solution.py:92
  331.1 4.2 %collective-permute-start.2 = (bf16[16,4608]{1,0:T(8,128)(2,1)S(1)}, bf16[16,4608]{1,0:T(8,128)(2,1)S(1)}, u32[]{:S(2)}, u32[]{:S(2)}) collective-permute-start(bf16[16,4608]{1,0:T(8,128)(2,1)S(1)} %fusion), channel_id=1, source_target_pairs={{0,2},{4,6},{8,10},{12,14},{16,18},{20,22},{24,26},{28,30},{32,34}... | collective-permute-start | bytes 442376 | tf_op jit(solution)/shard_map/ppermute | solution.py:92
  332.4 6.0 %collective-permute-start.1 = (bf16[16,4608]{1,0:T(8,128)(2,1)S(1)}, bf16[16,4608]{1,0:T(8,128)(2,1)S(1)}, u32[]{:S(2)}, u32[]{:S(2)}) collective-permute-start(bf16[16,4608]{1,0:T(8,128)(2,1)S(1)} %fusion), channel_id=1, source_target_pairs={{0,1},{4,5},{8,9},{12,13},{16,17},{20,21},{24,25},{28,29},{32,33},... | collective-permute-start | bytes 442376 | tf_op jit(solution)/shard_map/ppermute | solution.py:92
Sparse Core Ops, SparseCore 0:
  12.3 127.5 all-gather.5
  142.3 33.0 all-gather.3

commit v2 on v1

--- a/solution.py
+++ b/solution.py
@@ -46,7 +46,7 @@
     mine = (x == owner).astype(F32)
 
     strip = jnp.pad(gradient.T, ((0, 4), (0, 0)))
-    plane = lax.all_gather(strip, ("z", "y"), axis=0, tiled=False)
+    plane = lax.all_gather(strip, ("z", "y", "c"), axis=0, tiled=True)
 
     grad32 = gradient.astype(F32)
     sketch = sketch_ids.astype(F32)
@@ -55,22 +55,25 @@
     inner, decayed = small[:gradient.shape[1]], small[gradient.shape[1]:]
     place = (lax.broadcasted_iota(jnp.int32, (cols, rows), 0) == offset + lax.broadcasted_iota(jnp.int32, (cols, rows), 1)).astype(F32)
     partial = dot(jnp.concatenate([grad32, mine * place], axis=1), jnp.concatenate([inner, decayed], axis=0), 1, 0)
-    piece = scatter(scatter(scatter_core(partial, c), "y", NY), "z", NZ)
-    piece = join(spread(join(spread(piece, "z", NZ)), "y", NY))
+    piece = scatter(scatter_core(partial, c), ("z", "y"), NZ * NY)
+    piece = join(spread(piece, ("z", "y"), NZ * NY))
     ranged = lax.all_gather(piece, "c", axis=0, tiled=True)
 
     here = mine * lax.dynamic_slice_in_dim(ranged, offset, rows, 0)
     gram = dot(lax.dynamic_slice_in_dim(ranged, c * 128, 128, 1), ranged, 0, 0)
-    part = jnp.concatenate([gram, dot(grad32, ranged, 0, 0), here], axis=0)
+    wide = gradient.shape[1]
+    part = jnp.concatenate([gram, here, dot(grad32, ranged, 0, 0), decay_rate * dot(factor, ranged, 1, 0)], axis=0)
     part = jnp.sum(spread(part, "x", NX), axis=0)
-    gram, weighted, own_rows = part[:128], part[128:128 + gradient.shape[1]], part[128 + gradient.shape[1]:]
+    gram, own_rows = part[:128], part[128:128 + rows]
+    left = part[128:128 + rows + wide]
     gram_matrix = lax.all_gather(gram, "c", axis=0, tiled=True) / B
 
-    core = decay_rate * dot(own_rows, dot(factor, ranged, 1, 0), 0, 0)
-    core = core + (x == 0).astype(F32) * dot(weighted, weighted, 0, 0)
-    core = scatter(scatter_core(core, c), ("y", "x"), NY * NX)
+    right = jnp.concatenate([part[128 + rows + wide:], part[128 + rows:128 + rows + wide]], axis=0)
+    core = dot(left, right, 0, 0).reshape(NC, NX, 32, 256)
+    core = lax.dynamic_index_in_dim(core, x, 1, keepdims=False).reshape(64, 256)
+    core = scatter(scatter_core(core, c), "y", NY)
     core = jnp.sum(spread(core, "z", NZ), axis=0)
-    core = join(spread(core, ("y", "x"), NY * NX))
+    core = join(spread(core, ("x", "y"), NX * NY))
     core = lax.all_gather(core, "c", axis=0, tiled=True)
 
     lower_factor = jnp.linalg.cholesky(gram_matrix)
@@ -78,9 +81,8 @@
     range_basis = dot(own_rows, inverse, 1, 1)
     projected_core = dot(dot(inverse, core, 1, 0), inverse, 1, 1) / B
 
-    plane, _ = lax.optimization_barrier((plane, inverse))
-    plane = plane.reshape(-1, cols)
-    plane = lax.all_gather(plane, "c", axis=0, tiled=True)
+    late = (lower_factor[0, 0] > 0).astype(jnp.int32) >> 1
+    place = (lax.broadcasted_iota(jnp.int32, (cols, rows), 0) == offset + late + lax.broadcasted_iota(jnp.int32, (cols, rows), 1))
     picked = lax.dot_general(place.astype(jnp.bfloat16), plane, (((0,), (1,)), ((), ())), preferred_element_type=F32).astype(jnp.bfloat16)
     picked = picked * mine.astype(jnp.bfloat16)
     total = picked

time: 352 us -> 262 us (0.74)
  waiting for transfers between devices: 146 us -> 62.4 us
  starting transfers between devices: 53.6 us -> 46.2 us
    all_gather x2 -> x1, waiting for transfers between devices: 98.9 us -> 0.02 us  [shards(): plane = lax.all_gather(strip, ('z', 'y', 'c'), axis=0, tiled=True)]
    all_to_all x1, blocking collectives: 15.4 us -> 35.9 us  [scatter(): lax.all_to_all(v.reshape(n, v.shape[0] // n, v.shape[1]), axis, 0, 0)]
    all_to_all x1 -> x0, blocking collectives: 12 us -> none  [spread(): return lax.all_to_all(jnp.broadcast_to(v[None], (n,) + v.shape), axis, 0, 0)]
    all_to_all x5, waiting for transfers between devices: 42.2 us -> 53.6 us  [spread(): return lax.all_to_all(jnp.broadcast_to(v[None], (n,) + v.shape), axis, 0, 0)]
    all_gather x1, blocking collectives: 13.3 us -> 6.52 us  [shards(): ranged = lax.all_gather(piece, 'c', axis=0, tiled=True)]
    all_to_all x2 -> x1, waiting for transfers between devices: 0.01 us -> 5.36 us  [scatter(): lax.all_to_all(v.reshape(n, v.shape[0] // n, v.shape[1]), axis, 0, 0)]
    all_to_all x2 -> x1, starting transfers between devices: 7.53 us -> 3.34 us  [scatter(): lax.all_to_all(v.reshape(n, v.shape[0] // n, v.shape[1]), axis, 0, 0)]
    dot_general x11 -> x10, matrix products: 8.26 us -> 7.83 us  [dot(): lax.dot_general(a, b, (((ca,), (cb,)), ((), ())), precision=HI, preferred...]
  transfers between devices with their start and end apart: 14 -> 12, of which waited for: 9 -> 8; matrix products, arithmetic and copies ran while one was open for 21% -> 29% of each run, Pallas kernels for 0% -> 0%
where the time goes in v2:
time: 262 us; the launch traced here: 261 us
  waiting for transfers between devices  62.4 us (24%)
  other arithmetic  54.9 us (21%)
  blocking collectives  49.9 us (19%)
  starting transfers between devices  46.2 us (18%)
  matrix products  18.7 us (7%)
  between operations  16.4 us (6%)
  local copies, waits for them, and re-layouts  11.8 us (5%)
    all_to_all x5, waiting for transfers between devices, spread(): return lax.all_to_all(jnp.broadcast_to(v[None], (n,) + v.shape), axis, 0, 0)  53.6 us
    all_to_all x1, blocking collectives, scatter(): lax.all_to_all(v.reshape(n, v.shape[0] // n, v.shape[1]), axis, 0, 0)  35.9 us
    another operation x6, other arithmetic, shards(): lower_factor = jnp.linalg.cholesky(gram_matrix)  33.9 us
    all_to_all x5, starting transfers between devices, spread(): return lax.all_to_all(jnp.broadcast_to(v[None], (n,) + v.shape), axis, 0, 0)  22.8 us
    another operation x3, other arithmetic, shards(): jax.scipy.linalg.solve_triangular(lower_factor, jnp.eye(256, dtype=F32),...  19.7 us
    ppermute x2, starting transfers between devices, swap_core(): return lax.ppermute(v, 'c', [(0, 1), (1, 0)])  15.2 us
    dot_general x10, matrix products, dot(): lax.dot_general(a, b, (((ca,), (cb,)), ((), ())), precision=HI, preferred...  7.83 us
    all_gather x1, blocking collectives, shards(): ranged = lax.all_gather(piece, 'c', axis=0, tiled=True)  6.52 us
  transfers between devices with their start and end apart: 12, of which 8 were waited for; matrix products, arithmetic and copies ran while one was open for 29% of the time, Pallas kernels for 0%

profile of v2, /device:TPU:1, one launch (start us, length us, event | category | flops | bytes accessed | tf_op | source)
XLA Modules:
  0.0 260.7 jit_solution(3976892249437436009)
XLA Ops:
  12.5 4.8 %all-to-all-start = ((f32[4,36,256]{2,1,0:T(8,128)}), f32[4,36,256]{2,1,0:T(8,128)S(1)}, u32[]{:S(2)}, u32[]{:S(2)}) async-start(f32[4,36,256]{2,1,0:T(8,128)} %broadcast_in_dim.11), calls=%async_computation | async-start | bytes 327680 | tf_op jit(solution)/shard_map/all_to_all | solution.py:19
  18.2 4.1 %all-to-all-done = f32[4,36,256]{2,1,0:T(8,128)S(1)} async-done(((f32[4,36,256]{2,1,0:T(8,128)}), f32[4,36,256]{2,1,0:T(8,128)S(1)}, u32[]{:S(2)}, u32[]{:S(2)}) %all-to-all-start) | async-done | bytes 147488 | tf_op jit(solution)/shard_map/all_to_all | solution.py:19
  23.3 12.1 %collective-permute-start = (f32[384,256]{1,0:T(8,128)S(1)}, f32[384,256]{1,0:T(8,128)S(1)}, u32[]{:S(2)}, u32[]{:S(2)}) collective-permute-start(f32[384,256]{1,0:T(8,128)S(1)} %constant_dynamic-slice_fusion.3), channel_id=1, source_target_pairs={{0,4},{4,0},{1,5},{5,1},{2,6},{6,2},{3,7},{7,3},{8,12},{12,8},{9,1... | collective-permute-start | bytes 1179656 | tf_op jit(solution)/shard_map/ppermute | solution.py:23
  36.8 35.9 %all_to_all.35 = f32[96,4,256]{2,1,0:T(4,128)S(1)} all-to-all(f32[96,4,256]{2,1,0:T(4,128)S(1)} %reshape.54), channel_id=1, replica_groups=mesh['z'=12,'y'=8,'c'=2,'x'=4] {'z','y'}, dimensions={0} | all-to-all | bytes 786432 | tf_op jit(solution)/shard_map/all_to_all | solution.py:34
  73.6 7.1 %all-to-all-start.2 = ((f32[96,4,256]{2,1,0:T(4,128)}), f32[96,4,256]{2,1,0:T(4,128)S(1)}, u32[]{:S(2)}, u32[]{:S(2)}) async-start(f32[96,4,256]{2,1,0:T(4,128)} %broadcast_in_dim.12), calls=%async_computation.2 | async-start | bytes 786432 | tf_op jit(solution)/shard_map/all_to_all | solution.py:19
  80.7 20.4 %all-to-all-done.2 = f32[96,4,256]{2,1,0:T(4,128)S(1)} async-done(((f32[96,4,256]{2,1,0:T(4,128)}), f32[96,4,256]{2,1,0:T(4,128)S(1)}, u32[]{:S(2)}, u32[]{:S(2)}) %all-to-all-start.2) | async-done | bytes 393248 | tf_op jit(solution)/shard_map/all_to_all | solution.py:19
  101.2 6.5 %all_gather.12 = f32[768,256]{1,0:T(8,128)S(1)} all-gather(f32[384,256]{1,0:T(8,128)S(1)} %reshape.55), channel_id=1, replica_groups=mesh['z'=12,'y'=8,'c'=2,'x'=4] {'c'}, dimensions={0}, use_global_device_ids=true | all-gather | bytes 1179648 | tf_op jit(solution)/shard_map/all_gather | solution.py:60
  110.5 3.5 %all-to-all-start.3 = ((f32[4,180,256]{2,1,0:T(8,128)}), f32[4,180,256]{2,1,0:T(8,128)S(1)}, u32[]{:S(2)}, u32[]{:S(2)}) async-start(f32[4,180,256]{2,1,0:T(8,128)} %broadcast_in_dim.13), calls=%async_computation.3 | async-start | bytes 1507328 | tf_op jit(solution)/shard_map/all_to_all | solution.py:19
  114.0 11.6 %all-to-all-done.3 = f32[4,180,256]{2,1,0:T(8,128)S(1)} async-done(((f32[4,180,256]{2,1,0:T(8,128)}), f32[4,180,256]{2,1,0:T(8,128)S(1)}, u32[]{:S(2)}, u32[]{:S(2)}) %all-to-all-start.3) | async-done | bytes 737312 | tf_op jit(solution)/shard_map/all_to_all | solution.py:19
  126.2 3.1 %collective-permute-start.4 = (f32[32,256]{1,0:T(8,128)S(1)}, f32[32,256]{1,0:T(8,128)S(1)}, u32[]{:S(2)}, u32[]{:S(2)}) collective-permute-start(f32[32,256]{1,0:T(8,128)S(1)} %constant_dynamic-slice_fusion.1), channel_id=1, source_target_pairs={{0,4},{4,0},{1,5},{5,1},{2,6},{6,2},{3,7},{7,3},{8,12},{12,8},{9,1... | collective-permute-start | bytes 98312 | tf_op jit(solution)/shard_map/ppermute | solution.py:23
  131.8 11.7 %cholesky.50 = f32[128,128]{1,0:T(8,128)S(1)} custom-call(f32[128,128]{1,0:T(8,128)S(1)} %cholesky.118), custom_call_target="Cholesky" | custom-call | tf_op jit(solution)/shard_map/jit(cholesky)/cholesky | solution.py:79
  143.6 9.8 %custom-call.15 = f32[1,128,128]{1,2,0:T(8,128)S(1)} custom-call(f32[1,128,128]{2,1,0:T(8,128)S(1)} %get-tuple-element.38), custom_call_target="InvertDiagBlocksLowerTriangular" | custom-call | tf_op jit(solution)/shard_map/jit(cholesky)/cholesky | solution.py:79
  153.9 11.7 %cholesky.105 = f32[128,128]{1,0:T(8,128)S(1)} custom-call(f32[128,128]{1,0:T(8,128)S(1)} %convolution_subtract_fusion.1), custom_call_target="Cholesky" | custom-call | tf_op jit(solution)/shard_map/jit(cholesky)/cholesky | solution.py:79
  167.7 4.2 %while.1 = (s32[]{:T(128)}, f32[256,256]{1,0:T(8,128)S(1)}, s32[2,2]{1,0:T(2,128)S(1)}, f32[2,128,128]{2,1,0:T(8,128)S(1)}, s32[]{:T(128)}) while((s32[]{:T(128)}, f32[256,256]{1,0:T(8,128)S(1)}, s32[2,2]{1,0:T(2,128)S(1)}, f32[2,128,128]{2,1,0:T(8,128)S(1)}, s32[]{:T(128)}) %tuple.32), condition=%wide.while_cond, body=%wide.while_body.sunk | while | flops 2 | bytes 131181 | solution.py:80
  171.9 19.7 %custom-call.16 = f32[2,128,128]{1,2,0:T(8,128)S(1)} custom-call(f32[2,128,128]{2,1,0:T(8,128)S(1)} %get-tuple-element.10), custom_call_target="InvertDiagBlocksLowerTriangular" | custom-call | tf_op jit(solution)/shard_map/jit(_solve_triangular)/triangular_solve | solution.py:80
  192.5 3.3 %all-to-all-start.4 = ((f32[8,4,256]{2,1,0:T(4,128)}), f32[8,4,256]{2,1,0:T(4,128)S(1)}, u32[]{:S(2)}, u32[]{:S(2)}) async-start(f32[8,4,256]{2,1,0:T(4,128)} %reshape.58), calls=%async_computation.4 | async-start | bytes 65536 | tf_op jit(solution)/shard_map/all_to_all | solution.py:34
  197.3 5.4 %all-to-all-done.4 = f32[8,4,256]{2,1,0:T(4,128)S(1)} async-done(((f32[8,4,256]{2,1,0:T(4,128)}), f32[8,4,256]{2,1,0:T(4,128)S(1)}, u32[]{:S(2)}, u32[]{:S(2)}) %all-to-all-start.4) | async-done | bytes 32800 | tf_op jit(solution)/shard_map/all_to_all | solution.py:34
  203.3 3.5 %all-to-all-start.5 = ((f32[12,4,256]{2,1,0:T(4,128)}), f32[12,4,256]{2,1,0:T(4,128)S(1)}, u32[]{:S(2)}, u32[]{:S(2)}) async-start(f32[12,4,256]{2,1,0:T(4,128)} %broadcast_in_dim.14), calls=%async_computation.5 | async-start | bytes 98304 | tf_op jit(solution)/shard_map/all_to_all | solution.py:19
  207.1 9.3 %all-to-all-done.5 = f32[12,4,256]{2,1,0:T(4,128)S(1)} async-done(((f32[12,4,256]{2,1,0:T(4,128)}), f32[12,4,256]{2,1,0:T(4,128)S(1)}, u32[]{:S(2)}, u32[]{:S(2)}) %all-to-all-start.5) | async-done | bytes 49184 | tf_op jit(solution)/shard_map/all_to_all | solution.py:19
  217.1 3.9 %all-to-all-start.6 = ((f32[32,4,256]{2,1,0:T(4,128)}), f32[32,4,256]{2,1,0:T(4,128)S(1)}, u32[]{:S(2)}, u32[]{:S(2)}) async-start(f32[32,4,256]{2,1,0:T(4,128)} %broadcast_in_dim.15), calls=%async_computation.6 | async-start | bytes 262144 | tf_op jit(solution)/shard_map/all_to_all | solution.py:19
  221.9 8.2 %all-to-all-done.6 = f32[32,4,256]{2,1,0:T(4,128)S(1)} async-done(((f32[32,4,256]{2,1,0:T(4,128)}), f32[32,4,256]{2,1,0:T(4,128)S(1)}, u32[]{:S(2)}, u32[]{:S(2)}) %all-to-all-start.6) | async-done | bytes 131104 | tf_op jit(solution)/shard_map/all_to_all | solution.py:19
  230.2 5.4 %all_gather.15 = f32[256,256]{1,0:T(8,128)S(1)} all-gather(f32[128,256]{1,0:T(8,128)S(1)} %reshape.59), channel_id=1, replica_groups=mesh['z'=12,'y'=8,'c'=2,'x'=4] {'c'}, dimensions={0}, use_global_device_ids=true | all-gather | bytes 393216 | tf_op jit(solution)/shard_map/all_gather | solution.py:77
  236.0 4.9 %fusion = bf16[16,4608]{1,0:T(8,128)(2,1)S(1)} fusion(bf16[4608,768]{1,0:T(8,128)(2,1)} %all-gather.2.cloned.1.call-done, s32[16]{0:T(128)S(1)} %iota_add_fusion, bf16[]{:T(256)S(6)} %convert_element_type.29), kind=kOutput, calls=%fused_computation.3 | convolution fusion | flops 113418240 | bytes 7225410 | tf_op jit(solution)/shard_map/dot_general | solution.py:86
  249.2 4.7 %convolution_add_fusion = f32[16,768]{1,0:T(8,128)} fusion(bf16[4608,768]{1,0:T(8,128)(2,1)} %all-gather.2.cloned.1.call-done, bf16[16,4608]{1,0:T(8,128)(2,1)S(1)} %collective-permute-done.3, bf16[16,4608]{1,0:T(8,128)(2,1)S(1)} %collective-permute-done.2, bf16[16,4608]{1,0:T(8,128)(2,1)S(1)} %fusion, bf16[16,4608]{1,0:T(8,128)(2,1)S(1)} %collective-permute-done.1, ...), kind=kOutput, calls=%fused_computation.7 | convolution fusion | flops 113491968 | bytes 7766016 | tf_op jit(solution)/shard_map/dot_general | solution.py:95
  (83 shorter events, 33.5 us)
Async XLA Ops:
  7.2 100.6 %copy-start = (bf16[768,20]{0,1:T(8,128)(2,1)S(1)}, bf16[768,20]{0,1:T(8,128)(2,1)}, u32[]{:S(2)}) copy-start(bf16[768,20]{0,1:T(8,128)(2,1)} %param.4) | copy-start | bytes 92164
  7.2 101.0 %copy-start.1 = (f32[16,768]{1,0:T(8,128)S(1)}, f32[16,768]{1,0:T(8,128)}, u32[]{:S(2)}) copy-start(f32[16,768]{1,0:T(8,128)} %param.3) | copy-start | bytes 147460
  7.2 228.8 %all-gather.2.cloned.1.call-start = ((), (), s32[]{:S(2)}) async-start(), calls=%async_computation.7 | async-start | bytes 7114752 | tf_op jit(solution)/shard_map/all_gather | solution.py:49
  12.5 9.8 %all-to-all-start = ((f32[4,36,256]{2,1,0:T(8,128)}), f32[4,36,256]{2,1,0:T(8,128)S(1)}, u32[]{:S(2)}, u32[]{:S(2)}) async-start(f32[4,36,256]{2,1,0:T(8,128)} %broadcast_in_dim.11), calls=%async_computation | async-start | bytes 327680 | tf_op jit(solution)/shard_map/all_to_all | solution.py:19
  23.3 13.4 %collective-permute-start = (f32[384,256]{1,0:T(8,128)S(1)}, f32[384,256]{1,0:T(8,128)S(1)}, u32[]{:S(2)}, u32[]{:S(2)}) collective-permute-start(f32[384,256]{1,0:T(8,128)S(1)} %constant_dynamic-slice_fusion.3), channel_id=1, source_target_pairs={{0,4},{4,0},{1,5},{5,1},{2,6},{6,2},{3,7},{7,3},{8,12},{12,8},{9,1... | collective-permute-start | bytes 1179656 | tf_op jit(solution)/shard_map/ppermute | solution.py:23
  73.6 27.5 %all-to-all-start.2 = ((f32[96,4,256]{2,1,0:T(4,128)}), f32[96,4,256]{2,1,0:T(4,128)S(1)}, u32[]{:S(2)}, u32[]{:S(2)}) async-start(f32[96,4,256]{2,1,0:T(4,128)} %broadcast_in_dim.12), calls=%async_computation.2 | async-start | bytes 786432 | tf_op jit(solution)/shard_map/all_to_all | solution.py:19
  110.5 15.2 %all-to-all-start.3 = ((f32[4,180,256]{2,1,0:T(8,128)}), f32[4,180,256]{2,1,0:T(8,128)S(1)}, u32[]{:S(2)}, u32[]{:S(2)}) async-start(f32[4,180,256]{2,1,0:T(8,128)} %broadcast_in_dim.13), calls=%async_computation.3 | async-start | bytes 1507328 | tf_op jit(solution)/shard_map/all_to_all | solution.py:19
  126.2 65.6 %collective-permute-start.4 = (f32[32,256]{1,0:T(8,128)S(1)}, f32[32,256]{1,0:T(8,128)S(1)}, u32[]{:S(2)}, u32[]{:S(2)}) collective-permute-start(f32[32,256]{1,0:T(8,128)S(1)} %constant_dynamic-slice_fusion.1), channel_id=1, source_target_pairs={{0,4},{4,0},{1,5},{5,1},{2,6},{6,2},{3,7},{7,3},{8,12},{12,8},{9,1... | collective-permute-start | bytes 98312 | tf_op jit(solution)/shard_map/ppermute | solution.py:23
  192.5 10.1 %all-to-all-start.4 = ((f32[8,4,256]{2,1,0:T(4,128)}), f32[8,4,256]{2,1,0:T(4,128)S(1)}, u32[]{:S(2)}, u32[]{:S(2)}) async-start(f32[8,4,256]{2,1,0:T(4,128)} %reshape.58), calls=%async_computation.4 | async-start | bytes 65536 | tf_op jit(solution)/shard_map/all_to_all | solution.py:34
  203.3 13.1 %all-to-all-start.5 = ((f32[12,4,256]{2,1,0:T(4,128)}), f32[12,4,256]{2,1,0:T(4,128)S(1)}, u32[]{:S(2)}, u32[]{:S(2)}) async-start(f32[12,4,256]{2,1,0:T(4,128)} %broadcast_in_dim.14), calls=%async_computation.5 | async-start | bytes 98304 | tf_op jit(solution)/shard_map/all_to_all | solution.py:19
  217.1 13.0 %all-to-all-start.6 = ((f32[32,4,256]{2,1,0:T(4,128)}), f32[32,4,256]{2,1,0:T(4,128)S(1)}, u32[]{:S(2)}, u32[]{:S(2)}) async-start(f32[32,4,256]{2,1,0:T(4,128)} %broadcast_in_dim.15), calls=%async_computation.6 | async-start | bytes 262144 | tf_op jit(solution)/shard_map/all_to_all | solution.py:19
  240.9 6.2 %collective-permute-start.1 = (bf16[16,4608]{1,0:T(8,128)(2,1)S(1)}, bf16[16,4608]{1,0:T(8,128)(2,1)S(1)}, u32[]{:S(2)}, u32[]{:S(2)}) collective-permute-start(bf16[16,4608]{1,0:T(8,128)(2,1)S(1)} %fusion), channel_id=1, source_target_pairs={{0,1},{4,5},{8,9},{12,13},{16,17},{20,21},{24,25},{28,29},{32,33},... | collective-permute-start | bytes 442376 | tf_op jit(solution)/shard_map/ppermute | solution.py:94
  243.2 6.0 %collective-permute-start.2 = (bf16[16,4608]{1,0:T(8,128)(2,1)S(1)}, bf16[16,4608]{1,0:T(8,128)(2,1)S(1)}, u32[]{:S(2)}, u32[]{:S(2)}) collective-permute-start(bf16[16,4608]{1,0:T(8,128)(2,1)S(1)} %fusion), channel_id=1, source_target_pairs={{0,2},{4,6},{8,10},{12,14},{16,18},{20,22},{24,26},{28,30},{32,34}... | collective-permute-start | bytes 442376 | tf_op jit(solution)/shard_map/ppermute | solution.py:94
  244.5 4.6 %collective-permute-start.3 = (bf16[16,4608]{1,0:T(8,128)(2,1)S(1)}, bf16[16,4608]{1,0:T(8,128)(2,1)S(1)}, u32[]{:S(2)}, u32[]{:S(2)}) collective-permute-start(bf16[16,4608]{1,0:T(8,128)(2,1)S(1)} %fusion), channel_id=1, source_target_pairs={{0,3},{4,7},{8,11},{12,15},{16,19},{20,23},{24,27},{28,31},{32,35}... | collective-permute-start | bytes 442376 | tf_op jit(solution)/shard_map/ppermute | solution.py:94
Sparse Core Ops, SparseCore 0:
  11.8 135.4 all-gather.1

commit v3 on v2

--- a/solution.py
+++ b/solution.py
@@ -1,6 +1,8 @@
 import jax
 import jax.numpy as jnp
 from jax import lax
+from jax.experimental import pallas as pl
+from jax.experimental.pallas import tpu as pltpu
 from jax.sharding import Mesh, PartitionSpec as P
 
 B = 3072
@@ -8,6 +10,8 @@
 NZ, NY, NC, NX = 12, 8, 2, 4
 ALL = ("z", "y", "c", "x")
 F32 = jnp.float32
+BF16 = jnp.bfloat16
+R, PANEL, GROUP, LANES = 256, 32, 8, 128
 HI = lax.Precision.HIGHEST
 
 
@@ -38,6 +42,66 @@
     return v.reshape(v.shape[0] * v.shape[1], v.shape[2])
 
 
+def split3(v):
+    high = v.astype(BF16); rest = v - high.astype(F32)
+    mid = rest.astype(BF16)
+    return high, mid, (rest - mid.astype(F32)).astype(BF16)
+
+
+def panel_step(k, a_ref, x_ref, inv_ref):
+    tile = k * PANEL // LANES
+    rows = slice(k * PANEL, (k + 1) * PANEL)
+    n_a = 2 - tile
+    w = [a_ref[rows, t * LANES:(t + 1) * LANES] for t in range(tile, 2)]
+    w += [x_ref[rows, t * LANES:(t + 1) * LANES] for t in range(tile + 1)]
+    lane0 = k * PANEL - tile * LANES
+    row = lax.broadcasted_iota(jnp.int32, (PANEL, LANES), 0)
+    pivots = jnp.ones((PANEL, LANES), F32)
+    for g in range(PANEL // GROUP):
+        cols = [jnp.broadcast_to(w[0][:, lane0 + g * GROUP + j:lane0 + g * GROUP + j + 1], (PANEL, LANES)) for j in range(GROUP)]
+        for j in range(GROUP):
+            at = g * GROUP + j
+            pivot = cols[j][at:at + 1, :]
+            factor = jnp.where(row > at, cols[j] * (1.0 / pivot), 0.0)
+            for t in range(j + 1, GROUP):
+                cols[t] = cols[t] - factor * cols[t][at:at + 1, :]
+            w = [v - factor * v[at:at + 1, :] for v in w]
+            pivots = jnp.where(row == at, pivot, pivots)
+    scale = lax.rsqrt(pivots)
+    w = [v * scale for v in w]
+    for t in range(2):
+        inv_ref[rows, t * LANES:(t + 1) * LANES] = w[n_a + t] if t <= tile else jnp.zeros((PANEL, LANES), F32)
+    if k == R // PANEL - 1:
+        return
+    first = (k + 1) * PANEL // LANES
+    right = split3(jnp.concatenate(w, axis=1))
+    left = [s[:, (first - tile) * LANES:n_a * LANES] for s in right]
+    order = ((0, 0), (0, 1), (1, 0), (0, 2), (2, 0), (1, 1))
+    update = lax.dot_general(jnp.concatenate([left[i] for i, _ in order], axis=0), jnp.concatenate([right[j] for _, j in order], axis=0), (((0,), (0,)), ((), ())), preferred_element_type=F32)
+    below = slice(first * LANES, R)
+    a_ref[below, tile * LANES:] -= update[:, :n_a * LANES]
+    x_ref[below, :(tile + 1) * LANES] -= update[:, n_a * LANES:]
+
+
+def inverse_kernel(g_ref, after_ref, inv_ref, a_ref, x_ref):
+    a_ref[...] = g_ref[...]
+    x_ref[...] = (lax.broadcasted_iota(jnp.int32, (R, R), 0) == lax.broadcasted_iota(jnp.int32, (R, R), 1)).astype(F32)
+    for k in range(R // PANEL):
+        panel_step(k, a_ref, x_ref, inv_ref)
+
+
+def inverse_factor(gram_matrix, after):
+    return pl.pallas_call(
+        inverse_kernel,
+        out_shape=jax.ShapeDtypeStruct((R, R), F32),
+        in_specs=[pl.BlockSpec(memory_space=pltpu.VMEM), pl.BlockSpec(memory_space=pl.ANY)],
+        out_specs=pl.BlockSpec(memory_space=pltpu.VMEM),
+        scratch_shapes=[pltpu.VMEM((R, R), F32), pltpu.VMEM((R, R), F32)],
+        compiler_params=pltpu.CompilerParams(vmem_limit_bytes=24 << 20),
+        cost_estimate=pl.CostEstimate(flops=10**8, bytes_accessed=30 * 10**6, transcendentals=0),
+    )(gram_matrix, after)
+
+
 def shards(factor, gradient, sketch_ids):
     rows, cols = factor.shape
     z, y, c, x = (lax.axis_index(a) for a in ALL)
@@ -46,7 +110,7 @@
     mine = (x == owner).astype(F32)
 
     strip = jnp.pad(gradient.T, ((0, 4), (0, 0)))
-    plane = lax.all_gather(strip, ("z", "y", "c"), axis=0, tiled=True)
+    plane = lax.all_gather(strip, ("z", "y"), axis=0, tiled=True)
 
     grad32 = gradient.astype(F32)
     sketch = sketch_ids.astype(F32)
@@ -71,20 +135,18 @@
     right = jnp.concatenate([part[128 + rows + wide:], part[128 + rows:128 + rows + wide]], axis=0)
     core = dot(left, right, 0, 0).reshape(NC, NX, 32, 256)
     core = lax.dynamic_index_in_dim(core, x, 1, keepdims=False).reshape(64, 256)
-    core = scatter(scatter_core(core, c), "y", NY)
+    core = scatter_core(core, c)
+    inverse = inverse_factor(gram_matrix, core)
+    core = scatter(core, "y", NY)
+    late = (core[0, 0] > 0).astype(jnp.int32) >> 1
     core = jnp.sum(spread(core, "z", NZ), axis=0)
-    core = join(spread(core, ("x", "y"), NX * NY))
-    core = lax.all_gather(core, "c", axis=0, tiled=True)
 
-    lower_factor = jnp.linalg.cholesky(gram_matrix)
-    inverse = jax.scipy.linalg.solve_triangular(lower_factor, jnp.eye(256, dtype=F32), lower=True)
-    range_basis = dot(own_rows, inverse, 1, 1)
-    projected_core = dot(dot(inverse, core, 1, 0), inverse, 1, 1) / B
-
-    late = (lower_factor[0, 0] > 0).astype(jnp.int32) >> 1
-    place = (lax.broadcasted_iota(jnp.int32, (cols, rows), 0) == offset + late + lax.broadcasted_iota(jnp.int32, (cols, rows), 1))
-    picked = lax.dot_general(place.astype(jnp.bfloat16), plane, (((0,), (1,)), ((), ())), preferred_element_type=F32).astype(jnp.bfloat16)
-    picked = picked * mine.astype(jnp.bfloat16)
+    pair = 2 * rows
+    start = offset - rows * c + late
+    block = lax.dynamic_slice(plane, (0, start // LANES * LANES), (plane.shape[0], LANES))
+    place = (lax.broadcasted_iota(jnp.int32, (LANES, pair), 0) == start % LANES + lax.broadcasted_iota(jnp.int32, (LANES, pair), 1))
+    place = (place & (x == owner)).astype(BF16)
+    picked = lax.dot_general(place, block, (((0,), (1,)), ((), ())), preferred_element_type=F32).astype(BF16)
     total = picked
     for k in range(1, NX):
         pairs = []
@@ -93,7 +155,14 @@
             pairs.append((d * NX + src, d * NX + (src + k) % NX))
         total = total + lax.ppermute(picked, ALL, pairs)
     outer_sum = lax.dot_general(total, plane, (((1,), (0,)), ((), ())), preferred_element_type=F32)
-    factor_new = decay_rate * factor + outer_sum
+
+    core = join(spread(core, ("x", "y"), NX * NY))
+    core = core + 0.0 * outer_sum[:1, :1]
+    core = lax.all_gather(core, "c", axis=0, tiled=True)
+
+    range_basis = dot(own_rows, inverse, 1, 1)
+    projected_core = dot(dot(inverse, core, 1, 0), inverse, 1, 1) / B
+    factor_new = decay_rate * factor + scatter_core(outer_sum, c)
     return (factor_new, range_basis, projected_core)
 
 

time: 262 us -> 192 us (0.73)
  other arithmetic: 54.9 us -> 1.84 us
  waiting for transfers between devices: 62.4 us -> 44.9 us
  Pallas kernels: 0 us -> 7.65 us
  matrix products: 18.7 us -> 12.6 us
  starting transfers between devices: 46.2 us -> 52.1 us
  local copies, waits for them, and re-layouts: 11.8 us -> 7.16 us
    another operation x9 -> x0, other arithmetic: 53.7 us -> none  [the longest x6 33.9 us: shards(): lower_factor = jnp.linalg.cholesky(gram_matrix)]
    all_to_all x5, waiting for transfers between devices: 53.6 us -> 43.5 us  [spread(): return lax.all_to_all(jnp.broadcast_to(v[None], (n,) + v.shape), axis, 0, 0)]
    pallas_call x0 -> x1, Pallas kernels: none -> 7.65 us  [inverse_factor(): pl.pallas_call(inverse_kernel, out_shape=jax.ShapeDtypeStruct((R, R), F32...]
    all_to_all x1, waiting for transfers between devices: 5.36 us -> 0.01 us  [scatter(): lax.all_to_all(v.reshape(n, v.shape[0] // n, v.shape[1]), axis, 0, 0)]
    another operation x9 -> x0, local copies, waits for them, and re-layouts: 4.05 us -> none
    all_to_all x5, starting transfers between devices: 22.8 us -> 26.3 us  [spread(): return lax.all_to_all(jnp.broadcast_to(v[None], (n,) + v.shape), axis, 0, 0)]
    dot_general x1, matrix products: 4.93 us -> 1.4 us  [shards(): lax.dot_general(place, block, (((0,), (1,)), ((), ())), preferred_element...]
    ppermute x2 -> x3, starting transfers between devices: 15.2 us -> 17.4 us  [swap_core(): return lax.ppermute(v, 'c', [(0, 1), (1, 0)])]
  transfers between devices with their start and end apart: 12 -> 13, of which waited for: 8 -> 6; matrix products, arithmetic and copies ran while one was open for 29% -> 10% of each run, Pallas kernels for 0% -> 4%
where the time goes in v3:
time: 192 us; the launch traced here: 191 us
  starting transfers between devices  52.1 us (27%)
  blocking collectives  49.2 us (26%)
  waiting for transfers between devices  44.9 us (23%)
  between operations  15.7 us (8%)
  matrix products  12.6 us (7%)
  Pallas kernels  7.65 us (4%)
  local copies, waits for them, and re-layouts  7.16 us (4%)
    all_to_all x5, waiting for transfers between devices, spread(): return lax.all_to_all(jnp.broadcast_to(v[None], (n,) + v.shape), axis, 0, 0)  43.5 us
    all_to_all x1, blocking collectives, scatter(): lax.all_to_all(v.reshape(n, v.shape[0] // n, v.shape[1]), axis, 0, 0)  35.9 us
    all_to_all x5, starting transfers between devices, spread(): return lax.all_to_all(jnp.broadcast_to(v[None], (n,) + v.shape), axis, 0, 0)  26.3 us
    ppermute x3, starting transfers between devices, swap_core(): return lax.ppermute(v, 'c', [(0, 1), (1, 0)])  17.4 us
    dot_general x10, matrix products, dot(): lax.dot_general(a, b, (((ca,), (cb,)), ((), ())), precision=HI, preferred...  8.52 us
    pallas_call x1, Pallas kernels, inverse_factor(): pl.pallas_call(inverse_kernel, out_shape=jax.ShapeDtypeStruct((R, R), F32...  7.65 us
    all_gather x1, blocking collectives, shards(): ranged = lax.all_gather(piece, 'c', axis=0, tiled=True)  6.47 us
    all_gather x1, blocking collectives, shards(): core = lax.all_gather(core, 'c', axis=0, tiled=True)  4.88 us
  transfers between devices with their start and end apart: 13, of which 6 were waited for; matrix products, arithmetic and copies ran while one was open for 10% of the time, Pallas kernels for 4%

profile of v3, /device:TPU:1, one launch (start us, length us, event | category | flops | bytes accessed | tf_op | source)
XLA Modules:
  0.0 191.3 jit_solution(4673432377769671475)
XLA Ops:
  8.6 1.6 fusion.2
  10.2 1.6 convolution_multiply_fusion.2
  12.5 4.8 %all-to-all-start = ((f32[4,36,256]{2,1,0:T(8,128)}), f32[4,36,256]{2,1,0:T(8,128)S(1)}, u32[]{:S(2)}, u32[]{:S(2)}) async-start(f32[4,36,256]{2,1,0:T(8,128)} %broadcast_in_dim.10), calls=%async_computation | async-start | bytes 327680 | tf_op jit(solution)/shard_map/all_to_all | solution.py:23
  18.2 4.1 %all-to-all-done = f32[4,36,256]{2,1,0:T(8,128)S(1)} async-done(((f32[4,36,256]{2,1,0:T(8,128)}), f32[4,36,256]{2,1,0:T(8,128)S(1)}, u32[]{:S(2)}, u32[]{:S(2)}) %all-to-all-start) | async-done | bytes 147488 | tf_op jit(solution)/shard_map/all_to_all | solution.py:23
  23.2 12.0 %collective-permute-start = (f32[384,256]{1,0:T(8,128)S(1)}, f32[384,256]{1,0:T(8,128)S(1)}, u32[]{:S(2)}, u32[]{:S(2)}) collective-permute-start(f32[384,256]{1,0:T(8,128)S(1)} %constant_dynamic-slice_fusion.3), channel_id=1, source_target_pairs={{0,4},{4,0},{1,5},{5,1},{2,6},{6,2},{3,7},{7,3},{8,12},{12,8},{9,1... | collective-permute-start | bytes 1179656 | tf_op jit(solution)/shard_map/ppermute | solution.py:27
  36.8 35.9 %all_to_all.35 = f32[96,4,256]{2,1,0:T(4,128)S(1)} all-to-all(f32[96,4,256]{2,1,0:T(4,128)S(1)} %reshape.35), channel_id=1, replica_groups=mesh['z'=12,'y'=8,'c'=2,'x'=4] {'z','y'}, dimensions={0} | all-to-all | bytes 786432 | tf_op jit(solution)/shard_map/all_to_all | solution.py:38
  73.6 7.0 %all-to-all-start.2 = ((f32[96,4,256]{2,1,0:T(4,128)}), f32[96,4,256]{2,1,0:T(4,128)S(1)}, u32[]{:S(2)}, u32[]{:S(2)}) async-start(f32[96,4,256]{2,1,0:T(4,128)} %broadcast_in_dim.11), calls=%async_computation.2 | async-start | bytes 786432 | tf_op jit(solution)/shard_map/all_to_all | solution.py:23
  80.6 20.3 %all-to-all-done.2 = f32[96,4,256]{2,1,0:T(4,128)S(1)} async-done(((f32[96,4,256]{2,1,0:T(4,128)}), f32[96,4,256]{2,1,0:T(4,128)S(1)}, u32[]{:S(2)}, u32[]{:S(2)}) %all-to-all-start.2) | async-done | bytes 393248 | tf_op jit(solution)/shard_map/all_to_all | solution.py:23
  101.1 6.5 %all_gather.12 = f32[768,256]{1,0:T(8,128)S(1)} all-gather(f32[384,256]{1,0:T(8,128)S(1)} %reshape.36), channel_id=1, replica_groups=mesh['z'=12,'y'=8,'c'=2,'x'=4] {'c'}, dimensions={0}, use_global_device_ids=true | all-gather | bytes 1179648 | tf_op jit(solution)/shard_map/all_gather | solution.py:124
  110.3 3.5 %all-to-all-start.3 = ((f32[4,180,256]{2,1,0:T(8,128)}), f32[4,180,256]{2,1,0:T(8,128)S(1)}, u32[]{:S(2)}, u32[]{:S(2)}) async-start(f32[4,180,256]{2,1,0:T(8,128)} %broadcast_in_dim.12), calls=%async_computation.3 | async-start | bytes 1507328 | tf_op jit(solution)/shard_map/all_to_all | solution.py:23
  113.8 11.7 %all-to-all-done.3 = f32[4,180,256]{2,1,0:T(8,128)S(1)} async-done(((f32[4,180,256]{2,1,0:T(8,128)}), f32[4,180,256]{2,1,0:T(8,128)S(1)}, u32[]{:S(2)}, u32[]{:S(2)}) %all-to-all-start.3) | async-done | bytes 737312 | tf_op jit(solution)/shard_map/all_to_all | solution.py:23
  126.0 3.1 %collective-permute-start.1 = (f32[32,256]{1,0:T(8,128)S(1)}, f32[32,256]{1,0:T(8,128)S(1)}, u32[]{:S(2)}, u32[]{:S(2)}) collective-permute-start(f32[32,256]{1,0:T(8,128)S(1)} %constant_dynamic-slice_fusion.1), channel_id=1, source_target_pairs={{0,4},{4,0},{1,5},{5,1},{2,6},{6,2},{3,7},{7,3},{8,12},{12,8},{9,1... | collective-permute-start | bytes 98312 | tf_op jit(solution)/shard_map/ppermute | solution.py:27
  129.1 2.0 %all_gather.14 = f32[256,256]{1,0:T(8,128)S(1)} all-gather(f32[128,256]{1,0:T(8,128)S(1)} %slice.36), channel_id=1, replica_groups=mesh['z'=12,'y'=8,'c'=2,'x'=4] {'c'}, dimensions={0}, use_global_device_ids=true | all-gather | bytes 393216 | tf_op jit(solution)/shard_map/all_gather | solution.py:133
  131.8 3.5 %all-to-all-start.4 = ((f32[8,4,256]{2,1,0:T(4,128)}), f32[8,4,256]{2,1,0:T(4,128)S(1)}, u32[]{:S(2)}, u32[]{:S(2)}) async-start(f32[8,4,256]{2,1,0:T(4,128)} %reshape.39), calls=%async_computation.4 | async-start | bytes 65536 | tf_op jit(solution)/shard_map/all_to_all | solution.py:38
  135.3 7.7 %shard_map.58 = f32[256,256]{1,0:T(8,128)S(1)} custom-call(f32[256,256]{1,0:T(8,128)S(1)} %broadcast_multiply_fusion.g_ref, f32[32,256]{1,0:T(8,128)S(1)} %dynamic-slice_add_fusion.1.after_ref), custom_call_target="tpu_custom_call" | custom-call | flops 100000000 | bytes 30000000 | tf_op jit(solution)/shard_map/pallas_call | solution.py:94
  144.9 3.5 %all-to-all-start.5 = ((f32[12,4,256]{2,1,0:T(4,128)}), f32[12,4,256]{2,1,0:T(4,128)S(1)}, u32[]{:S(2)}, u32[]{:S(2)}) async-start(f32[12,4,256]{2,1,0:T(4,128)} %broadcast_in_dim.13), calls=%async_computation.5 | async-start | bytes 98304 | tf_op jit(solution)/shard_map/all_to_all | solution.py:23
  148.4 1.4 convolution_convert_fusion
  149.8 2.2 %collective-permute-start.2 = (bf16[32,2304]{1,0:T(8,128)(2,1)S(1)}, bf16[32,2304]{1,0:T(8,128)(2,1)S(1)}, u32[]{:S(2)}, u32[]{:S(2)}) collective-permute-start(bf16[32,2304]{1,0:T(8,128)(2,1)S(1)} %convolution_convert_fusion), channel_id=1, source_target_pairs={{0,1},{4,5},{8,9},{12,13},{16,17},{20,21},{24,25},{28,29},{32,33},... | collective-permute-start | bytes 442376 | tf_op jit(solution)/shard_map/ppermute | solution.py:156
  155.6 2.1 %all-to-all-done.5 = f32[12,4,256]{2,1,0:T(4,128)S(1)} async-done(((f32[12,4,256]{2,1,0:T(4,128)}), f32[12,4,256]{2,1,0:T(4,128)S(1)}, u32[]{:S(2)}, u32[]{:S(2)}) %all-to-all-start.5) | async-done | bytes 49184 | tf_op jit(solution)/shard_map/all_to_all | solution.py:23
  158.4 7.5 %all-to-all-start.6 = ((f32[32,4,256]{2,1,0:T(4,128)}), f32[32,4,256]{2,1,0:T(4,128)S(1)}, u32[]{:S(2)}, u32[]{:S(2)}) async-start(f32[32,4,256]{2,1,0:T(4,128)} %broadcast_in_dim.14), calls=%async_computation.6 | async-start | bytes 262144 | tf_op jit(solution)/shard_map/all_to_all | solution.py:23
  165.9 2.7 %fusion.7 = f32[32,768]{1,0:T(8,128)S(1)} fusion(bf16[2304,768]{1,0:T(8,128)(2,1)} %all-gather.2.cloned.1.call-done, bf16[32,2304]{1,0:T(8,128)(2,1)S(1)} %collective-permute-done.4, bf16[32,2304]{1,0:T(8,128)(2,1)S(1)} %collective-permute-done.3, bf16[32,2304]{1,0:T(8,128)(2,1)S(1)} %convolution_convert_fusion, bf16[32,2304]{1,0:T(8,128)(2,1)S(1)} %collective-permute-done.2), kind=kOutput, calls=%fused_computation.14 | convolution fusion | flops 113467392 | bytes 4227072 | tf_op jit(solution)/shard_map/dot_general | solution.py:157
  169.8 5.3 %all-to-all-done.6 = f32[32,4,256]{2,1,0:T(4,128)S(1)} async-done(((f32[32,4,256]{2,1,0:T(4,128)}), f32[32,4,256]{2,1,0:T(4,128)S(1)}, u32[]{:S(2)}, u32[]{:S(2)}) %all-to-all-start.6) | async-done | bytes 131104 | tf_op jit(solution)/shard_map/all_to_all | solution.py:23
  175.1 4.9 %all_gather.15 = f32[256,256]{1,0:T(8,128)S(1)} all-gather(f32[128,256]{1,0:T(8,128)S(1)} %add.128), channel_id=1, replica_groups=mesh['z'=12,'y'=8,'c'=2,'x'=4] {'c'}, dimensions={0}, use_global_device_ids=true | all-gather | bytes 393216 | tf_op jit(solution)/shard_map/all_gather | solution.py:161
  180.4 2.3 %collective-permute-start.5 = (f32[16,768]{1,0:T(8,128)S(1)}, f32[16,768]{1,0:T(8,128)S(1)}, u32[]{:S(2)}, u32[]{:S(2)}) collective-permute-start(f32[16,768]{1,0:T(8,128)S(1)} %constant_dynamic-slice_fusion), channel_id=1, source_target_pairs={{0,4},{4,0},{1,5},{5,1},{2,6},{6,2},{3,7},{7,3},{8,12},{12,8},{9,1... | collective-permute-start | bytes 147464 | tf_op jit(solution)/shard_map/ppermute | solution.py:27
  (60 shorter events, 18.4 us)
Async XLA Ops:
  7.2 141.2 %all-gather.2.cloned.1.call-start = ((), (), s32[]{:S(2)}) async-start(), calls=%async_computation.7 | async-start | bytes 3575808 | tf_op jit(solution)/shard_map/all_gather | solution.py:113
  12.5 9.8 %all-to-all-start = ((f32[4,36,256]{2,1,0:T(8,128)}), f32[4,36,256]{2,1,0:T(8,128)S(1)}, u32[]{:S(2)}, u32[]{:S(2)}) async-start(f32[4,36,256]{2,1,0:T(8,128)} %broadcast_in_dim.10), calls=%async_computation | async-start | bytes 327680 | tf_op jit(solution)/shard_map/all_to_all | solution.py:23
  23.2 84.4 %copy-start = (bf16[768,20]{0,1:T(8,128)(2,1)S(1)}, bf16[768,20]{0,1:T(8,128)(2,1)}, u32[]{:S(2)}) copy-start(bf16[768,20]{0,1:T(8,128)(2,1)} %param.4) | copy-start | bytes 92164
  23.2 13.4 %collective-permute-start = (f32[384,256]{1,0:T(8,128)S(1)}, f32[384,256]{1,0:T(8,128)S(1)}, u32[]{:S(2)}, u32[]{:S(2)}) collective-permute-start(f32[384,256]{1,0:T(8,128)S(1)} %constant_dynamic-slice_fusion.3), channel_id=1, source_target_pairs={{0,4},{4,0},{1,5},{5,1},{2,6},{6,2},{3,7},{7,3},{8,12},{12,8},{9,1... | collective-permute-start | bytes 1179656 | tf_op jit(solution)/shard_map/ppermute | solution.py:27
  35.3 72.7 %copy-start.1 = (f32[16,768]{1,0:T(8,128)S(1)}, f32[16,768]{1,0:T(8,128)}, u32[]{:S(2)}) copy-start(f32[16,768]{1,0:T(8,128)} %param.3) | copy-start | bytes 147460
  73.6 27.4 %all-to-all-start.2 = ((f32[96,4,256]{2,1,0:T(4,128)}), f32[96,4,256]{2,1,0:T(4,128)S(1)}, u32[]{:S(2)}, u32[]{:S(2)}) async-start(f32[96,4,256]{2,1,0:T(4,128)} %broadcast_in_dim.11), calls=%async_computation.2 | async-start | bytes 786432 | tf_op jit(solution)/shard_map/all_to_all | solution.py:23
  110.3 15.2 %all-to-all-start.3 = ((f32[4,180,256]{2,1,0:T(8,128)}), f32[4,180,256]{2,1,0:T(8,128)S(1)}, u32[]{:S(2)}, u32[]{:S(2)}) async-start(f32[4,180,256]{2,1,0:T(8,128)} %broadcast_in_dim.12), calls=%async_computation.3 | async-start | bytes 1507328 | tf_op jit(solution)/shard_map/all_to_all | solution.py:23
  126.0 5.1 %collective-permute-start.1 = (f32[32,256]{1,0:T(8,128)S(1)}, f32[32,256]{1,0:T(8,128)S(1)}, u32[]{:S(2)}, u32[]{:S(2)}) collective-permute-start(f32[32,256]{1,0:T(8,128)S(1)} %constant_dynamic-slice_fusion.1), channel_id=1, source_target_pairs={{0,4},{4,0},{1,5},{5,1},{2,6},{6,2},{3,7},{7,3},{8,12},{12,8},{9,1... | collective-permute-start | bytes 98312 | tf_op jit(solution)/shard_map/ppermute | solution.py:27
  131.8 11.2 %all-to-all-start.4 = ((f32[8,4,256]{2,1,0:T(4,128)}), f32[8,4,256]{2,1,0:T(4,128)S(1)}, u32[]{:S(2)}, u32[]{:S(2)}) async-start(f32[8,4,256]{2,1,0:T(4,128)} %reshape.39), calls=%async_computation.4 | async-start | bytes 65536 | tf_op jit(solution)/shard_map/all_to_all | solution.py:38
  144.9 12.8 %all-to-all-start.5 = ((f32[12,4,256]{2,1,0:T(4,128)}), f32[12,4,256]{2,1,0:T(4,128)S(1)}, u32[]{:S(2)}, u32[]{:S(2)}) async-start(f32[12,4,256]{2,1,0:T(4,128)} %broadcast_in_dim.13), calls=%async_computation.5 | async-start | bytes 98304 | tf_op jit(solution)/shard_map/all_to_all | solution.py:23
  149.8 16.1 %collective-permute-start.2 = (bf16[32,2304]{1,0:T(8,128)(2,1)S(1)}, bf16[32,2304]{1,0:T(8,128)(2,1)S(1)}, u32[]{:S(2)}, u32[]{:S(2)}) collective-permute-start(bf16[32,2304]{1,0:T(8,128)(2,1)S(1)} %convolution_convert_fusion), channel_id=1, source_target_pairs={{0,1},{4,5},{8,9},{12,13},{16,17},{20,21},{24,25},{28,29},{32,33},... | collective-permute-start | bytes 442376 | tf_op jit(solution)/shard_map/ppermute | solution.py:156
  152.0 13.9 %collective-permute-start.3 = (bf16[32,2304]{1,0:T(8,128)(2,1)S(1)}, bf16[32,2304]{1,0:T(8,128)(2,1)S(1)}, u32[]{:S(2)}, u32[]{:S(2)}) collective-permute-start(bf16[32,2304]{1,0:T(8,128)(2,1)S(1)} %convolution_convert_fusion), channel_id=1, source_target_pairs={{0,2},{4,6},{8,10},{12,14},{16,18},{20,22},{24,26},{28,30},{32,34}... | collective-permute-start | bytes 442376 | tf_op jit(solution)/shard_map/ppermute | solution.py:156
  153.3 12.6 %collective-permute-start.4 = (bf16[32,2304]{1,0:T(8,128)(2,1)S(1)}, bf16[32,2304]{1,0:T(8,128)(2,1)S(1)}, u32[]{:S(2)}, u32[]{:S(2)}) collective-permute-start(bf16[32,2304]{1,0:T(8,128)(2,1)S(1)} %convolution_convert_fusion), channel_id=1, source_target_pairs={{0,3},{4,7},{8,11},{12,15},{16,19},{20,23},{24,27},{28,31},{32,35}... | collective-permute-start | bytes 442376 | tf_op jit(solution)/shard_map/ppermute | solution.py:156
  158.4 16.6 %all-to-all-start.6 = ((f32[32,4,256]{2,1,0:T(4,128)}), f32[32,4,256]{2,1,0:T(4,128)S(1)}, u32[]{:S(2)}, u32[]{:S(2)}) async-start(f32[32,4,256]{2,1,0:T(4,128)} %broadcast_in_dim.14), calls=%async_computation.6 | async-start | bytes 262144 | tf_op jit(solution)/shard_map/all_to_all | solution.py:23
  180.4 3.4 %collective-permute-start.5 = (f32[16,768]{1,0:T(8,128)S(1)}, f32[16,768]{1,0:T(8,128)S(1)}, u32[]{:S(2)}, u32[]{:S(2)}) collective-permute-start(f32[16,768]{1,0:T(8,128)S(1)} %constant_dynamic-slice_fusion), channel_id=1, source_target_pairs={{0,4},{4,0},{1,5},{5,1},{2,6},{6,2},{3,7},{7,3},{8,12},{12,8},{9,1... | collective-permute-start | bytes 147464 | tf_op jit(solution)/shard_map/ppermute | solution.py:27
Sparse Core Ops, SparseCore 0:
  11.7 129.7 all-gather.1

commit v4 on v3

--- a/solution.py
+++ b/solution.py
@@ -36,6 +36,10 @@
 
 def scatter(v, axis, n):
     return jnp.sum(lax.all_to_all(v.reshape(n, v.shape[0] // n, v.shape[1]), axis, 0, 0), axis=0)
+
+
+def after(v, w):
+    return v + (0.0 * w[:1, :1]).astype(v.dtype)
 
 
 def join(v):
@@ -102,6 +106,32 @@
     )(gram_matrix, after)
 
 
+def front_kernel(grad_ref, factor_ref, sketch_ref, small_ref, strip_ref):
+    wide, rows = grad_ref.shape[0], factor_ref.shape[0]
+    sketch = sketch_ref[...].astype(F32).astype(BF16)
+    grad = grad_ref[...]
+    strip_ref[...] = jnp.concatenate([grad.astype(F32), jnp.zeros((strip_ref.shape[0] - wide, grad.shape[1]), F32)], axis=0).astype(BF16)
+    inner = jnp.dot(grad, sketch, preferred_element_type=F32)
+    parts = jnp.dot(jnp.concatenate(split3(factor_ref[...]), axis=0), sketch, preferred_element_type=F32)
+    decayed = decay_rate * (parts[:rows] + (parts[rows:2 * rows] + parts[2 * rows:]))
+    for k in range(NX):
+        small_ref[k, :wide, :] = inner
+        small_ref[k, wide:, :] = decayed
+
+
+def front(grad, factor, sketch_ids):
+    wide, rows, cols = grad.shape[0], factor.shape[0], sketch_ids.shape[1]
+    whole = pl.BlockSpec(memory_space=pltpu.VMEM)
+    return pl.pallas_call(
+        front_kernel,
+        out_shape=(jax.ShapeDtypeStruct((NX, wide + rows, cols), F32), jax.ShapeDtypeStruct((24, grad.shape[1]), BF16)),
+        in_specs=[whole] * 3,
+        out_specs=(whole, whole),
+        compiler_params=pltpu.CompilerParams(vmem_limit_bytes=24 << 20),
+        cost_estimate=pl.CostEstimate(flops=10**8, bytes_accessed=4 * 10**6, transcendentals=0),
+    )(grad, factor, sketch_ids)
+
+
 def shards(factor, gradient, sketch_ids):
     rows, cols = factor.shape
     z, y, c, x = (lax.axis_index(a) for a in ALL)
@@ -109,13 +139,10 @@
     offset = rows * (((z % (NZ // NX)) * NY + y) * NC + c)
     mine = (x == owner).astype(F32)
 
-    strip = jnp.pad(gradient.T, ((0, 4), (0, 0)))
+    small, strip = front(gradient.T, factor, sketch_ids)
     plane = lax.all_gather(strip, ("z", "y"), axis=0, tiled=True)
-
     grad32 = gradient.astype(F32)
-    sketch = sketch_ids.astype(F32)
-    small = jnp.concatenate([dot(grad32, sketch, 0, 0), decay_rate * dot(factor, sketch, 1, 0)], axis=0)
-    small = jnp.sum(spread(small, "x", NX), axis=0)
+    small = jnp.sum(lax.all_to_all(small, "x", 0, 0), axis=0)
     inner, decayed = small[:gradient.shape[1]], small[gradient.shape[1]:]
     place = (lax.broadcasted_iota(jnp.int32, (cols, rows), 0) == offset + lax.broadcasted_iota(jnp.int32, (cols, rows), 1)).astype(F32)
     partial = dot(jnp.concatenate([grad32, mine * place], axis=1), jnp.concatenate([inner, decayed], axis=0), 1, 0)
@@ -128,14 +155,14 @@
     wide = gradient.shape[1]
     part = jnp.concatenate([gram, here, dot(grad32, ranged, 0, 0), decay_rate * dot(factor, ranged, 1, 0)], axis=0)
     part = jnp.sum(spread(part, "x", NX), axis=0)
-    gram, own_rows = part[:128], part[128:128 + rows]
+    own_rows = part[128:128 + rows]
     left = part[128:128 + rows + wide]
-    gram_matrix = lax.all_gather(gram, "c", axis=0, tiled=True) / B
-
     right = jnp.concatenate([part[128 + rows + wide:], part[128 + rows:128 + rows + wide]], axis=0)
     core = dot(left, right, 0, 0).reshape(NC, NX, 32, 256)
     core = lax.dynamic_index_in_dim(core, x, 1, keepdims=False).reshape(64, 256)
-    core = scatter_core(core, c)
+    both = lax.all_gather(jnp.concatenate([part[:128], core], axis=0), "c", axis=0, tiled=False)
+    gram_matrix = both[:, :128].reshape(R, R) / B
+    core = lax.dynamic_slice_in_dim(both[0, 128:] + both[1, 128:], 32 * c, 32, 0)
     inverse = inverse_factor(gram_matrix, core)
     core = scatter(core, "y", NY)
     late = (core[0, 0] > 0).astype(jnp.int32) >> 1
@@ -155,14 +182,14 @@
             pairs.append((d * NX + src, d * NX + (src + k) % NX))
         total = total + lax.ppermute(picked, ALL, pairs)
     outer_sum = lax.dot_general(total, plane, (((1,), (0,)), ((), ())), preferred_element_type=F32)
+    factor_new = decay_rate * factor + scatter_core(outer_sum, c)
 
     core = join(spread(core, ("x", "y"), NX * NY))
-    core = core + 0.0 * outer_sum[:1, :1]
+    core = after(core, factor_new)
     core = lax.all_gather(core, "c", axis=0, tiled=True)
 
     range_basis = dot(own_rows, inverse, 1, 1)
     projected_core = dot(dot(inverse, core, 1, 0), inverse, 1, 1) / B
-    factor_new = decay_rate * factor + scatter_core(outer_sum, c)
     return (factor_new, range_basis, projected_core)
 
 

time: 192 us -> 192 us (level)
  matrix products: 12.6 us -> 9.46 us
    all_to_all x5 -> x4, waiting for transfers between devices: 43.5 us -> 32.2 us  [spread(): return lax.all_to_all(jnp.broadcast_to(v[None], (n,) + v.shape), axis, 0, 0)]
    all_to_all x5 -> x4, starting transfers between devices: 26.3 us -> 18.6 us  [spread(): return lax.all_to_all(jnp.broadcast_to(v[None], (n,) + v.shape), axis, 0, 0)]
    all_to_all x1, waiting for transfers between devices: 0.01 us -> 6.79 us  [scatter(): lax.all_to_all(v.reshape(n, v.shape[0] // n, v.shape[1]), axis, 0, 0)]
    all_to_all x0 -> x1, starting transfers between devices: none -> 4.85 us  [shards(): small = jnp.sum(lax.all_to_all(small, 'x', 0, 0), axis=0)]
    all_to_all x0 -> x1, waiting for transfers between devices: none -> 4.15 us  [shards(): small = jnp.sum(lax.all_to_all(small, 'x', 0, 0), axis=0)]
    ppermute x3 -> x2, starting transfers between devices: 17.4 us -> 21.5 us  [swap_core(): return lax.ppermute(v, 'c', [(0, 1), (1, 0)])]
    dot_general x10 -> x8, matrix products: 8.52 us -> 5.38 us  [dot(): lax.dot_general(a, b, (((ca,), (cb,)), ((), ())), precision=HI, preferred...]
    unnamed x4 -> x12, local copies, waits for them, and re-layouts: 0.04 us -> 2.73 us
  transfers between devices with their start and end apart: 13 -> 12, of which waited for: 6 -> 5; matrix products, arithmetic and copies ran while one was open for 10% -> 7% of each run, Pallas kernels for 4% -> 4%
where the time goes in v4:
time: 192 us; the launch traced here: 191 us
  starting transfers between devices  53.3 us (28%)
  blocking collectives  50.4 us (26%)
  waiting for transfers between devices  44.4 us (23%)
  between operations  15.7 us (8%)
  matrix products  9.46 us (5%)
  Pallas kernels  8.57 us (4%)
  local copies, waits for them, and re-layouts  7.81 us (4%)
    all_to_all x1, blocking collectives, scatter(): lax.all_to_all(v.reshape(n, v.shape[0] // n, v.shape[1]), axis, 0, 0)  35.9 us
    all_to_all x4, waiting for transfers between devices, spread(): return lax.all_to_all(jnp.broadcast_to(v[None], (n,) + v.shape), axis, 0, 0)  32.2 us
    ppermute x2, starting transfers between devices, swap_core(): return lax.ppermute(v, 'c', [(0, 1), (1, 0)])  21.5 us
    all_to_all x4, starting transfers between devices, spread(): return lax.all_to_all(jnp.broadcast_to(v[None], (n,) + v.shape), axis, 0, 0)  18.6 us
    pallas_call x1, Pallas kernels, inverse_factor(): pl.pallas_call(inverse_kernel, out_shape=jax.ShapeDtypeStruct((R, R), F32...  7.65 us
    all_to_all x1, waiting for transfers between devices, scatter(): lax.all_to_all(v.reshape(n, v.shape[0] // n, v.shape[1]), axis, 0, 0)  6.79 us
    all_gather x1, blocking collectives, shards(): ranged = lax.all_gather(piece, 'c', axis=0, tiled=True)  6.32 us
    dot_general x8, matrix products, dot(): lax.dot_general(a, b, (((ca,), (cb,)), ((), ())), precision=HI, preferred...  5.38 us
  transfers between devices with their start and end apart: 12, of which 5 were waited for; matrix products, arithmetic and copies ran while one was open for 7% of the time, Pallas kernels for 4%

profile of v4, /device:TPU:1, one launch (start us, length us, event | category | flops | bytes accessed | tf_op | source)
XLA Modules:
  0.0 190.9 jit_solution(367062358352245832)
XLA Ops:
  7.2 1.1 copy-done
  10.9 4.9 %all-to-all-start = ((f32[4,36,256]{2,1,0:T(8,128)}), f32[4,36,256]{2,1,0:T(8,128)S(1)}, u32[]{:S(2)}, u32[]{:S(2)}) async-start(f32[4,36,256]{2,1,0:T(8,128)} %get-tuple-element.5), calls=%async_computation | async-start | bytes 327680 | tf_op jit(solution)/shard_map/all_to_all | solution.py:145
  16.6 4.1 %all-to-all-done = f32[4,36,256]{2,1,0:T(8,128)S(1)} async-done(((f32[4,36,256]{2,1,0:T(8,128)}), f32[4,36,256]{2,1,0:T(8,128)S(1)}, u32[]{:S(2)}, u32[]{:S(2)}) %all-to-all-start) | async-done | bytes 147488 | tf_op jit(solution)/shard_map/all_to_all | solution.py:145
  21.6 12.0 %collective-permute-start = (f32[384,256]{1,0:T(8,128)S(1)}, f32[384,256]{1,0:T(8,128)S(1)}, u32[]{:S(2)}, u32[]{:S(2)}) collective-permute-start(f32[384,256]{1,0:T(8,128)S(1)} %constant_dynamic-slice_fusion.2), channel_id=1, source_target_pairs={{0,4},{4,0},{1,5},{5,1},{2,6},{6,2},{3,7},{7,3},{8,12},{12,8},{9,1... | collective-permute-start | bytes 1179656 | tf_op jit(solution)/shard_map/ppermute | solution.py:27
  33.7 1.3 collective-permute-done
  35.2 35.9 %all_to_all.35 = f32[96,4,256]{2,1,0:T(4,128)S(1)} all-to-all(f32[96,4,256]{2,1,0:T(4,128)S(1)} %reshape.40), channel_id=1, replica_groups=mesh['z'=12,'y'=8,'c'=2,'x'=4] {'z','y'}, dimensions={0} | all-to-all | bytes 786432 | tf_op jit(solution)/shard_map/all_to_all | solution.py:38
  72.0 7.1 %all-to-all-start.2 = ((f32[96,4,256]{2,1,0:T(4,128)}), f32[96,4,256]{2,1,0:T(4,128)S(1)}, u32[]{:S(2)}, u32[]{:S(2)}) async-start(f32[96,4,256]{2,1,0:T(4,128)} %broadcast_in_dim.8), calls=%async_computation.2 | async-start | bytes 786432 | tf_op jit(solution)/shard_map/all_to_all | solution.py:23
  79.2 20.5 %all-to-all-done.2 = f32[96,4,256]{2,1,0:T(4,128)S(1)} async-done(((f32[96,4,256]{2,1,0:T(4,128)}), f32[96,4,256]{2,1,0:T(4,128)S(1)}, u32[]{:S(2)}, u32[]{:S(2)}) %all-to-all-start.2) | async-done | bytes 393248 | tf_op jit(solution)/shard_map/all_to_all | solution.py:23
  99.8 6.3 %all_gather.15 = f32[768,256]{1,0:T(8,128)S(1)} all-gather(f32[384,256]{1,0:T(8,128)S(1)} %reshape.41), channel_id=1, replica_groups=mesh['z'=12,'y'=8,'c'=2,'x'=4] {'c'}, dimensions={0}, use_global_device_ids=true | all-gather | bytes 1179648 | tf_op jit(solution)/shard_map/all_gather | solution.py:151
  108.8 3.5 %all-to-all-start.3 = ((f32[4,180,256]{2,1,0:T(8,128)}), f32[4,180,256]{2,1,0:T(8,128)S(1)}, u32[]{:S(2)}, u32[]{:S(2)}) async-start(f32[4,180,256]{2,1,0:T(8,128)} %broadcast_in_dim.9), calls=%async_computation.3 | async-start | bytes 1507328 | tf_op jit(solution)/shard_map/all_to_all | solution.py:23
  112.3 11.7 %all-to-all-done.3 = f32[4,180,256]{2,1,0:T(8,128)S(1)} async-done(((f32[4,180,256]{2,1,0:T(8,128)}), f32[4,180,256]{2,1,0:T(8,128)S(1)}, u32[]{:S(2)}, u32[]{:S(2)}) %all-to-all-start.3) | async-done | bytes 737312 | tf_op jit(solution)/shard_map/all_to_all | solution.py:23
  124.6 2.9 %all-gather = f32[384,256]{1,0:T(8,128)S(1)} all-gather(f32[192,256]{1,0:T(8,128)S(1)} %pad_maximum_fusion), channel_id=2, replica_groups=mesh['z'=12,'y'=8,'c'=2,'x'=4] {'c'}, dimensions={0}, use_global_device_ids=true | all-gather | bytes 589824 | tf_op jit(solution)/shard_map/all_gather | solution.py:163
  128.1 3.3 %all-to-all-start.4 = ((f32[8,4,256]{2,1,0:T(4,128)}), f32[8,4,256]{2,1,0:T(4,128)S(1)}, u32[]{:S(2)}, u32[]{:S(2)}) async-start(f32[8,4,256]{2,1,0:T(4,128)} %reshape.44), calls=%async_computation.4 | async-start | bytes 65536 | tf_op jit(solution)/shard_map/all_to_all | solution.py:38
  131.5 6.8 %all-to-all-done.4 = f32[8,4,256]{2,1,0:T(4,128)S(1)} async-done(((f32[8,4,256]{2,1,0:T(4,128)}), f32[8,4,256]{2,1,0:T(4,128)S(1)}, u32[]{:S(2)}, u32[]{:S(2)}) %all-to-all-start.4) | async-done | bytes 32800 | tf_op jit(solution)/shard_map/all_to_all | solution.py:38
  140.1 3.5 %all-to-all-start.5 = ((f32[12,4,256]{2,1,0:T(4,128)}), f32[12,4,256]{2,1,0:T(4,128)S(1)}, u32[]{:S(2)}, u32[]{:S(2)}) async-start(f32[12,4,256]{2,1,0:T(4,128)} %broadcast_in_dim.10), calls=%async_computation.5 | async-start | bytes 98304 | tf_op jit(solution)/shard_map/all_to_all | solution.py:23
  143.7 1.4 convolution_convert_fusion
  145.1 2.2 %collective-permute-start.1 = (bf16[32,2304]{1,0:T(8,128)(2,1)S(1)}, bf16[32,2304]{1,0:T(8,128)(2,1)S(1)}, u32[]{:S(2)}, u32[]{:S(2)}) collective-permute-start(bf16[32,2304]{1,0:T(8,128)(2,1)S(1)} %convolution_convert_fusion), channel_id=1, source_target_pairs={{0,1},{4,5},{8,9},{12,13},{16,17},{20,21},{24,25},{28,29},{32,33},... | collective-permute-start | bytes 442376 | tf_op jit(solution)/shard_map/ppermute | solution.py:183
  147.3 1.3 collective-permute-start.2
  148.6 1.5 collective-permute-start.3
  150.1 7.7 %shard_map.59 = f32[256,256]{1,0:T(8,128)S(1)} custom-call(f32[256,256]{1,0:T(8,128)S(1)} %bitcast.26, f32[32,256]{1,0:T(8,128)S(1)} %bitcast.28), custom_call_target="tpu_custom_call" | custom-call | flops 100000000 | bytes 30000000 | tf_op jit(solution)/shard_map/pallas_call | solution.py:98
  158.5 4.5 %all-to-all-start.6 = ((f32[32,4,256]{2,1,0:T(4,128)}), f32[32,4,256]{2,1,0:T(4,128)S(1)}, u32[]{:S(2)}, u32[]{:S(2)}) async-start(f32[32,4,256]{2,1,0:T(4,128)} %broadcast_in_dim.11), calls=%async_computation.6 | async-start | bytes 262144 | tf_op jit(solution)/shard_map/all_to_all | solution.py:23
  163.0 2.7 %fusion.4 = f32[32,768]{1,0:T(8,128)S(1)} fusion(bf16[2304,768]{1,0:T(8,128)(2,1)} %all-gather.3.cloned.1.call-done, bf16[32,2304]{1,0:T(8,128)(2,1)S(1)} %collective-permute-done.3, bf16[32,2304]{1,0:T(8,128)(2,1)S(1)} %collective-permute-done.2, bf16[32,2304]{1,0:T(8,128)(2,1)S(1)} %convolution_convert_fusion, bf16[32,2304]{1,0:T(8,128)(2,1)S(1)} %collective-permute-done.1), kind=kOutput, calls=%fused_computation.12 | convolution fusion | flops 113467392 | bytes 4227072 | tf_op jit(solution)/shard_map/dot_general | solution.py:184
  165.7 9.4 %collective-permute-start.4 = (f32[16,768]{1,0:T(8,128)S(1)}, f32[16,768]{1,0:T(8,128)S(1)}, u32[]{:S(2)}, u32[]{:S(2)}) collective-permute-start(f32[16,768]{1,0:T(8,128)S(1)} %constant_dynamic-slice_fusion), channel_id=1, source_target_pairs={{0,4},{4,0},{1,5},{5,1},{2,6},{6,2},{3,7},{7,3},{8,12},{12,8},{9,1... | collective-permute-start | bytes 147464 | tf_op jit(solution)/shard_map/ppermute | solution.py:27
  177.3 5.2 %all_gather.19 = f32[256,256]{1,0:T(8,128)S(1)} all-gather(f32[128,256]{1,0:T(8,128)S(1)} %add.123), channel_id=1, replica_groups=mesh['z'=12,'y'=8,'c'=2,'x'=4] {'c'}, dimensions={0}, use_global_device_ids=true | all-gather | bytes 393216 | tf_op jit(solution)/shard_map/all_gather | solution.py:189
  (63 shorter events, 14.3 us)
Async XLA Ops:
  7.2 136.5 %all-gather.3.cloned.1.call-start = ((), (), s32[]{:S(2)}) async-start(), calls=%async_computation.7 | async-start | bytes 3575808 | tf_op jit(solution)/shard_map/all_gather | solution.py:143
  7.2 1.1 copy-start
  8.3 0.8 copy-start.1
  9.1 0.8 copy-start.3
  10.9 9.9 %all-to-all-start = ((f32[4,36,256]{2,1,0:T(8,128)}), f32[4,36,256]{2,1,0:T(8,128)S(1)}, u32[]{:S(2)}, u32[]{:S(2)}) async-start(f32[4,36,256]{2,1,0:T(8,128)} %get-tuple-element.5), calls=%async_computation | async-start | bytes 327680 | tf_op jit(solution)/shard_map/all_to_all | solution.py:145
  21.6 84.5 %copy-start.4 = (bf16[768,20]{0,1:T(8,128)(2,1)S(1)}, bf16[768,20]{0,1:T(8,128)(2,1)}, u32[]{:S(2)}) copy-start(bf16[768,20]{0,1:T(8,128)(2,1)} %param.4) | copy-start | bytes 92164
  21.6 13.4 %collective-permute-start = (f32[384,256]{1,0:T(8,128)S(1)}, f32[384,256]{1,0:T(8,128)S(1)}, u32[]{:S(2)}, u32[]{:S(2)}) collective-permute-start(f32[384,256]{1,0:T(8,128)S(1)} %constant_dynamic-slice_fusion.2), channel_id=1, source_target_pairs={{0,4},{4,0},{1,5},{5,1},{2,6},{6,2},{3,7},{7,3},{8,12},{12,8},{9,1... | collective-permute-start | bytes 1179656 | tf_op jit(solution)/shard_map/ppermute | solution.py:27
  33.7 72.8 %copy-start.2 = (f32[16,768]{1,0:T(8,128)S(1)}, f32[16,768]{1,0:T(8,128)}, u32[]{:S(2)}) copy-start(f32[16,768]{1,0:T(8,128)} %factor_ref.1) | copy-start | bytes 147460
  72.0 27.6 %all-to-all-start.2 = ((f32[96,4,256]{2,1,0:T(4,128)}), f32[96,4,256]{2,1,0:T(4,128)S(1)}, u32[]{:S(2)}, u32[]{:S(2)}) async-start(f32[96,4,256]{2,1,0:T(4,128)} %broadcast_in_dim.8), calls=%async_computation.2 | async-start | bytes 786432 | tf_op jit(solution)/shard_map/all_to_all | solution.py:23
  108.8 15.2 %all-to-all-start.3 = ((f32[4,180,256]{2,1,0:T(8,128)}), f32[4,180,256]{2,1,0:T(8,128)S(1)}, u32[]{:S(2)}, u32[]{:S(2)}) async-start(f32[4,180,256]{2,1,0:T(8,128)} %broadcast_in_dim.9), calls=%async_computation.3 | async-start | bytes 1507328 | tf_op jit(solution)/shard_map/all_to_all | solution.py:23
  128.1 10.1 %all-to-all-start.4 = ((f32[8,4,256]{2,1,0:T(4,128)}), f32[8,4,256]{2,1,0:T(4,128)S(1)}, u32[]{:S(2)}, u32[]{:S(2)}) async-start(f32[8,4,256]{2,1,0:T(4,128)} %reshape.44), calls=%async_computation.4 | async-start | bytes 65536 | tf_op jit(solution)/shard_map/all_to_all | solution.py:38
  140.1 17.7 %all-to-all-start.5 = ((f32[12,4,256]{2,1,0:T(4,128)}), f32[12,4,256]{2,1,0:T(4,128)S(1)}, u32[]{:S(2)}, u32[]{:S(2)}) async-start(f32[12,4,256]{2,1,0:T(4,128)} %broadcast_in_dim.10), calls=%async_computation.5 | async-start | bytes 98304 | tf_op jit(solution)/shard_map/all_to_all | solution.py:23
  145.1 17.9 %collective-permute-start.1 = (bf16[32,2304]{1,0:T(8,128)(2,1)S(1)}, bf16[32,2304]{1,0:T(8,128)(2,1)S(1)}, u32[]{:S(2)}, u32[]{:S(2)}) collective-permute-start(bf16[32,2304]{1,0:T(8,128)(2,1)S(1)} %convolution_convert_fusion), channel_id=1, source_target_pairs={{0,1},{4,5},{8,9},{12,13},{16,17},{20,21},{24,25},{28,29},{32,33},... | collective-permute-start | bytes 442376 | tf_op jit(solution)/shard_map/ppermute | solution.py:183
  147.3 15.7 %collective-permute-start.2 = (bf16[32,2304]{1,0:T(8,128)(2,1)S(1)}, bf16[32,2304]{1,0:T(8,128)(2,1)S(1)}, u32[]{:S(2)}, u32[]{:S(2)}) collective-permute-start(bf16[32,2304]{1,0:T(8,128)(2,1)S(1)} %convolution_convert_fusion), channel_id=1, source_target_pairs={{0,2},{4,6},{8,10},{12,14},{16,18},{20,22},{24,26},{28,30},{32,34}... | collective-permute-start | bytes 442376 | tf_op jit(solution)/shard_map/ppermute | solution.py:183
  148.6 14.4 %collective-permute-start.3 = (bf16[32,2304]{1,0:T(8,128)(2,1)S(1)}, bf16[32,2304]{1,0:T(8,128)(2,1)S(1)}, u32[]{:S(2)}, u32[]{:S(2)}) collective-permute-start(bf16[32,2304]{1,0:T(8,128)(2,1)S(1)} %convolution_convert_fusion), channel_id=1, source_target_pairs={{0,3},{4,7},{8,11},{12,15},{16,19},{20,23},{24,27},{28,31},{32,35}... | collective-permute-start | bytes 442376 | tf_op jit(solution)/shard_map/ppermute | solution.py:183
  158.5 18.7 %all-to-all-start.6 = ((f32[32,4,256]{2,1,0:T(4,128)}), f32[32,4,256]{2,1,0:T(4,128)S(1)}, u32[]{:S(2)}, u32[]{:S(2)}) async-start(f32[32,4,256]{2,1,0:T(4,128)} %broadcast_in_dim.11), calls=%async_computation.6 | async-start | bytes 262144 | tf_op jit(solution)/shard_map/all_to_all | solution.py:23
  165.7 10.4 %collective-permute-start.4 = (f32[16,768]{1,0:T(8,128)S(1)}, f32[16,768]{1,0:T(8,128)S(1)}, u32[]{:S(2)}, u32[]{:S(2)}) collective-permute-start(f32[16,768]{1,0:T(8,128)S(1)} %constant_dynamic-slice_fusion), channel_id=1, source_target_pairs={{0,4},{4,0},{1,5},{5,1},{2,6},{6,2},{3,7},{7,3},{8,12},{12,8},{9,1... | collective-permute-start | bytes 147464 | tf_op jit(solution)/shard_map/ppermute | solution.py:27
  176.1 7.9 %copy-start.5 = (f32[16,768]{1,0:T(8,128)}, f32[16,768]{1,0:T(8,128)S(1)}, u32[]{:S(2)}) copy-start(f32[16,768]{1,0:T(8,128)S(1)} %add_add_fusion) | copy-start | bytes 147460
Sparse Core Ops, SparseCore 0:
  11.7 128.2 all-gather.2

commit v5 on v4

--- a/solution.py
+++ b/solution.py
@@ -38,8 +38,12 @@
     return jnp.sum(lax.all_to_all(v.reshape(n, v.shape[0] // n, v.shape[1]), axis, 0, 0), axis=0)
 
 
+def nothing(w):
+    return (w[0, 0] > 0).astype(jnp.int32) >> 1
+
+
 def after(v, w):
-    return v + (0.0 * w[:1, :1]).astype(v.dtype)
+    return v + nothing(w).astype(v.dtype)
 
 
 def join(v):
@@ -87,14 +91,19 @@
     x_ref[below, :(tile + 1) * LANES] -= update[:, n_a * LANES:]
 
 
-def inverse_kernel(g_ref, after_ref, inv_ref, a_ref, x_ref):
-    a_ref[...] = g_ref[...]
+def inverse_kernel(both_ref, after_ref, inv_ref, a_ref, x_ref):
+    for core in range(NC):
+        a_ref[64 * core:64 * core + 64, :] = both_ref[core, :64, :] * (1.0 / B)
+        for k in range(2):
+            at = LANES + 64 * core + 32 * k
+            a_ref[at:at + 32, :LANES] = jnp.zeros((32, LANES), F32)
+            a_ref[at:at + 32, LANES:] = both_ref[core, 64:96, k * LANES:(k + 1) * LANES] * (1.0 / B)
     x_ref[...] = (lax.broadcasted_iota(jnp.int32, (R, R), 0) == lax.broadcasted_iota(jnp.int32, (R, R), 1)).astype(F32)
     for k in range(R // PANEL):
         panel_step(k, a_ref, x_ref, inv_ref)
 
 
-def inverse_factor(gram_matrix, after):
+def inverse_factor(both, after):
     return pl.pallas_call(
         inverse_kernel,
         out_shape=jax.ShapeDtypeStruct((R, R), F32),
@@ -103,16 +112,24 @@
         scratch_shapes=[pltpu.VMEM((R, R), F32), pltpu.VMEM((R, R), F32)],
         compiler_params=pltpu.CompilerParams(vmem_limit_bytes=24 << 20),
         cost_estimate=pl.CostEstimate(flops=10**8, bytes_accessed=30 * 10**6, transcendentals=0),
-    )(gram_matrix, after)
-
-
-def front_kernel(grad_ref, factor_ref, sketch_ref, small_ref, strip_ref):
+    )(both, after)
+
+
+def front_kernel(grad_hbm, factor_hbm, sketch_hbm, small_ref, strip_ref, grad_ref, factor_ref, sketch_ref, sems):
+    pairs = ((grad_hbm, grad_ref), (factor_hbm, factor_ref), (sketch_hbm, sketch_ref))
+    copies = [pltpu.make_async_copy(src, dst, sems.at[i]) for i, (src, dst) in enumerate(pairs)]
+    for copy in copies:
+        copy.start()
     wide, rows = grad_ref.shape[0], factor_ref.shape[0]
-    sketch = sketch_ref[...].astype(F32).astype(BF16)
+    copies[0].wait()
     grad = grad_ref[...]
     strip_ref[...] = jnp.concatenate([grad.astype(F32), jnp.zeros((strip_ref.shape[0] - wide, grad.shape[1]), F32)], axis=0).astype(BF16)
+    copies[1].wait()
+    pieces = jnp.concatenate(split3(factor_ref[...]), axis=0)
+    copies[2].wait()
+    sketch = sketch_ref[...].astype(F32).astype(BF16)
     inner = jnp.dot(grad, sketch, preferred_element_type=F32)
-    parts = jnp.dot(jnp.concatenate(split3(factor_ref[...]), axis=0), sketch, preferred_element_type=F32)
+    parts = jnp.dot(pieces, sketch, preferred_element_type=F32)
     decayed = decay_rate * (parts[:rows] + (parts[rows:2 * rows] + parts[2 * rows:]))
     for k in range(NX):
         small_ref[k, :wide, :] = inner
@@ -125,11 +142,45 @@
     return pl.pallas_call(
         front_kernel,
         out_shape=(jax.ShapeDtypeStruct((NX, wide + rows, cols), F32), jax.ShapeDtypeStruct((24, grad.shape[1]), BF16)),
-        in_specs=[whole] * 3,
+        in_specs=[pl.BlockSpec(memory_space=pl.ANY)] * 3,
         out_specs=(whole, whole),
+        scratch_shapes=[pltpu.VMEM(v.shape, v.dtype) for v in (grad, factor, sketch_ids)] + [pltpu.SemaphoreType.DMA((3,))],
+        compiler_params=pltpu.CompilerParams(vmem_limit_bytes=56 << 20),
+        cost_estimate=pl.CostEstimate(flops=10**8, bytes_accessed=4 * 10**6, transcendentals=0),
+    )(grad, factor, sketch_ids)
+
+
+def middle_kernel(at_ref, ranged_ref, grad_ref, factor_ref, part_ref):
+    offset, mine, core = pl.multiple_of(at_ref[0], 16), at_ref[1], at_ref[2]
+    wide, rows = grad_ref.shape[0], factor_ref.shape[0]
+    ranged = ranged_ref[...]
+    halves = [ranged[:, :LANES], ranged[:, LANES:]]
+    moved = [pltpu.roll(v, 64, 1) for v in halves]
+    low = lax.broadcasted_iota(jnp.int32, halves[0].shape, 1) < 64
+    pick = jnp.where(core == 0, jnp.where(low, halves[0], moved[1]), jnp.where(low, moved[0], halves[1]))
+    gram = dot(pick, ranged, 0, 0)
+    here = jnp.where(mine == 1, ranged_ref[pl.ds(offset, rows), :], 0.0)
+    weighted = sum(jnp.dot(grad_ref[...], v, preferred_element_type=F32) for v in split3(ranged))
+    applied = decay_rate * dot(factor_ref[...], ranged, 1, 0)
+    for k in range(NX):
+        part_ref[k, :64, :] = gram[:64]
+        part_ref[k, 64:96, :LANES] = gram[64:96, LANES:]
+        part_ref[k, 64:96, LANES:] = gram[96:, LANES:]
+        part_ref[k, 96:96 + rows, :] = here
+        part_ref[k, 96 + rows:96 + rows + wide, :] = weighted
+        part_ref[k, 96 + rows + wide:, :] = applied
+
+
+def middle(at, ranged, grad, factor):
+    whole = pl.BlockSpec(memory_space=pltpu.VMEM)
+    return pl.pallas_call(
+        middle_kernel,
+        out_shape=jax.ShapeDtypeStruct((NX, 96 + 2 * factor.shape[0] + grad.shape[0], R), F32),
+        in_specs=[pl.BlockSpec(memory_space=pltpu.SMEM)] + [whole] * 3,
+        out_specs=whole,
         compiler_params=pltpu.CompilerParams(vmem_limit_bytes=24 << 20),
         cost_estimate=pl.CostEstimate(flops=10**8, bytes_accessed=4 * 10**6, transcendentals=0),
-    )(grad, factor, sketch_ids)
+    )(at, ranged, grad, factor)
 
 
 def shards(factor, gradient, sketch_ids):
@@ -150,26 +201,23 @@
     piece = join(spread(piece, ("z", "y"), NZ * NY))
     ranged = lax.all_gather(piece, "c", axis=0, tiled=True)
 
-    here = mine * lax.dynamic_slice_in_dim(ranged, offset, rows, 0)
-    gram = dot(lax.dynamic_slice_in_dim(ranged, c * 128, 128, 1), ranged, 0, 0)
     wide = gradient.shape[1]
-    part = jnp.concatenate([gram, here, dot(grad32, ranged, 0, 0), decay_rate * dot(factor, ranged, 1, 0)], axis=0)
-    part = jnp.sum(spread(part, "x", NX), axis=0)
-    own_rows = part[128:128 + rows]
-    left = part[128:128 + rows + wide]
-    right = jnp.concatenate([part[128 + rows + wide:], part[128 + rows:128 + rows + wide]], axis=0)
+    at = jnp.stack([offset, (x == owner).astype(jnp.int32), c])
+    part = jnp.sum(lax.all_to_all(middle(at, ranged, gradient.T, factor), "x", 0, 0), axis=0)
+    own_rows = part[96:96 + rows]
+    left = part[96:96 + rows + wide]
+    right = jnp.concatenate([part[96 + rows + wide:], part[96 + rows:96 + rows + wide]], axis=0)
     core = dot(left, right, 0, 0).reshape(NC, NX, 32, 256)
     core = lax.dynamic_index_in_dim(core, x, 1, keepdims=False).reshape(64, 256)
-    both = lax.all_gather(jnp.concatenate([part[:128], core], axis=0), "c", axis=0, tiled=False)
-    gram_matrix = both[:, :128].reshape(R, R) / B
-    core = lax.dynamic_slice_in_dim(both[0, 128:] + both[1, 128:], 32 * c, 32, 0)
-    inverse = inverse_factor(gram_matrix, core)
-    core = scatter(core, "y", NY)
-    late = (core[0, 0] > 0).astype(jnp.int32) >> 1
+    both = lax.all_gather(jnp.concatenate([part[:96], core], axis=0), "c", axis=0, tiled=False)
+    core = lax.dynamic_slice_in_dim(both[0, 96:] + both[1, 96:], 32 * c, 32, 0)
+    inverse = inverse_factor(both, core)
+    core = core_y = scatter(core, "y", NY)
+    range_basis = dot(own_rows, inverse, 1, 1)
     core = jnp.sum(spread(core, "z", NZ), axis=0)
 
     pair = 2 * rows
-    start = offset - rows * c + late
+    start = offset - rows * c + nothing(core_y)
     block = lax.dynamic_slice(plane, (0, start // LANES * LANES), (plane.shape[0], LANES))
     place = (lax.broadcasted_iota(jnp.int32, (LANES, pair), 0) == start % LANES + lax.broadcasted_iota(jnp.int32, (LANES, pair), 1))
     place = (place & (x == owner)).astype(BF16)
@@ -185,10 +233,9 @@
     factor_new = decay_rate * factor + scatter_core(outer_sum, c)
 
     core = join(spread(core, ("x", "y"), NX * NY))
-    core = after(core, factor_new)
+    core = after(core, outer_sum)
     core = lax.all_gather(core, "c", axis=0, tiled=True)
 
-    range_basis = dot(own_rows, inverse, 1, 1)
     projected_core = dot(dot(inverse, core, 1, 0), inverse, 1, 1) / B
     return (factor_new, range_basis, projected_core)
 

time: 192 us -> 188 us (0.979)
  Pallas kernels: 8.57 us -> 12.3 us
  local copies, waits for them, and re-layouts: 7.81 us -> 4.16 us
  starting transfers between devices: 53.3 us -> 49.9 us
    all_to_all x0 -> x1, waiting for transfers between devices: none -> 10.2 us  [shards(): lax.all_to_all(middle(at, ranged, gradient.T, factor), 'x', 0, 0)]
    ppermute x2, starting transfers between devices: 21.5 us -> 14.3 us  [swap_core(): return lax.ppermute(v, 'c', [(0, 1), (1, 0)])]
    all_to_all x1, waiting for transfers between devices: 6.79 us -> 0.01 us  [scatter(): lax.all_to_all(v.reshape(n, v.shape[0] // n, v.shape[1]), axis, 0, 0)]
    all_to_all x4 -> x3, waiting for transfers between devices: 32.2 us -> 27.3 us  [spread(): return lax.all_to_all(jnp.broadcast_to(v[None], (n,) + v.shape), axis, 0, 0)]
    all_to_all x0 -> x1, starting transfers between devices: none -> 3.48 us  [shards(): lax.all_to_all(middle(at, ranged, gradient.T, factor), 'x', 0, 0)]
    unnamed x12 -> x4, local copies, waits for them, and re-layouts: 2.73 us -> 0.01 us
    pallas_call x0 -> x1, Pallas kernels: none -> 2.53 us  [middle(): pl.pallas_call(middle_kernel, out_shape=jax.ShapeDtypeStruct((NX, 96 + 2...]
    dot_general x8 -> x5, matrix products: 5.38 us -> 3.67 us  [dot(): lax.dot_general(a, b, (((ca,), (cb,)), ((), ())), precision=HI, preferred...]
  transfers between devices with their start and end apart: 12 -> 12, of which waited for: 5 -> 6; matrix products, arithmetic and copies ran while one was open for 7% -> 7% of each run, Pallas kernels for 4% -> 5%
where the time goes in v5:
time: 188 us; the launch traced here: 187 us
  blocking collectives  52.3 us (28%)
  starting transfers between devices  49.9 us (27%)
  waiting for transfers between devices  43.1 us (23%)
  between operations  15.7 us (8%)
  Pallas kernels  12.3 us (7%)
  matrix products  7.76 us (4%)
  local copies, waits for them, and re-layouts  4.16 us (2%)
    all_to_all x1, blocking collectives, scatter(): lax.all_to_all(v.reshape(n, v.shape[0] // n, v.shape[1]), axis, 0, 0)  36.2 us
    all_to_all x3, waiting for transfers between devices, spread(): return lax.all_to_all(jnp.broadcast_to(v[None], (n,) + v.shape), axis, 0, 0)  27.3 us
    all_to_all x3, starting transfers between devices, spread(): return lax.all_to_all(jnp.broadcast_to(v[None], (n,) + v.shape), axis, 0, 0)  18.2 us
    ppermute x2, starting transfers between devices, swap_core(): return lax.ppermute(v, 'c', [(0, 1), (1, 0)])  14.3 us
    all_to_all x1, waiting for transfers between devices, shards(): lax.all_to_all(middle(at, ranged, gradient.T, factor), 'x', 0, 0)  10.2 us
    pallas_call x1, Pallas kernels, inverse_factor(): pl.pallas_call(inverse_kernel, out_shape=jax.ShapeDtypeStruct((R, R), F32...  7.65 us
    all_gather x1, blocking collectives, shards(): core = lax.all_gather(core, 'c', axis=0, tiled=True)  6.91 us
    all_gather x1, blocking collectives, shards(): ranged = lax.all_gather(piece, 'c', axis=0, tiled=True)  6.25 us
  transfers between devices with their start and end apart: 12, of which 6 were waited for; matrix products, arithmetic and copies ran while one was open for 7% of the time, Pallas kernels for 5%

profile of v5, /device:TPU:1, one launch (start us, length us, event | category | flops | bytes accessed | tf_op | source)
XLA Modules:
  0.0 187.0 jit_solution(6592294917763348712)
XLA Ops:
  7.2 2.1 %shard_map.58 = (f32[4,36,256]{2,1,0:T(8,128)}, bf16[24,768]{1,0:T(8,128)(2,1)}) custom-call(bf16[20,768]{1,0:T(8,128)(2,1)} %bitcast.21, f32[16,768]{1,0:T(8,128)} %factor_ref.1, s32[768,256]{1,0:T(8,128)} %sketch_hbm.1), custom_call_target="tpu_custom_call" | custom-call | flops 100000000 | bytes 4000000 | tf_op jit(solution)/shard_map/pallas_call | solution.py:142
  9.4 4.9 %all-to-all-start = ((f32[4,36,256]{2,1,0:T(8,128)}), f32[4,36,256]{2,1,0:T(8,128)S(1)}, u32[]{:S(2)}, u32[]{:S(2)}) async-start(f32[4,36,256]{2,1,0:T(8,128)} %get-tuple-element.5), calls=%async_computation | async-start | bytes 327680 | tf_op jit(solution)/shard_map/all_to_all | solution.py:196
  15.1 4.1 %all-to-all-done = f32[4,36,256]{2,1,0:T(8,128)S(1)} async-done(((f32[4,36,256]{2,1,0:T(8,128)}), f32[4,36,256]{2,1,0:T(8,128)S(1)}, u32[]{:S(2)}, u32[]{:S(2)}) %all-to-all-start) | async-done | bytes 147488 | tf_op jit(solution)/shard_map/all_to_all | solution.py:196
  20.1 12.0 %collective-permute-start = (f32[384,256]{1,0:T(8,128)S(1)}, f32[384,256]{1,0:T(8,128)S(1)}, u32[]{:S(2)}, u32[]{:S(2)}) collective-permute-start(f32[384,256]{1,0:T(8,128)S(1)} %constant_dynamic-slice_fusion.2), channel_id=1, source_target_pairs={{0,4},{4,0},{1,5},{5,1},{2,6},{6,2},{3,7},{7,3},{8,12},{12,8},{9,1... | collective-permute-start | bytes 1179656 | tf_op jit(solution)/shard_map/ppermute | solution.py:27
  33.7 36.2 %all_to_all.35 = f32[96,4,256]{2,1,0:T(4,128)S(1)} all-to-all(f32[96,4,256]{2,1,0:T(4,128)S(1)} %reshape.42), channel_id=1, replica_groups=mesh['z'=12,'y'=8,'c'=2,'x'=4] {'z','y'}, dimensions={0} | all-to-all | bytes 786432 | tf_op jit(solution)/shard_map/all_to_all | solution.py:38
  70.9 7.0 %all-to-all-start.2 = ((f32[96,4,256]{2,1,0:T(4,128)}), f32[96,4,256]{2,1,0:T(4,128)S(1)}, u32[]{:S(2)}, u32[]{:S(2)}) async-start(f32[96,4,256]{2,1,0:T(4,128)} %broadcast_in_dim.6), calls=%async_computation.2 | async-start | bytes 786432 | tf_op jit(solution)/shard_map/all_to_all | solution.py:23
  78.0 20.5 %all-to-all-done.2 = f32[96,4,256]{2,1,0:T(4,128)S(1)} async-done(((f32[96,4,256]{2,1,0:T(4,128)}), f32[96,4,256]{2,1,0:T(4,128)S(1)}, u32[]{:S(2)}, u32[]{:S(2)}) %all-to-all-start.2) | async-done | bytes 393248 | tf_op jit(solution)/shard_map/all_to_all | solution.py:23
  98.6 6.3 %all_gather.15.ranged_ref = f32[768,256]{1,0:T(8,128)S(1)} all-gather(f32[384,256]{1,0:T(8,128)S(1)} %reshape.43), channel_id=1, replica_groups=mesh['z'=12,'y'=8,'c'=2,'x'=4] {'c'}, dimensions={0}, use_global_device_ids=true | all-gather | bytes 1179648 | tf_op jit(solution)/shard_map/all_gather | solution.py:202
  104.8 2.5 %shard_map.59 = f32[4,148,256]{2,1,0:T(8,128)} custom-call(s32[3]{0:T(128)S(1)} %pad_add_fusion.at_ref, f32[768,256]{1,0:T(8,128)S(1)} %all_gather.15.ranged_ref, bf16[20,768]{1,0:T(8,128)(2,1)S(1)} %bitcast.22, f32[16,768]{1,0:T(8,128)S(1)} %copy-done), custom_call_target="tpu_custom_call" | custom-call | flops 100000000 | bytes 4000000 | tf_op jit(solution)/shard_map/pallas_call | solution.py:176
  107.4 3.5 %all-to-all-start.3 = ((f32[4,148,256]{2,1,0:T(8,128)}), f32[4,148,256]{2,1,0:T(8,128)S(1)}, u32[]{:S(2)}, u32[]{:S(2)}) async-start(f32[4,148,256]{2,1,0:T(8,128)} %shard_map.59), calls=%async_computation.3 | async-start | bytes 1245184 | tf_op jit(solution)/shard_map/all_to_all | solution.py:206
  110.9 10.2 %all-to-all-done.3 = f32[4,148,256]{2,1,0:T(8,128)S(1)} async-done(((f32[4,148,256]{2,1,0:T(8,128)}), f32[4,148,256]{2,1,0:T(8,128)S(1)}, u32[]{:S(2)}, u32[]{:S(2)}) %all-to-all-start.3) | async-done | bytes 606240 | tf_op jit(solution)/shard_map/all_to_all | solution.py:206
  121.7 2.9 %all-gather = f32[320,256]{1,0:T(8,128)S(1)} all-gather(f32[160,256]{1,0:T(8,128)S(1)} %pad_maximum_fusion), channel_id=2, replica_groups=mesh['z'=12,'y'=8,'c'=2,'x'=4] {'c'}, dimensions={0}, use_global_device_ids=true | all-gather | bytes 491520 | tf_op jit(solution)/shard_map/all_gather | solution.py:212
  125.2 3.3 %all-to-all-start.4 = ((f32[8,4,256]{2,1,0:T(4,128)}), f32[8,4,256]{2,1,0:T(4,128)S(1)}, u32[]{:S(2)}, u32[]{:S(2)}) async-start(f32[8,4,256]{2,1,0:T(4,128)} %reshape.46), calls=%async_computation.4 | async-start | bytes 65536 | tf_op jit(solution)/shard_map/all_to_all | solution.py:38
  128.6 7.7 %shard_map.60 = f32[256,256]{1,0:T(8,128)S(1)} custom-call(f32[2,160,256]{2,1,0:T(8,128)S(1)} %bitcast.20, f32[32,256]{1,0:T(8,128)S(1)} %bitcast.23), custom_call_target="tpu_custom_call" | custom-call | flops 100000000 | bytes 30000000 | tf_op jit(solution)/shard_map/pallas_call | solution.py:107
  138.1 3.7 %all-to-all-start.5 = ((f32[12,4,256]{2,1,0:T(4,128)}), f32[12,4,256]{2,1,0:T(4,128)S(1)}, u32[]{:S(2)}, u32[]{:S(2)}) async-start(f32[12,4,256]{2,1,0:T(4,128)} %broadcast_in_dim.7), calls=%async_computation.5 | async-start | bytes 98304 | tf_op jit(solution)/shard_map/all_to_all | solution.py:23
  141.8 1.4 convolution_convert_fusion
  143.2 2.3 %collective-permute-start.1 = (bf16[32,2304]{1,0:T(8,128)(2,1)S(1)}, bf16[32,2304]{1,0:T(8,128)(2,1)S(1)}, u32[]{:S(2)}, u32[]{:S(2)}) collective-permute-start(bf16[32,2304]{1,0:T(8,128)(2,1)S(1)} %convolution_convert_fusion), channel_id=1, source_target_pairs={{0,1},{4,5},{8,9},{12,13},{16,17},{20,21},{24,25},{28,29},{32,33},... | collective-permute-start | bytes 442376 | tf_op jit(solution)/shard_map/ppermute | solution.py:231
  145.6 2.0 %collective-permute-start.2 = (bf16[32,2304]{1,0:T(8,128)(2,1)S(1)}, bf16[32,2304]{1,0:T(8,128)(2,1)S(1)}, u32[]{:S(2)}, u32[]{:S(2)}) collective-permute-start(bf16[32,2304]{1,0:T(8,128)(2,1)S(1)} %convolution_convert_fusion), channel_id=1, source_target_pairs={{0,2},{4,6},{8,10},{12,14},{16,18},{20,22},{24,26},{28,30},{32,34}... | collective-permute-start | bytes 442376 | tf_op jit(solution)/shard_map/ppermute | solution.py:231
  149.8 1.6 all-to-all-done.5
  152.1 7.6 %all-to-all-start.6 = ((f32[32,4,256]{2,1,0:T(4,128)}), f32[32,4,256]{2,1,0:T(4,128)S(1)}, u32[]{:S(2)}, u32[]{:S(2)}) async-start(f32[32,4,256]{2,1,0:T(4,128)} %broadcast_in_dim.8), calls=%async_computation.6 | async-start | bytes 262144 | tf_op jit(solution)/shard_map/all_to_all | solution.py:23
  159.7 2.7 %fusion.1 = f32[32,768]{1,0:T(8,128)S(1)} fusion(bf16[2304,768]{1,0:T(8,128)(2,1)} %all-gather.3.cloned.1.call-done, bf16[32,2304]{1,0:T(8,128)(2,1)S(1)} %collective-permute-done.3, bf16[32,2304]{1,0:T(8,128)(2,1)S(1)} %collective-permute-done.2, bf16[32,2304]{1,0:T(8,128)(2,1)S(1)} %convolution_convert_fusion, bf16[32,2304]{1,0:T(8,128)(2,1)S(1)} %collective-permute-done.1), kind=kOutput, calls=%fused_computation.5 | convolution fusion | flops 113467392 | bytes 4227072 | tf_op jit(solution)/shard_map/dot_general | solution.py:232
  163.5 5.3 %all-to-all-done.6 = f32[32,4,256]{2,1,0:T(4,128)S(1)} async-done(((f32[32,4,256]{2,1,0:T(4,128)}), f32[32,4,256]{2,1,0:T(4,128)S(1)}, u32[]{:S(2)}, u32[]{:S(2)}) %all-to-all-start.6) | async-done | bytes 131104 | tf_op jit(solution)/shard_map/all_to_all | solution.py:23
  168.8 6.9 %all_gather.19 = f32[256,256]{1,0:T(8,128)S(1)} all-gather(f32[128,256]{1,0:T(8,128)S(1)} %add.110), channel_id=1, replica_groups=mesh['z'=12,'y'=8,'c'=2,'x'=4] {'c'}, dimensions={0}, use_global_device_ids=true | all-gather | bytes 393216 | tf_op jit(solution)/shard_map/all_gather | solution.py:237
  176.2 2.3 %collective-permute-start.4 = (f32[16,768]{1,0:T(8,128)S(1)}, f32[16,768]{1,0:T(8,128)S(1)}, u32[]{:S(2)}, u32[]{:S(2)}) collective-permute-start(f32[16,768]{1,0:T(8,128)S(1)} %constant_dynamic-slice_fusion), channel_id=1, source_target_pairs={{0,4},{4,0},{1,5},{5,1},{2,6},{6,2},{3,7},{7,3},{8,12},{12,8},{9,1... | collective-permute-start | bytes 147464 | tf_op jit(solution)/shard_map/ppermute | solution.py:27
  (50 shorter events, 12.4 us)
Async XLA Ops:
  7.2 134.7 %all-gather.3.cloned.1.call-start = ((), (), s32[]{:S(2)}) async-start(), calls=%async_computation.7 | async-start | bytes 3575808 | tf_op jit(solution)/shard_map/all_gather | solution.py:194
  9.4 9.9 %all-to-all-start = ((f32[4,36,256]{2,1,0:T(8,128)}), f32[4,36,256]{2,1,0:T(8,128)S(1)}, u32[]{:S(2)}, u32[]{:S(2)}) async-start(f32[4,36,256]{2,1,0:T(8,128)} %get-tuple-element.5), calls=%async_computation | async-start | bytes 327680 | tf_op jit(solution)/shard_map/all_to_all | solution.py:196
  20.1 84.8 %copy-start = (f32[16,768]{1,0:T(8,128)S(1)}, f32[16,768]{1,0:T(8,128)}, u32[]{:S(2)}) copy-start(f32[16,768]{1,0:T(8,128)} %factor_ref.1) | copy-start | bytes 147460
  20.1 84.7 %copy-start.1 = (bf16[768,20]{0,1:T(8,128)(2,1)S(1)}, bf16[768,20]{0,1:T(8,128)(2,1)}, u32[]{:S(2)}) copy-start(bf16[768,20]{0,1:T(8,128)(2,1)} %param.4) | copy-start | bytes 92164
  20.1 13.4 %collective-permute-start = (f32[384,256]{1,0:T(8,128)S(1)}, f32[384,256]{1,0:T(8,128)S(1)}, u32[]{:S(2)}, u32[]{:S(2)}) collective-permute-start(f32[384,256]{1,0:T(8,128)S(1)} %constant_dynamic-slice_fusion.2), channel_id=1, source_target_pairs={{0,4},{4,0},{1,5},{5,1},{2,6},{6,2},{3,7},{7,3},{8,12},{12,8},{9,1... | collective-permute-start | bytes 1179656 | tf_op jit(solution)/shard_map/ppermute | solution.py:27
  70.9 27.6 %all-to-all-start.2 = ((f32[96,4,256]{2,1,0:T(4,128)}), f32[96,4,256]{2,1,0:T(4,128)S(1)}, u32[]{:S(2)}, u32[]{:S(2)}) async-start(f32[96,4,256]{2,1,0:T(4,128)} %broadcast_in_dim.6), calls=%async_computation.2 | async-start | bytes 786432 | tf_op jit(solution)/shard_map/all_to_all | solution.py:23
  107.4 13.7 %all-to-all-start.3 = ((f32[4,148,256]{2,1,0:T(8,128)}), f32[4,148,256]{2,1,0:T(8,128)S(1)}, u32[]{:S(2)}, u32[]{:S(2)}) async-start(f32[4,148,256]{2,1,0:T(8,128)} %shard_map.59), calls=%async_computation.3 | async-start | bytes 1245184 | tf_op jit(solution)/shard_map/all_to_all | solution.py:206
  125.2 11.0 %all-to-all-start.4 = ((f32[8,4,256]{2,1,0:T(4,128)}), f32[8,4,256]{2,1,0:T(4,128)S(1)}, u32[]{:S(2)}, u32[]{:S(2)}) async-start(f32[8,4,256]{2,1,0:T(4,128)} %reshape.46), calls=%async_computation.4 | async-start | bytes 65536 | tf_op jit(solution)/shard_map/all_to_all | solution.py:38
  138.1 13.3 %all-to-all-start.5 = ((f32[12,4,256]{2,1,0:T(4,128)}), f32[12,4,256]{2,1,0:T(4,128)S(1)}, u32[]{:S(2)}, u32[]{:S(2)}) async-start(f32[12,4,256]{2,1,0:T(4,128)} %broadcast_in_dim.7), calls=%async_computation.5 | async-start | bytes 98304 | tf_op jit(solution)/shard_map/all_to_all | solution.py:23
  143.2 16.4 %collective-permute-start.1 = (bf16[32,2304]{1,0:T(8,128)(2,1)S(1)}, bf16[32,2304]{1,0:T(8,128)(2,1)S(1)}, u32[]{:S(2)}, u32[]{:S(2)}) collective-permute-start(bf16[32,2304]{1,0:T(8,128)(2,1)S(1)} %convolution_convert_fusion), channel_id=1, source_target_pairs={{0,1},{4,5},{8,9},{12,13},{16,17},{20,21},{24,25},{28,29},{32,33},... | collective-permute-start | bytes 442376 | tf_op jit(solution)/shard_map/ppermute | solution.py:231
  145.6 14.1 %collective-permute-start.2 = (bf16[32,2304]{1,0:T(8,128)(2,1)S(1)}, bf16[32,2304]{1,0:T(8,128)(2,1)S(1)}, u32[]{:S(2)}, u32[]{:S(2)}) collective-permute-start(bf16[32,2304]{1,0:T(8,128)(2,1)S(1)} %convolution_convert_fusion), channel_id=1, source_target_pairs={{0,2},{4,6},{8,10},{12,14},{16,18},{20,22},{24,26},{28,30},{32,34}... | collective-permute-start | bytes 442376 | tf_op jit(solution)/shard_map/ppermute | solution.py:231
  147.5 12.1 %collective-permute-start.3 = (bf16[32,2304]{1,0:T(8,128)(2,1)S(1)}, bf16[32,2304]{1,0:T(8,128)(2,1)S(1)}, u32[]{:S(2)}, u32[]{:S(2)}) collective-permute-start(bf16[32,2304]{1,0:T(8,128)(2,1)S(1)} %convolution_convert_fusion), channel_id=1, source_target_pairs={{0,3},{4,7},{8,11},{12,15},{16,19},{20,23},{24,27},{28,31},{32,35}... | collective-permute-start | bytes 442376 | tf_op jit(solution)/shard_map/ppermute | solution.py:231
  152.1 16.7 %all-to-all-start.6 = ((f32[32,4,256]{2,1,0:T(4,128)}), f32[32,4,256]{2,1,0:T(4,128)S(1)}, u32[]{:S(2)}, u32[]{:S(2)}) async-start(f32[32,4,256]{2,1,0:T(4,128)} %broadcast_in_dim.8), calls=%async_computation.6 | async-start | bytes 262144 | tf_op jit(solution)/shard_map/all_to_all | solution.py:23
  176.2 3.4 %collective-permute-start.4 = (f32[16,768]{1,0:T(8,128)S(1)}, f32[16,768]{1,0:T(8,128)S(1)}, u32[]{:S(2)}, u32[]{:S(2)}) collective-permute-start(f32[16,768]{1,0:T(8,128)S(1)} %constant_dynamic-slice_fusion), channel_id=1, source_target_pairs={{0,4},{4,0},{1,5},{5,1},{2,6},{6,2},{3,7},{7,3},{8,12},{12,8},{9,1... | collective-permute-start | bytes 147464 | tf_op jit(solution)/shard_map/ppermute | solution.py:27
Sparse Core Ops, SparseCore 0:
  11.7 129.5 all-gather.2

commit v6 on v5

--- a/solution.py
+++ b/solution.py
@@ -217,7 +217,7 @@
     core = jnp.sum(spread(core, "z", NZ), axis=0)
 
     pair = 2 * rows
-    start = offset - rows * c + nothing(core_y)
+    start = offset - rows * c + nothing(core)
     block = lax.dynamic_slice(plane, (0, start // LANES * LANES), (plane.shape[0], LANES))
     place = (lax.broadcasted_iota(jnp.int32, (LANES, pair), 0) == start % LANES + lax.broadcasted_iota(jnp.int32, (LANES, pair), 1))
     place = (place & (x == owner)).astype(BF16)
@@ -233,7 +233,7 @@
     factor_new = decay_rate * factor + scatter_core(outer_sum, c)
 
     core = join(spread(core, ("x", "y"), NX * NY))
-    core = after(core, outer_sum)
+    core = after(core, picked)
     core = lax.all_gather(core, "c", axis=0, tiled=True)
 
     projected_core = dot(dot(inverse, core, 1, 0), inverse, 1, 1) / B

time: 188 us -> 188 us (level)
  blocking collectives: 52.3 us -> 50.2 us
    all_gather x1, blocking collectives: 6.91 us -> 4.81 us  [shards(): core = lax.all_gather(core, 'c', axis=0, tiled=True)]
  transfers between devices with their start and end apart: 12 -> 12, of which waited for: 6 -> 5; matrix products, arithmetic and copies ran while one was open for 7% -> 6% of each run, Pallas kernels for 5% -> 5%
where the time goes in v6:
time: 188 us
  starting transfers between devices  50.8 us (27%)
  blocking collectives  50.2 us (27%)
  waiting for transfers between devices  44.7 us (24%)
  between operations  15.7 us (8%)
  Pallas kernels  12.3 us (7%)
  matrix products  7.75 us (4%)
  local copies, waits for them, and re-layouts  4.16 us (2%)
    all_to_all x1, blocking collectives, scatter(): lax.all_to_all(v.reshape(n, v.shape[0] // n, v.shape[1]), axis, 0, 0)  36.2 us
    all_to_all x3, waiting for transfers between devices, spread(): return lax.all_to_all(jnp.broadcast_to(v[None], (n,) + v.shape), axis, 0, 0)  29 us
    all_to_all x3, starting transfers between devices, spread(): return lax.all_to_all(jnp.broadcast_to(v[None], (n,) + v.shape), axis, 0, 0)  18.2 us
    ppermute x2, starting transfers between devices, swap_core(): return lax.ppermute(v, 'c', [(0, 1), (1, 0)])  14.3 us
    all_to_all x1, waiting for transfers between devices, shards(): lax.all_to_all(middle(at, ranged, gradient.T, factor), 'x', 0, 0)  10.2 us
    pallas_call x1, Pallas kernels, inverse_factor(): pl.pallas_call(inverse_kernel, out_shape=jax.ShapeDtypeStruct((R, R), F32...  7.65 us
    ppermute x3, starting transfers between devices, shards(): total = total + lax.ppermute(picked, ALL, pairs)  6.61 us
    all_gather x1, blocking collectives, shards(): ranged = lax.all_gather(piece, 'c', axis=0, tiled=True)  6.25 us
  transfers between devices with their start and end apart: 12, of which 5 were waited for; matrix products, arithmetic and copies ran while one was open for 6% of the time, Pallas kernels for 5%

profile of v6, /device:TPU:1, one launch (start us, length us, event | category | flops | bytes accessed | tf_op | source)
XLA Modules:
  0.0 187.5 jit_solution(4648487843722023466)
XLA Ops:
  7.2 2.1 %shard_map.58 = (f32[4,36,256]{2,1,0:T(8,128)}, bf16[24,768]{1,0:T(8,128)(2,1)}) custom-call(bf16[20,768]{1,0:T(8,128)(2,1)} %bitcast.21, f32[16,768]{1,0:T(8,128)} %factor_ref.1, s32[768,256]{1,0:T(8,128)} %sketch_hbm.1), custom_call_target="tpu_custom_call" | custom-call | flops 100000000 | bytes 4000000 | tf_op jit(solution)/shard_map/pallas_call | solution.py:142
  9.4 4.9 %all-to-all-start = ((f32[4,36,256]{2,1,0:T(8,128)}), f32[4,36,256]{2,1,0:T(8,128)S(1)}, u32[]{:S(2)}, u32[]{:S(2)}) async-start(f32[4,36,256]{2,1,0:T(8,128)} %get-tuple-element.5), calls=%async_computation | async-start | bytes 327680 | tf_op jit(solution)/shard_map/all_to_all | solution.py:196
  15.1 4.1 %all-to-all-done = f32[4,36,256]{2,1,0:T(8,128)S(1)} async-done(((f32[4,36,256]{2,1,0:T(8,128)}), f32[4,36,256]{2,1,0:T(8,128)S(1)}, u32[]{:S(2)}, u32[]{:S(2)}) %all-to-all-start) | async-done | bytes 147488 | tf_op jit(solution)/shard_map/all_to_all | solution.py:196
  20.1 12.0 %collective-permute-start = (f32[384,256]{1,0:T(8,128)S(1)}, f32[384,256]{1,0:T(8,128)S(1)}, u32[]{:S(2)}, u32[]{:S(2)}) collective-permute-start(f32[384,256]{1,0:T(8,128)S(1)} %constant_dynamic-slice_fusion.2), channel_id=1, source_target_pairs={{0,4},{4,0},{1,5},{5,1},{2,6},{6,2},{3,7},{7,3},{8,12},{12,8},{9,1... | collective-permute-start | bytes 1179656 | tf_op jit(solution)/shard_map/ppermute | solution.py:27
  32.2 1.3 collective-permute-done
  33.7 36.2 %all_to_all.35 = f32[96,4,256]{2,1,0:T(4,128)S(1)} all-to-all(f32[96,4,256]{2,1,0:T(4,128)S(1)} %reshape.42), channel_id=1, replica_groups=mesh['z'=12,'y'=8,'c'=2,'x'=4] {'z','y'}, dimensions={0} | all-to-all | bytes 786432 | tf_op jit(solution)/shard_map/all_to_all | solution.py:38
  70.9 7.0 %all-to-all-start.2 = ((f32[96,4,256]{2,1,0:T(4,128)}), f32[96,4,256]{2,1,0:T(4,128)S(1)}, u32[]{:S(2)}, u32[]{:S(2)}) async-start(f32[96,4,256]{2,1,0:T(4,128)} %broadcast_in_dim.6), calls=%async_computation.2 | async-start | bytes 786432 | tf_op jit(solution)/shard_map/all_to_all | solution.py:23
  78.0 20.5 %all-to-all-done.2 = f32[96,4,256]{2,1,0:T(4,128)S(1)} async-done(((f32[96,4,256]{2,1,0:T(4,128)}), f32[96,4,256]{2,1,0:T(4,128)S(1)}, u32[]{:S(2)}, u32[]{:S(2)}) %all-to-all-start.2) | async-done | bytes 393248 | tf_op jit(solution)/shard_map/all_to_all | solution.py:23
  98.6 6.3 %all_gather.15.ranged_ref = f32[768,256]{1,0:T(8,128)S(1)} all-gather(f32[384,256]{1,0:T(8,128)S(1)} %reshape.43), channel_id=1, replica_groups=mesh['z'=12,'y'=8,'c'=2,'x'=4] {'c'}, dimensions={0}, use_global_device_ids=true | all-gather | bytes 1179648 | tf_op jit(solution)/shard_map/all_gather | solution.py:202
  104.8 2.5 %shard_map.59 = f32[4,148,256]{2,1,0:T(8,128)} custom-call(s32[3]{0:T(128)S(1)} %pad_add_fusion.at_ref, f32[768,256]{1,0:T(8,128)S(1)} %all_gather.15.ranged_ref, bf16[20,768]{1,0:T(8,128)(2,1)S(1)} %bitcast.22, f32[16,768]{1,0:T(8,128)S(1)} %copy-done), custom_call_target="tpu_custom_call" | custom-call | flops 100000000 | bytes 4000000 | tf_op jit(solution)/shard_map/pallas_call | solution.py:176
  107.4 3.5 %all-to-all-start.3 = ((f32[4,148,256]{2,1,0:T(8,128)}), f32[4,148,256]{2,1,0:T(8,128)S(1)}, u32[]{:S(2)}, u32[]{:S(2)}) async-start(f32[4,148,256]{2,1,0:T(8,128)} %shard_map.59), calls=%async_computation.3 | async-start | bytes 1245184 | tf_op jit(solution)/shard_map/all_to_all | solution.py:206
  110.9 10.2 %all-to-all-done.3 = f32[4,148,256]{2,1,0:T(8,128)S(1)} async-done(((f32[4,148,256]{2,1,0:T(8,128)}), f32[4,148,256]{2,1,0:T(8,128)S(1)}, u32[]{:S(2)}, u32[]{:S(2)}) %all-to-all-start.3) | async-done | bytes 606240 | tf_op jit(solution)/shard_map/all_to_all | solution.py:206
  121.7 2.9 %all-gather = f32[320,256]{1,0:T(8,128)S(1)} all-gather(f32[160,256]{1,0:T(8,128)S(1)} %pad_maximum_fusion), channel_id=2, replica_groups=mesh['z'=12,'y'=8,'c'=2,'x'=4] {'c'}, dimensions={0}, use_global_device_ids=true | all-gather | bytes 491520 | tf_op jit(solution)/shard_map/all_gather | solution.py:212
  125.2 3.3 %all-to-all-start.4 = ((f32[8,4,256]{2,1,0:T(4,128)}), f32[8,4,256]{2,1,0:T(4,128)S(1)}, u32[]{:S(2)}, u32[]{:S(2)}) async-start(f32[8,4,256]{2,1,0:T(4,128)} %reshape.46), calls=%async_computation.4 | async-start | bytes 65536 | tf_op jit(solution)/shard_map/all_to_all | solution.py:38
  128.6 7.7 %shard_map.60 = f32[256,256]{1,0:T(8,128)S(1)} custom-call(f32[2,160,256]{2,1,0:T(8,128)S(1)} %bitcast.20, f32[32,256]{1,0:T(8,128)S(1)} %bitcast.23), custom_call_target="tpu_custom_call" | custom-call | flops 100000000 | bytes 30000000 | tf_op jit(solution)/shard_map/pallas_call | solution.py:107
  136.9 3.7 %all-to-all-start.5 = ((f32[12,4,256]{2,1,0:T(4,128)}), f32[12,4,256]{2,1,0:T(4,128)S(1)}, u32[]{:S(2)}, u32[]{:S(2)}) async-start(f32[12,4,256]{2,1,0:T(4,128)} %broadcast_in_dim.7), calls=%async_computation.5 | async-start | bytes 98304 | tf_op jit(solution)/shard_map/all_to_all | solution.py:23
  141.5 8.5 %all-to-all-done.5 = f32[12,4,256]{2,1,0:T(4,128)S(1)} async-done(((f32[12,4,256]{2,1,0:T(4,128)}), f32[12,4,256]{2,1,0:T(4,128)S(1)}, u32[]{:S(2)}, u32[]{:S(2)}) %all-to-all-start.5) | async-done | bytes 49184 | tf_op jit(solution)/shard_map/all_to_all | solution.py:23
  151.9 7.5 %all-to-all-start.6 = ((f32[32,4,256]{2,1,0:T(4,128)}), f32[32,4,256]{2,1,0:T(4,128)S(1)}, u32[]{:S(2)}, u32[]{:S(2)}) async-start(f32[32,4,256]{2,1,0:T(4,128)} %broadcast_in_dim.8), calls=%async_computation.6 | async-start | bytes 262144 | tf_op jit(solution)/shard_map/all_to_all | solution.py:23
  159.5 1.4 convolution_convert_fusion
  161.4 3.1 %collective-permute-start.1 = (bf16[32,2304]{1,0:T(8,128)(2,1)S(1)}, bf16[32,2304]{1,0:T(8,128)(2,1)S(1)}, u32[]{:S(2)}, u32[]{:S(2)}) collective-permute-start(bf16[32,2304]{1,0:T(8,128)(2,1)S(1)} %convolution_convert_fusion), channel_id=1, source_target_pairs={{0,1},{4,5},{8,9},{12,13},{16,17},{20,21},{24,25},{28,29},{32,33},... | collective-permute-start | bytes 442376 | tf_op jit(solution)/shard_map/ppermute | solution.py:231
  164.5 2.2 %collective-permute-start.2 = (bf16[32,2304]{1,0:T(8,128)(2,1)S(1)}, bf16[32,2304]{1,0:T(8,128)(2,1)S(1)}, u32[]{:S(2)}, u32[]{:S(2)}) collective-permute-start(bf16[32,2304]{1,0:T(8,128)(2,1)S(1)} %convolution_convert_fusion), channel_id=1, source_target_pairs={{0,2},{4,6},{8,10},{12,14},{16,18},{20,22},{24,26},{28,30},{32,34}... | collective-permute-start | bytes 442376 | tf_op jit(solution)/shard_map/ppermute | solution.py:231
  168.8 4.8 %all_gather.19 = f32[256,256]{1,0:T(8,128)S(1)} all-gather(f32[128,256]{1,0:T(8,128)S(1)} %add.110), channel_id=1, replica_groups=mesh['z'=12,'y'=8,'c'=2,'x'=4] {'c'}, dimensions={0}, use_global_device_ids=true | all-gather | bytes 393216 | tf_op jit(solution)/shard_map/all_gather | solution.py:237
  174.0 2.7 %fusion.1 = f32[32,768]{1,0:T(8,128)S(1)} fusion(bf16[2304,768]{1,0:T(8,128)(2,1)} %all-gather.3.cloned.1.call-done, bf16[32,2304]{1,0:T(8,128)(2,1)S(1)} %collective-permute-done.3, bf16[32,2304]{1,0:T(8,128)(2,1)S(1)} %collective-permute-done.2, bf16[32,2304]{1,0:T(8,128)(2,1)S(1)} %convolution_convert_fusion, bf16[32,2304]{1,0:T(8,128)(2,1)S(1)} %collective-permute-done.1), kind=kOutput, calls=%fused_computation.5 | convolution fusion | flops 113467392 | bytes 4227072 | tf_op jit(solution)/shard_map/dot_general | solution.py:232
  176.7 2.3 %collective-permute-start.4 = (f32[16,768]{1,0:T(8,128)S(1)}, f32[16,768]{1,0:T(8,128)S(1)}, u32[]{:S(2)}, u32[]{:S(2)}) collective-permute-start(f32[16,768]{1,0:T(8,128)S(1)} %constant_dynamic-slice_fusion), channel_id=1, source_target_pairs={{0,4},{4,0},{1,5},{5,1},{2,6},{6,2},{3,7},{7,3},{8,12},{12,8},{9,1... | collective-permute-start | bytes 147464 | tf_op jit(solution)/shard_map/ppermute | solution.py:27
  (50 shorter events, 11.1 us)
Async XLA Ops:
  7.2 152.3 %all-gather.3.cloned.1.call-start = ((), (), s32[]{:S(2)}) async-start(), calls=%async_computation.7 | async-start | bytes 3575808 | tf_op jit(solution)/shard_map/all_gather | solution.py:194
  9.4 9.9 %all-to-all-start = ((f32[4,36,256]{2,1,0:T(8,128)}), f32[4,36,256]{2,1,0:T(8,128)S(1)}, u32[]{:S(2)}, u32[]{:S(2)}) async-start(f32[4,36,256]{2,1,0:T(8,128)} %get-tuple-element.5), calls=%async_computation | async-start | bytes 327680 | tf_op jit(solution)/shard_map/all_to_all | solution.py:196
  20.1 84.8 %copy-start = (f32[16,768]{1,0:T(8,128)S(1)}, f32[16,768]{1,0:T(8,128)}, u32[]{:S(2)}) copy-start(f32[16,768]{1,0:T(8,128)} %factor_ref.1) | copy-start | bytes 147460
  20.1 84.7 %copy-start.1 = (bf16[768,20]{0,1:T(8,128)(2,1)S(1)}, bf16[768,20]{0,1:T(8,128)(2,1)}, u32[]{:S(2)}) copy-start(bf16[768,20]{0,1:T(8,128)(2,1)} %param.4) | copy-start | bytes 92164
  20.1 13.4 %collective-permute-start = (f32[384,256]{1,0:T(8,128)S(1)}, f32[384,256]{1,0:T(8,128)S(1)}, u32[]{:S(2)}, u32[]{:S(2)}) collective-permute-start(f32[384,256]{1,0:T(8,128)S(1)} %constant_dynamic-slice_fusion.2), channel_id=1, source_target_pairs={{0,4},{4,0},{1,5},{5,1},{2,6},{6,2},{3,7},{7,3},{8,12},{12,8},{9,1... | collective-permute-start | bytes 1179656 | tf_op jit(solution)/shard_map/ppermute | solution.py:27
  70.9 27.6 %all-to-all-start.2 = ((f32[96,4,256]{2,1,0:T(4,128)}), f32[96,4,256]{2,1,0:T(4,128)S(1)}, u32[]{:S(2)}, u32[]{:S(2)}) async-start(f32[96,4,256]{2,1,0:T(4,128)} %broadcast_in_dim.6), calls=%async_computation.2 | async-start | bytes 786432 | tf_op jit(solution)/shard_map/all_to_all | solution.py:23
  107.4 13.7 %all-to-all-start.3 = ((f32[4,148,256]{2,1,0:T(8,128)}), f32[4,148,256]{2,1,0:T(8,128)S(1)}, u32[]{:S(2)}, u32[]{:S(2)}) async-start(f32[4,148,256]{2,1,0:T(8,128)} %shard_map.59), calls=%async_computation.3 | async-start | bytes 1245184 | tf_op jit(solution)/shard_map/all_to_all | solution.py:206
  125.2 11.0 %all-to-all-start.4 = ((f32[8,4,256]{2,1,0:T(4,128)}), f32[8,4,256]{2,1,0:T(4,128)S(1)}, u32[]{:S(2)}, u32[]{:S(2)}) async-start(f32[8,4,256]{2,1,0:T(4,128)} %reshape.46), calls=%async_computation.4 | async-start | bytes 65536 | tf_op jit(solution)/shard_map/all_to_all | solution.py:38
  136.9 13.1 %all-to-all-start.5 = ((f32[12,4,256]{2,1,0:T(4,128)}), f32[12,4,256]{2,1,0:T(4,128)S(1)}, u32[]{:S(2)}, u32[]{:S(2)}) async-start(f32[12,4,256]{2,1,0:T(4,128)} %broadcast_in_dim.7), calls=%async_computation.5 | async-start | bytes 98304 | tf_op jit(solution)/shard_map/all_to_all | solution.py:23
  151.9 16.8 %all-to-all-start.6 = ((f32[32,4,256]{2,1,0:T(4,128)}), f32[32,4,256]{2,1,0:T(4,128)S(1)}, u32[]{:S(2)}, u32[]{:S(2)}) async-start(f32[32,4,256]{2,1,0:T(4,128)} %broadcast_in_dim.8), calls=%async_computation.6 | async-start | bytes 262144 | tf_op jit(solution)/shard_map/all_to_all | solution.py:23
  161.4 12.6 %collective-permute-start.1 = (bf16[32,2304]{1,0:T(8,128)(2,1)S(1)}, bf16[32,2304]{1,0:T(8,128)(2,1)S(1)}, u32[]{:S(2)}, u32[]{:S(2)}) collective-permute-start(bf16[32,2304]{1,0:T(8,128)(2,1)S(1)} %convolution_convert_fusion), channel_id=1, source_target_pairs={{0,1},{4,5},{8,9},{12,13},{16,17},{20,21},{24,25},{28,29},{32,33},... | collective-permute-start | bytes 442376 | tf_op jit(solution)/shard_map/ppermute | solution.py:231
  164.5 9.4 %collective-permute-start.2 = (bf16[32,2304]{1,0:T(8,128)(2,1)S(1)}, bf16[32,2304]{1,0:T(8,128)(2,1)S(1)}, u32[]{:S(2)}, u32[]{:S(2)}) collective-permute-start(bf16[32,2304]{1,0:T(8,128)(2,1)S(1)} %convolution_convert_fusion), channel_id=1, source_target_pairs={{0,2},{4,6},{8,10},{12,14},{16,18},{20,22},{24,26},{28,30},{32,34}... | collective-permute-start | bytes 442376 | tf_op jit(solution)/shard_map/ppermute | solution.py:231
  166.7 7.3 %collective-permute-start.3 = (bf16[32,2304]{1,0:T(8,128)(2,1)S(1)}, bf16[32,2304]{1,0:T(8,128)(2,1)S(1)}, u32[]{:S(2)}, u32[]{:S(2)}) collective-permute-start(bf16[32,2304]{1,0:T(8,128)(2,1)S(1)} %convolution_convert_fusion), channel_id=1, source_target_pairs={{0,3},{4,7},{8,11},{12,15},{16,19},{20,23},{24,27},{28,31},{32,35}... | collective-permute-start | bytes 442376 | tf_op jit(solution)/shard_map/ppermute | solution.py:231
  176.7 3.4 %collective-permute-start.4 = (f32[16,768]{1,0:T(8,128)S(1)}, f32[16,768]{1,0:T(8,128)S(1)}, u32[]{:S(2)}, u32[]{:S(2)}) collective-permute-start(f32[16,768]{1,0:T(8,128)S(1)} %constant_dynamic-slice_fusion), channel_id=1, source_target_pairs={{0,4},{4,0},{1,5},{5,1},{2,6},{6,2},{3,7},{7,3},{8,12},{12,8},{9,1... | collective-permute-start | bytes 147464 | tf_op jit(solution)/shard_map/ppermute | solution.py:27
Sparse Core Ops, SparseCore 0:
  11.7 129.3 all-gather.2

commit v7 on v5

--- a/solution.py
+++ b/solution.py
@@ -191,13 +191,18 @@
     mine = (x == owner).astype(F32)
 
     small, strip = front(gradient.T, factor, sketch_ids)
-    plane = lax.all_gather(strip, ("z", "y"), axis=0, tiled=True)
     grad32 = gradient.astype(F32)
     small = jnp.sum(lax.all_to_all(small, "x", 0, 0), axis=0)
     inner, decayed = small[:gradient.shape[1]], small[gradient.shape[1]:]
     place = (lax.broadcasted_iota(jnp.int32, (cols, rows), 0) == offset + lax.broadcasted_iota(jnp.int32, (cols, rows), 1)).astype(F32)
     partial = dot(jnp.concatenate([grad32, mine * place], axis=1), jnp.concatenate([inner, decayed], axis=0), 1, 0)
-    piece = scatter(scatter_core(partial, c), ("z", "y"), NZ * NY)
+    partial = scatter_core(partial, c)
+    strip = after(strip, partial)
+    strips = [strip]
+    for k in range(1, NY):
+        strips.append(lax.ppermute(strip, "y", [(d, (d + k) % NY) for d in range(NY)]))
+    piece = scatter(partial, ("z", "y"), NZ * NY)
+    plane = lax.all_gather(after(jnp.concatenate(strips, axis=0), piece), "z", axis=0, tiled=True)
     piece = join(spread(piece, ("z", "y"), NZ * NY))
     ranged = lax.all_gather(piece, "c", axis=0, tiled=True)
 

time: 188 us -> 206 us (1.096)
  starting transfers between devices: 49.9 us -> 96.6 us
  blocking collectives: 52.3 us -> 17.9 us
    all_to_all x1 -> x0, blocking collectives: 36.2 us -> none  [scatter(): lax.all_to_all(v.reshape(n, v.shape[0] // n, v.shape[1]), axis, 0, 0)]
    ppermute x0 -> x7, starting transfers between devices: none -> 27.6 us  [shards(): lax.ppermute(strip, 'y', [(d, (d + k) % NY) for d in range(NY)])]
    all_to_all x1 -> x2, starting transfers between devices: 3.34 us -> 17.2 us  [scatter(): lax.all_to_all(v.reshape(n, v.shape[0] // n, v.shape[1]), axis, 0, 0)]
    all_to_all x3, starting transfers between devices: 18.2 us -> 23.7 us  [spread(): return lax.all_to_all(jnp.broadcast_to(v[None], (n,) + v.shape), axis, 0, 0)]
    all_gather x1, blocking collectives: 6.25 us -> 9.76 us  [shards(): ranged = lax.all_gather(piece, 'c', axis=0, tiled=True)]
  transfers between devices with their start and end apart: 12 -> 20, of which waited for: 6 -> 7; matrix products, arithmetic and copies ran while one was open for 7% -> 6% of each run, Pallas kernels for 5% -> 5%
where the time goes in v7:
time: 206 us; the launch traced here: 205 us
  starting transfers between devices  96.6 us (47%)
  waiting for transfers between devices  44.2 us (21%)
  blocking collectives  17.9 us (9%)
  between operations  17.2 us (8%)
  Pallas kernels  12.3 us (6%)
  matrix products  7.76 us (4%)
  local copies, waits for them, and re-layouts  5.97 us (3%)
  other arithmetic  2.64 us (1%)
    ppermute x7, starting transfers between devices, shards(): lax.ppermute(strip, 'y', [(d, (d + k) % NY) for d in range(NY)])  27.6 us
    all_to_all x3, waiting for transfers between devices, spread(): return lax.all_to_all(jnp.broadcast_to(v[None], (n,) + v.shape), axis, 0, 0)  26.9 us
    all_to_all x3, starting transfers between devices, spread(): return lax.all_to_all(jnp.broadcast_to(v[None], (n,) + v.shape), axis, 0, 0)  23.7 us
    all_to_all x2, starting transfers between devices, scatter(): lax.all_to_all(v.reshape(n, v.shape[0] // n, v.shape[1]), axis, 0, 0)  17.2 us
    ppermute x2, starting transfers between devices, swap_core(): return lax.ppermute(v, 'c', [(0, 1), (1, 0)])  14.3 us
    all_to_all x1, waiting for transfers between devices, shards(): lax.all_to_all(middle(at, ranged, gradient.T, factor), 'x', 0, 0)  10.2 us
    all_gather x1, blocking collectives, shards(): ranged = lax.all_gather(piece, 'c', axis=0, tiled=True)  9.76 us
    pallas_call x1, Pallas kernels, inverse_factor(): pl.pallas_call(inverse_kernel, out_shape=jax.ShapeDtypeStruct((R, R), F32...  7.65 us
  transfers between devices with their start and end apart: 20, of which 7 were waited for; matrix products, arithmetic and copies ran while one was open for 6% of the time, Pallas kernels for 5%

profile of v7, /device:TPU:1, one launch (start us, length us, event | category | flops | bytes accessed | tf_op | source)
XLA Modules:
  0.0 204.5 jit_solution(6621871234708222484)
XLA Ops:
  9.3 4.9 %all-to-all-start = ((f32[4,36,256]{2,1,0:T(8,128)}), f32[4,36,256]{2,1,0:T(8,128)S(1)}, u32[]{:S(2)}, u32[]{:S(2)}) async-start(f32[4,36,256]{2,1,0:T(8,128)} %get-tuple-element.5), calls=%async_computation | async-start | bytes 327680 | tf_op jit(solution)/shard_map/all_to_all | solution.py:195
  15.0 4.1 %all-to-all-done = f32[4,36,256]{2,1,0:T(8,128)S(1)} async-done(((f32[4,36,256]{2,1,0:T(8,128)}), f32[4,36,256]{2,1,0:T(8,128)S(1)}, u32[]{:S(2)}, u32[]{:S(2)}) %all-to-all-start) | async-done | bytes 147488 | tf_op jit(solution)/shard_map/all_to_all | solution.py:195
  20.1 12.0 %collective-permute-start = (f32[384,256]{1,0:T(8,128)S(1)}, f32[384,256]{1,0:T(8,128)S(1)}, u32[]{:S(2)}, u32[]{:S(2)}) collective-permute-start(f32[384,256]{1,0:T(8,128)S(1)} %constant_dynamic-slice_fusion.2), channel_id=1, source_target_pairs={{0,4},{4,0},{1,5},{5,1},{2,6},{6,2},{3,7},{7,3},{8,12},{12,8},{9,1... | collective-permute-start | bytes 1179656 | tf_op jit(solution)/shard_map/ppermute | solution.py:27
  34.4 13.7 %all-to-all-start.1 = ((f32[96,4,256]{2,1,0:T(4,128)}), f32[96,4,256]{2,1,0:T(4,128)S(1)}, u32[]{:S(2)}, u32[]{:S(2)}) async-start(f32[96,4,256]{2,1,0:T(4,128)} %reshape.54), calls=%async_computation.1 | async-start | bytes 786432 | tf_op jit(solution)/shard_map/all_to_all | solution.py:38
  49.3 2.7 %collective-permute-start.1 = (bf16[24,768]{1,0:T(8,128)(2,1)S(1)}, bf16[24,768]{1,0:T(8,128)(2,1)S(1)}, u32[]{:S(2)}, u32[]{:S(2)}) collective-permute-start(bf16[24,768]{1,0:T(8,128)(2,1)S(1)} %get-tuple-element.8), channel_id=1, source_target_pairs={{0,8},{8,16},{16,24},{24,32},{32,40},{40,48},{48,56},{56,0},{1,9},... | collective-permute-start | bytes 110600 | tf_op jit(solution)/shard_map/ppermute | solution.py:203
  52.0 4.0 %collective-permute-start.2 = (bf16[24,768]{1,0:T(8,128)(2,1)S(1)}, bf16[24,768]{1,0:T(8,128)(2,1)S(1)}, u32[]{:S(2)}, u32[]{:S(2)}) collective-permute-start(bf16[24,768]{1,0:T(8,128)(2,1)S(1)} %get-tuple-element.8), channel_id=1, source_target_pairs={{0,16},{8,24},{16,32},{24,40},{32,48},{40,56},{48,0},{56,8},{1,17}... | collective-permute-start | bytes 110600 | tf_op jit(solution)/shard_map/ppermute | solution.py:203
  56.0 4.3 %collective-permute-start.3 = (bf16[24,768]{1,0:T(8,128)(2,1)S(1)}, bf16[24,768]{1,0:T(8,128)(2,1)S(1)}, u32[]{:S(2)}, u32[]{:S(2)}) collective-permute-start(bf16[24,768]{1,0:T(8,128)(2,1)S(1)} %get-tuple-element.8), channel_id=1, source_target_pairs={{0,24},{8,32},{16,40},{24,48},{32,56},{40,0},{48,8},{56,16},{1,25}... | collective-permute-start | bytes 110600 | tf_op jit(solution)/shard_map/ppermute | solution.py:203
  60.4 4.0 %collective-permute-start.4 = (bf16[24,768]{1,0:T(8,128)(2,1)S(1)}, bf16[24,768]{1,0:T(8,128)(2,1)S(1)}, u32[]{:S(2)}, u32[]{:S(2)}) collective-permute-start(bf16[24,768]{1,0:T(8,128)(2,1)S(1)} %get-tuple-element.8), channel_id=1, source_target_pairs={{0,32},{8,40},{16,48},{24,56},{32,0},{40,8},{48,16},{56,24},{1,33}... | collective-permute-start | bytes 110600 | tf_op jit(solution)/shard_map/ppermute | solution.py:203
  64.3 4.3 %collective-permute-start.5 = (bf16[24,768]{1,0:T(8,128)(2,1)S(1)}, bf16[24,768]{1,0:T(8,128)(2,1)S(1)}, u32[]{:S(2)}, u32[]{:S(2)}) collective-permute-start(bf16[24,768]{1,0:T(8,128)(2,1)S(1)} %get-tuple-element.8), channel_id=1, source_target_pairs={{0,40},{8,48},{16,56},{24,0},{32,8},{40,16},{48,24},{56,32},{1,41}... | collective-permute-start | bytes 110600 | tf_op jit(solution)/shard_map/ppermute | solution.py:203
  68.7 5.2 %collective-permute-start.6 = (bf16[24,768]{1,0:T(8,128)(2,1)S(1)}, bf16[24,768]{1,0:T(8,128)(2,1)S(1)}, u32[]{:S(2)}, u32[]{:S(2)}) collective-permute-start(bf16[24,768]{1,0:T(8,128)(2,1)S(1)} %get-tuple-element.8), channel_id=1, source_target_pairs={{0,48},{8,56},{16,0},{24,8},{32,16},{40,24},{48,32},{56,40},{1,49}... | collective-permute-start | bytes 110600 | tf_op jit(solution)/shard_map/ppermute | solution.py:203
  73.9 3.1 %collective-permute-start.7 = (bf16[24,768]{1,0:T(8,128)(2,1)S(1)}, bf16[24,768]{1,0:T(8,128)(2,1)S(1)}, u32[]{:S(2)}, u32[]{:S(2)}) collective-permute-start(bf16[24,768]{1,0:T(8,128)(2,1)S(1)} %get-tuple-element.8), channel_id=1, source_target_pairs={{0,56},{8,0},{16,8},{24,16},{32,24},{40,32},{48,40},{56,48},{1,57}... | collective-permute-start | bytes 110600 | tf_op jit(solution)/shard_map/ppermute | solution.py:203
  81.5 12.8 %all-to-all-start.2 = ((f32[96,4,256]{2,1,0:T(4,128)}), f32[96,4,256]{2,1,0:T(4,128)S(1)}, u32[]{:S(2)}, u32[]{:S(2)}) async-start(f32[96,4,256]{2,1,0:T(4,128)} %broadcast_in_dim.6), calls=%async_computation.2 | async-start | bytes 786432 | tf_op jit(solution)/shard_map/all_to_all | solution.py:23
  94.4 19.8 %all-to-all-done.2 = f32[96,4,256]{2,1,0:T(4,128)S(1)} async-done(((f32[96,4,256]{2,1,0:T(4,128)}), f32[96,4,256]{2,1,0:T(4,128)S(1)}, u32[]{:S(2)}, u32[]{:S(2)}) %all-to-all-start.2) | async-done | bytes 393248 | tf_op jit(solution)/shard_map/all_to_all | solution.py:23
  114.3 9.8 %all_gather.15.ranged_ref = f32[768,256]{1,0:T(8,128)S(1)} all-gather(f32[384,256]{1,0:T(8,128)S(1)} %reshape.55), channel_id=1, replica_groups=mesh['z'=12,'y'=8,'c'=2,'x'=4] {'c'}, dimensions={0}, use_global_device_ids=true | all-gather | bytes 1179648 | tf_op jit(solution)/shard_map/all_gather | solution.py:207
  126.6 3.5 %all-to-all-start.3 = ((f32[4,148,256]{2,1,0:T(8,128)}), f32[4,148,256]{2,1,0:T(8,128)S(1)}, u32[]{:S(2)}, u32[]{:S(2)}) async-start(f32[4,148,256]{2,1,0:T(8,128)} %shard_map.59), calls=%async_computation.3 | async-start | bytes 1245184 | tf_op jit(solution)/shard_map/all_to_all | solution.py:211
  130.1 10.2 %all-to-all-done.3 = f32[4,148,256]{2,1,0:T(8,128)S(1)} async-done(((f32[4,148,256]{2,1,0:T(8,128)}), f32[4,148,256]{2,1,0:T(8,128)S(1)}, u32[]{:S(2)}, u32[]{:S(2)}) %all-to-all-start.3) | async-done | bytes 606240 | tf_op jit(solution)/shard_map/all_to_all | solution.py:211
  140.9 2.9 %all-gather = f32[320,256]{1,0:T(8,128)S(1)} all-gather(f32[160,256]{1,0:T(8,128)S(1)} %pad_maximum_fusion), channel_id=2, replica_groups=mesh['z'=12,'y'=8,'c'=2,'x'=4] {'c'}, dimensions={0}, use_global_device_ids=true | all-gather | bytes 491520 | tf_op jit(solution)/shard_map/all_gather | solution.py:217
  144.4 3.5 %all-to-all-start.4 = ((f32[8,4,256]{2,1,0:T(4,128)}), f32[8,4,256]{2,1,0:T(4,128)S(1)}, u32[]{:S(2)}, u32[]{:S(2)}) async-start(f32[8,4,256]{2,1,0:T(4,128)} %reshape.58), calls=%async_computation.4 | async-start | bytes 65536 | tf_op jit(solution)/shard_map/all_to_all | solution.py:38
  148.0 7.7 %shard_map.60 = f32[256,256]{1,0:T(8,128)S(1)} custom-call(f32[2,160,256]{2,1,0:T(8,128)S(1)} %bitcast.22, f32[32,256]{1,0:T(8,128)S(1)} %bitcast.25), custom_call_target="tpu_custom_call" | custom-call | flops 100000000 | bytes 30000000 | tf_op jit(solution)/shard_map/pallas_call | solution.py:107
  157.5 3.5 %all-to-all-start.5 = ((f32[12,4,256]{2,1,0:T(4,128)}), f32[12,4,256]{2,1,0:T(4,128)S(1)}, u32[]{:S(2)}, u32[]{:S(2)}) async-start(f32[12,4,256]{2,1,0:T(4,128)} %broadcast_in_dim.7), calls=%async_computation.5 | async-start | bytes 98304 | tf_op jit(solution)/shard_map/all_to_all | solution.py:23
  162.5 2.8 %collective-permute-start.10 = (bf16[32,2304]{1,0:T(8,128)(2,1)S(1)}, bf16[32,2304]{1,0:T(8,128)(2,1)S(1)}, u32[]{:S(2)}, u32[]{:S(2)}) collective-permute-start(bf16[32,2304]{1,0:T(8,128)(2,1)S(1)} %convolution_convert_fusion), channel_id=1, source_target_pairs={{0,3},{4,7},{8,11},{12,15},{16,19},{20,23},{24,27},{28,31},{32,35}... | collective-permute-start | bytes 442376 | tf_op jit(solution)/shard_map/ppermute | solution.py:236
  171.4 7.4 %all-to-all-start.6 = ((f32[32,4,256]{2,1,0:T(4,128)}), f32[32,4,256]{2,1,0:T(4,128)S(1)}, u32[]{:S(2)}, u32[]{:S(2)}) async-start(f32[32,4,256]{2,1,0:T(4,128)} %broadcast_in_dim.8), calls=%async_computation.6 | async-start | bytes 262144 | tf_op jit(solution)/shard_map/all_to_all | solution.py:23
  182.7 5.3 %all-to-all-done.6 = f32[32,4,256]{2,1,0:T(4,128)S(1)} async-done(((f32[32,4,256]{2,1,0:T(4,128)}), f32[32,4,256]{2,1,0:T(4,128)S(1)}, u32[]{:S(2)}, u32[]{:S(2)}) %all-to-all-start.6) | async-done | bytes 131104 | tf_op jit(solution)/shard_map/all_to_all | solution.py:23
  188.0 5.2 %all_gather.19 = f32[256,256]{1,0:T(8,128)S(1)} all-gather(f32[128,256]{1,0:T(8,128)S(1)} %add.126), channel_id=1, replica_groups=mesh['z'=12,'y'=8,'c'=2,'x'=4] {'c'}, dimensions={0}, use_global_device_ids=true | all-gather | bytes 393216 | tf_op jit(solution)/shard_map/all_gather | solution.py:242
  (78 shorter events, 30.7 us)
Async XLA Ops:
  9.3 40.0 %copy-start.2 = (bf16[24,768]{1,0:T(8,128)(2,1)S(1)}, bf16[24,768]{1,0:T(8,128)(2,1)}, u32[]{:S(2)}) copy-start(bf16[24,768]{1,0:T(8,128)(2,1)} %get-tuple-element.6) | copy-start | bytes 110596
  9.3 9.9 %all-to-all-start = ((f32[4,36,256]{2,1,0:T(8,128)}), f32[4,36,256]{2,1,0:T(8,128)S(1)}, u32[]{:S(2)}, u32[]{:S(2)}) async-start(f32[4,36,256]{2,1,0:T(8,128)} %get-tuple-element.5), calls=%async_computation | async-start | bytes 327680 | tf_op jit(solution)/shard_map/all_to_all | solution.py:195
  20.1 13.4 %collective-permute-start = (f32[384,256]{1,0:T(8,128)S(1)}, f32[384,256]{1,0:T(8,128)S(1)}, u32[]{:S(2)}, u32[]{:S(2)}) collective-permute-start(f32[384,256]{1,0:T(8,128)S(1)} %constant_dynamic-slice_fusion.2), channel_id=1, source_target_pairs={{0,4},{4,0},{1,5},{5,1},{2,6},{6,2},{3,7},{7,3},{8,12},{12,8},{9,1... | collective-permute-start | bytes 1179656 | tf_op jit(solution)/shard_map/ppermute | solution.py:27
  33.5 90.6 %copy-start = (f32[16,768]{1,0:T(8,128)S(1)}, f32[16,768]{1,0:T(8,128)}, u32[]{:S(2)}) copy-start(f32[16,768]{1,0:T(8,128)} %factor_ref.1) | copy-start | bytes 147460
  33.5 90.5 %copy-start.1 = (bf16[768,20]{0,1:T(8,128)(2,1)S(1)}, bf16[768,20]{0,1:T(8,128)(2,1)}, u32[]{:S(2)}) copy-start(bf16[768,20]{0,1:T(8,128)(2,1)} %param.4) | copy-start | bytes 92164
  34.4 44.2 %all-to-all-start.1 = ((f32[96,4,256]{2,1,0:T(4,128)}), f32[96,4,256]{2,1,0:T(4,128)S(1)}, u32[]{:S(2)}, u32[]{:S(2)}) async-start(f32[96,4,256]{2,1,0:T(4,128)} %reshape.54), calls=%async_computation.1 | async-start | bytes 786432 | tf_op jit(solution)/shard_map/all_to_all | solution.py:38
  48.1 113.0 %all-gather.3.cloned.1.call-start = ((), (), s32[]{:S(2)}) async-start(), calls=%async_computation.7 | async-start | bytes 3833856 | tf_op jit(solution)/shard_map/all_gather | solution.py:205
  49.3 19.3 %collective-permute-start.1 = (bf16[24,768]{1,0:T(8,128)(2,1)S(1)}, bf16[24,768]{1,0:T(8,128)(2,1)S(1)}, u32[]{:S(2)}, u32[]{:S(2)}) collective-permute-start(bf16[24,768]{1,0:T(8,128)(2,1)S(1)} %get-tuple-element.8), channel_id=1, source_target_pairs={{0,8},{8,16},{16,24},{24,32},{32,40},{40,48},{48,56},{56,0},{1,9},... | collective-permute-start | bytes 110600 | tf_op jit(solution)/shard_map/ppermute | solution.py:203
  52.0 21.9 %collective-permute-start.2 = (bf16[24,768]{1,0:T(8,128)(2,1)S(1)}, bf16[24,768]{1,0:T(8,128)(2,1)S(1)}, u32[]{:S(2)}, u32[]{:S(2)}) collective-permute-start(bf16[24,768]{1,0:T(8,128)(2,1)S(1)} %get-tuple-element.8), channel_id=1, source_target_pairs={{0,16},{8,24},{16,32},{24,40},{32,48},{40,56},{48,0},{56,8},{1,17}... | collective-permute-start | bytes 110600 | tf_op jit(solution)/shard_map/ppermute | solution.py:203
  56.0 21.0 %collective-permute-start.3 = (bf16[24,768]{1,0:T(8,128)(2,1)S(1)}, bf16[24,768]{1,0:T(8,128)(2,1)S(1)}, u32[]{:S(2)}, u32[]{:S(2)}) collective-permute-start(bf16[24,768]{1,0:T(8,128)(2,1)S(1)} %get-tuple-element.8), channel_id=1, source_target_pairs={{0,24},{8,32},{16,40},{24,48},{32,56},{40,0},{48,8},{56,16},{1,25}... | collective-permute-start | bytes 110600 | tf_op jit(solution)/shard_map/ppermute | solution.py:203
  60.4 16.7 %collective-permute-start.4 = (bf16[24,768]{1,0:T(8,128)(2,1)S(1)}, bf16[24,768]{1,0:T(8,128)(2,1)S(1)}, u32[]{:S(2)}, u32[]{:S(2)}) collective-permute-start(bf16[24,768]{1,0:T(8,128)(2,1)S(1)} %get-tuple-element.8), channel_id=1, source_target_pairs={{0,32},{8,40},{16,48},{24,56},{32,0},{40,8},{48,16},{56,24},{1,33}... | collective-permute-start | bytes 110600 | tf_op jit(solution)/shard_map/ppermute | solution.py:203
  64.3 12.7 %collective-permute-start.5 = (bf16[24,768]{1,0:T(8,128)(2,1)S(1)}, bf16[24,768]{1,0:T(8,128)(2,1)S(1)}, u32[]{:S(2)}, u32[]{:S(2)}) collective-permute-start(bf16[24,768]{1,0:T(8,128)(2,1)S(1)} %get-tuple-element.8), channel_id=1, source_target_pairs={{0,40},{8,48},{16,56},{24,0},{32,8},{40,16},{48,24},{56,32},{1,41}... | collective-permute-start | bytes 110600 | tf_op jit(solution)/shard_map/ppermute | solution.py:203
  68.7 8.4 %collective-permute-start.6 = (bf16[24,768]{1,0:T(8,128)(2,1)S(1)}, bf16[24,768]{1,0:T(8,128)(2,1)S(1)}, u32[]{:S(2)}, u32[]{:S(2)}) collective-permute-start(bf16[24,768]{1,0:T(8,128)(2,1)S(1)} %get-tuple-element.8), channel_id=1, source_target_pairs={{0,48},{8,56},{16,0},{24,8},{32,16},{40,24},{48,32},{56,40},{1,49}... | collective-permute-start | bytes 110600 | tf_op jit(solution)/shard_map/ppermute | solution.py:203
  73.9 4.7 %collective-permute-start.7 = (bf16[24,768]{1,0:T(8,128)(2,1)S(1)}, bf16[24,768]{1,0:T(8,128)(2,1)S(1)}, u32[]{:S(2)}, u32[]{:S(2)}) collective-permute-start(bf16[24,768]{1,0:T(8,128)(2,1)S(1)} %get-tuple-element.8), channel_id=1, source_target_pairs={{0,56},{8,0},{16,8},{24,16},{32,24},{40,32},{48,40},{56,48},{1,57}... | collective-permute-start | bytes 110600 | tf_op jit(solution)/shard_map/ppermute | solution.py:203
  81.5 32.7 %all-to-all-start.2 = ((f32[96,4,256]{2,1,0:T(4,128)}), f32[96,4,256]{2,1,0:T(4,128)S(1)}, u32[]{:S(2)}, u32[]{:S(2)}) async-start(f32[96,4,256]{2,1,0:T(4,128)} %broadcast_in_dim.6), calls=%async_computation.2 | async-start | bytes 786432 | tf_op jit(solution)/shard_map/all_to_all | solution.py:23
  126.6 13.7 %all-to-all-start.3 = ((f32[4,148,256]{2,1,0:T(8,128)}), f32[4,148,256]{2,1,0:T(8,128)S(1)}, u32[]{:S(2)}, u32[]{:S(2)}) async-start(f32[4,148,256]{2,1,0:T(8,128)} %shard_map.59), calls=%async_computation.3 | async-start | bytes 1245184 | tf_op jit(solution)/shard_map/all_to_all | solution.py:211
  144.4 11.2 %all-to-all-start.4 = ((f32[8,4,256]{2,1,0:T(4,128)}), f32[8,4,256]{2,1,0:T(4,128)S(1)}, u32[]{:S(2)}, u32[]{:S(2)}) async-start(f32[8,4,256]{2,1,0:T(4,128)} %reshape.58), calls=%async_computation.4 | async-start | bytes 65536 | tf_op jit(solution)/shard_map/all_to_all | solution.py:38
  157.5 13.2 %all-to-all-start.5 = ((f32[12,4,256]{2,1,0:T(4,128)}), f32[12,4,256]{2,1,0:T(4,128)S(1)}, u32[]{:S(2)}, u32[]{:S(2)}) async-start(f32[12,4,256]{2,1,0:T(4,128)} %broadcast_in_dim.7), calls=%async_computation.5 | async-start | bytes 98304 | tf_op jit(solution)/shard_map/all_to_all | solution.py:23
  162.5 16.3 %collective-permute-start.10 = (bf16[32,2304]{1,0:T(8,128)(2,1)S(1)}, bf16[32,2304]{1,0:T(8,128)(2,1)S(1)}, u32[]{:S(2)}, u32[]{:S(2)}) collective-permute-start(bf16[32,2304]{1,0:T(8,128)(2,1)S(1)} %convolution_convert_fusion), channel_id=1, source_target_pairs={{0,3},{4,7},{8,11},{12,15},{16,19},{20,23},{24,27},{28,31},{32,35}... | collective-permute-start | bytes 442376 | tf_op jit(solution)/shard_map/ppermute | solution.py:236
  165.3 13.5 %collective-permute-start.8 = (bf16[32,2304]{1,0:T(8,128)(2,1)S(1)}, bf16[32,2304]{1,0:T(8,128)(2,1)S(1)}, u32[]{:S(2)}, u32[]{:S(2)}) collective-permute-start(bf16[32,2304]{1,0:T(8,128)(2,1)S(1)} %convolution_convert_fusion), channel_id=1, source_target_pairs={{0,1},{4,5},{8,9},{12,13},{16,17},{20,21},{24,25},{28,29},{32,33},... | collective-permute-start | bytes 442376 | tf_op jit(solution)/shard_map/ppermute | solution.py:236
  166.6 12.2 %collective-permute-start.9 = (bf16[32,2304]{1,0:T(8,128)(2,1)S(1)}, bf16[32,2304]{1,0:T(8,128)(2,1)S(1)}, u32[]{:S(2)}, u32[]{:S(2)}) collective-permute-start(bf16[32,2304]{1,0:T(8,128)(2,1)S(1)} %convolution_convert_fusion), channel_id=1, source_target_pairs={{0,2},{4,6},{8,10},{12,14},{16,18},{20,22},{24,26},{28,30},{32,34}... | collective-permute-start | bytes 442376 | tf_op jit(solution)/shard_map/ppermute | solution.py:236
  171.4 16.5 %all-to-all-start.6 = ((f32[32,4,256]{2,1,0:T(4,128)}), f32[32,4,256]{2,1,0:T(4,128)S(1)}, u32[]{:S(2)}, u32[]{:S(2)}) async-start(f32[32,4,256]{2,1,0:T(4,128)} %broadcast_in_dim.8), calls=%async_computation.6 | async-start | bytes 262144 | tf_op jit(solution)/shard_map/all_to_all | solution.py:23
  193.6 3.4 %collective-permute-start.11 = (f32[16,768]{1,0:T(8,128)S(1)}, f32[16,768]{1,0:T(8,128)S(1)}, u32[]{:S(2)}, u32[]{:S(2)}) collective-permute-start(f32[16,768]{1,0:T(8,128)S(1)} %constant_dynamic-slice_fusion), channel_id=1, source_target_pairs={{0,4},{4,0},{1,5},{5,1},{2,6},{6,2},{3,7},{7,3},{8,12},{12,8},{9,1... | collective-permute-start | bytes 147464 | tf_op jit(solution)/shard_map/ppermute | solution.py:27
Sparse Core Ops, SparseCore 0:
  80.8 67.0 all-gather.2

commit v8 on v6

--- a/solution.py
+++ b/solution.py
@@ -115,7 +115,27 @@
     )(both, after)
 
 
-def front_kernel(grad_hbm, factor_hbm, sketch_hbm, small_ref, strip_ref, grad_ref, factor_ref, sketch_ref, sems):
+def strip_kernel(grad_hbm, strip_ref, grad_ref, sem):
+    copy = pltpu.make_async_copy(grad_hbm, grad_ref, sem)
+    copy.start()
+    copy.wait()
+    grad = grad_ref[...].astype(F32)
+    strip_ref[...] = jnp.concatenate([grad, jnp.zeros((strip_ref.shape[0] - grad.shape[0], grad.shape[1]), F32)], axis=0).astype(BF16)
+
+
+def padded(grad):
+    return pl.pallas_call(
+        strip_kernel,
+        out_shape=jax.ShapeDtypeStruct((24, grad.shape[1]), BF16),
+        in_specs=[pl.BlockSpec(memory_space=pl.ANY)],
+        out_specs=pl.BlockSpec(memory_space=pltpu.VMEM),
+        scratch_shapes=[pltpu.VMEM(grad.shape, BF16), pltpu.SemaphoreType.DMA],
+        compiler_params=pltpu.CompilerParams(vmem_limit_bytes=56 << 20),
+        cost_estimate=pl.CostEstimate(flops=10**5, bytes_accessed=10**5, transcendentals=0),
+    )(grad)
+
+
+def front_kernel(grad_hbm, factor_hbm, sketch_hbm, small_ref, grad_ref, factor_ref, sketch_ref, sems):
     pairs = ((grad_hbm, grad_ref), (factor_hbm, factor_ref), (sketch_hbm, sketch_ref))
     copies = [pltpu.make_async_copy(src, dst, sems.at[i]) for i, (src, dst) in enumerate(pairs)]
     for copy in copies:
@@ -123,7 +143,6 @@
     wide, rows = grad_ref.shape[0], factor_ref.shape[0]
     copies[0].wait()
     grad = grad_ref[...]
-    strip_ref[...] = jnp.concatenate([grad.astype(F32), jnp.zeros((strip_ref.shape[0] - wide, grad.shape[1]), F32)], axis=0).astype(BF16)
     copies[1].wait()
     pieces = jnp.concatenate(split3(factor_ref[...]), axis=0)
     copies[2].wait()
@@ -141,9 +160,9 @@
     whole = pl.BlockSpec(memory_space=pltpu.VMEM)
     return pl.pallas_call(
         front_kernel,
-        out_shape=(jax.ShapeDtypeStruct((NX, wide + rows, cols), F32), jax.ShapeDtypeStruct((24, grad.shape[1]), BF16)),
+        out_shape=jax.ShapeDtypeStruct((NX, wide + rows, cols), F32),
         in_specs=[pl.BlockSpec(memory_space=pl.ANY)] * 3,
-        out_specs=(whole, whole),
+        out_specs=whole,
         scratch_shapes=[pltpu.VMEM(v.shape, v.dtype) for v in (grad, factor, sketch_ids)] + [pltpu.SemaphoreType.DMA((3,))],
         compiler_params=pltpu.CompilerParams(vmem_limit_bytes=56 << 20),
         cost_estimate=pl.CostEstimate(flops=10**8, bytes_accessed=4 * 10**6, transcendentals=0),
@@ -183,6 +202,30 @@
     )(at, ranged, grad, factor)
 
 
+def pick_kernel(at_ref, plane_hbm, after_ref, out_ref, block_ref, sem):
+    start, mine = at_ref[0], at_ref[1]
+    tile = pl.multiple_of((start >> 7) << 7, LANES)
+    copy = pltpu.make_async_copy(plane_hbm.at[:, pl.ds(tile, LANES)], block_ref, sem)
+    copy.start()
+    shape = (out_ref.shape[0], LANES)
+    place = lax.broadcasted_iota(jnp.int32, shape, 1) == (start & 127) + lax.broadcasted_iota(jnp.int32, shape, 0)
+    place = jnp.where(place, mine.astype(F32), 0.0).astype(BF16)
+    copy.wait()
+    out_ref[...] = lax.dot_general(place, block_ref[...], (((1,), (1,)), ((), ())), preferred_element_type=F32).astype(BF16)
+
+
+def pick(at, plane, after, count):
+    return pl.pallas_call(
+        pick_kernel,
+        out_shape=jax.ShapeDtypeStruct((count, plane.shape[0]), BF16),
+        in_specs=[pl.BlockSpec(memory_space=pltpu.SMEM)] + [pl.BlockSpec(memory_space=pl.ANY)] * 2,
+        out_specs=pl.BlockSpec(memory_space=pltpu.VMEM),
+        scratch_shapes=[pltpu.VMEM((plane.shape[0], LANES), BF16), pltpu.SemaphoreType.DMA],
+        compiler_params=pltpu.CompilerParams(vmem_limit_bytes=56 << 20),
+        cost_estimate=pl.CostEstimate(flops=10**8, bytes_accessed=30 * 10**6, transcendentals=0),
+    )(at, plane, after)
+
+
 def shards(factor, gradient, sketch_ids):
     rows, cols = factor.shape
     z, y, c, x = (lax.axis_index(a) for a in ALL)
@@ -190,7 +233,8 @@
     offset = rows * (((z % (NZ // NX)) * NY + y) * NC + c)
     mine = (x == owner).astype(F32)
 
-    small, strip = front(gradient.T, factor, sketch_ids)
+    strip = padded(gradient.T)
+    small = front(gradient.T, factor, sketch_ids)
     plane = lax.all_gather(strip, ("z", "y"), axis=0, tiled=True)
     grad32 = gradient.astype(F32)
     small = jnp.sum(lax.all_to_all(small, "x", 0, 0), axis=0)
@@ -214,14 +258,9 @@
     inverse = inverse_factor(both, core)
     core = core_y = scatter(core, "y", NY)
     range_basis = dot(own_rows, inverse, 1, 1)
-    core = jnp.sum(spread(core, "z", NZ), axis=0)
 
     pair = 2 * rows
-    start = offset - rows * c + nothing(core)
-    block = lax.dynamic_slice(plane, (0, start // LANES * LANES), (plane.shape[0], LANES))
-    place = (lax.broadcasted_iota(jnp.int32, (LANES, pair), 0) == start % LANES + lax.broadcasted_iota(jnp.int32, (LANES, pair), 1))
-    place = (place & (x == owner)).astype(BF16)
-    picked = lax.dot_general(place, block, (((0,), (1,)), ((), ())), preferred_element_type=F32).astype(BF16)
+    picked = pick(jnp.stack([offset - rows * c, (x == owner).astype(jnp.int32)]), plane, core_y, pair)
     total = picked
     for k in range(1, NX):
         pairs = []
@@ -229,12 +268,16 @@
             src = (d // (NY * NC)) // (NZ // NX)
             pairs.append((d * NX + src, d * NX + (src + k) % NX))
         total = total + lax.ppermute(picked, ALL, pairs)
+    core = after(jnp.sum(spread(core, "z", NZ), axis=0), total)
     outer_sum = lax.dot_general(total, plane, (((1,), (0,)), ((), ())), preferred_element_type=F32)
-    factor_new = decay_rate * factor + scatter_core(outer_sum, c)
 
     core = join(spread(core, ("x", "y"), NX * NY))
-    core = after(core, picked)
-    core = lax.all_gather(core, "c", axis=0, tiled=True)
+    other = lax.dynamic_slice_in_dim(outer_sum, (1 - c) * rows, rows, 0)
+    both = lax.all_gather(jnp.concatenate([core] + [other[:, k:k + R] for k in range(0, cols, R)], axis=0), "c", axis=0, tiled=False)
+    core = both[:, :128].reshape(R, R)
+    other = lax.dynamic_index_in_dim(both[:, 128:], 1 - c, 0, keepdims=False)
+    other = jnp.concatenate([other[k:k + rows] for k in range(0, other.shape[0], rows)], axis=1)
+    factor_new = decay_rate * factor + (lax.dynamic_slice_in_dim(outer_sum, c * rows, rows, 0) + other)
 
     projected_core = dot(dot(inverse, core, 1, 0), inverse, 1, 1) / B
     return (factor_new, range_basis, projected_core)

time: 188 us -> 194 us (1.032)
  blocking collectives: 50.2 us -> 54.6 us
  Pallas kernels: 12.3 us -> 16.4 us
    all_gather x1, blocking collectives: 4.81 us -> 9.64 us  [shards(): lax.all_gather(jnp.concatenate([core] + [other[:, k:k + R] for k in range...]
    pallas_call x1 -> x3, Pallas kernels: 2.13 us -> 6.24 us  [the longest x1 2.72 us: pick(): pl.pallas_call(pick_kernel, out_shape=jax.ShapeDtypeStruct((count, plane....]
    all_to_all x3, starting transfers between devices: 18.2 us -> 20.7 us  [spread(): return lax.all_to_all(jnp.broadcast_to(v[None], (n,) + v.shape), axis, 0, 0)]
    ppermute x2 -> x1, starting transfers between devices: 14.3 us -> 12 us  [swap_core(): return lax.ppermute(v, 'c', [(0, 1), (1, 0)])]
  transfers between devices with their start and end apart: 12 -> 11, of which waited for: 5 -> 7; matrix products, arithmetic and copies ran while one was open for 6% -> 5% of each run, Pallas kernels for 5% -> 8%
where the time goes in v8:
time: 194 us; the launch traced here: 193 us
  blocking collectives  54.6 us (28%)
  starting transfers between devices  49.2 us (25%)
  waiting for transfers between devices  43.8 us (23%)
  Pallas kernels  16.4 us (8%)
  between operations  15 us (8%)
  matrix products  6.39 us (3%)
  local copies, waits for them, and re-layouts  3.68 us (2%)
  other arithmetic  3.41 us (2%)
    all_to_all x1, blocking collectives, scatter(): lax.all_to_all(v.reshape(n, v.shape[0] // n, v.shape[1]), axis, 0, 0)  35.6 us
    all_to_all x3, waiting for transfers between devices, spread(): return lax.all_to_all(jnp.broadcast_to(v[None], (n,) + v.shape), axis, 0, 0)  27.4 us
    all_to_all x3, starting transfers between devices, spread(): return lax.all_to_all(jnp.broadcast_to(v[None], (n,) + v.shape), axis, 0, 0)  20.7 us
    ppermute x1, starting transfers between devices, swap_core(): return lax.ppermute(v, 'c', [(0, 1), (1, 0)])  12 us
    all_to_all x1, waiting for transfers between devices, shards(): lax.all_to_all(middle(at, ranged, gradient.T, factor), 'x', 0, 0)  10.2 us
    all_gather x1, blocking collectives, shards(): lax.all_gather(jnp.concatenate([core] + [other[:, k:k + R] for k in range...  9.64 us
    pallas_call x1, Pallas kernels, inverse_factor(): pl.pallas_call(inverse_kernel, out_shape=jax.ShapeDtypeStruct((R, R), F32...  7.66 us
    all_gather x1, blocking collectives, shards(): ranged = lax.all_gather(piece, 'c', axis=0, tiled=True)  6.53 us
  transfers between devices with their start and end apart: 11, of which 7 were waited for; matrix products, arithmetic and copies ran while one was open for 5% of the time, Pallas kernels for 8%

profile of v8, /device:TPU:1, one launch (start us, length us, event | category | flops | bytes accessed | tf_op | source)
XLA Modules:
  0.0 192.6 jit_solution(13437618206601937991)
XLA Ops:
  7.2 1.4 shard_map.58
  8.6 2.1 %shard_map.59 = f32[4,36,256]{2,1,0:T(8,128)} custom-call(bf16[20,768]{1,0:T(8,128)(2,1)} %bitcast.29, f32[16,768]{1,0:T(8,128)} %factor_ref.1, s32[768,256]{1,0:T(8,128)} %sketch_hbm.1), custom_call_target="tpu_custom_call" | custom-call | flops 100000000 | bytes 4000000 | tf_op jit(solution)/shard_map/pallas_call | solution.py:161
  10.8 4.9 %all-to-all-start = ((f32[4,36,256]{2,1,0:T(8,128)}), f32[4,36,256]{2,1,0:T(8,128)S(1)}, u32[]{:S(2)}, u32[]{:S(2)}) async-start(f32[4,36,256]{2,1,0:T(8,128)} %shard_map.59), calls=%async_computation | async-start | bytes 327680 | tf_op jit(solution)/shard_map/all_to_all | solution.py:240
  16.5 4.1 %all-to-all-done = f32[4,36,256]{2,1,0:T(8,128)S(1)} async-done(((f32[4,36,256]{2,1,0:T(8,128)}), f32[4,36,256]{2,1,0:T(8,128)S(1)}, u32[]{:S(2)}, u32[]{:S(2)}) %all-to-all-start) | async-done | bytes 147488 | tf_op jit(solution)/shard_map/all_to_all | solution.py:240
  21.5 12.0 %collective-permute-start = (f32[384,256]{1,0:T(8,128)S(1)}, f32[384,256]{1,0:T(8,128)S(1)}, u32[]{:S(2)}, u32[]{:S(2)}) collective-permute-start(f32[384,256]{1,0:T(8,128)S(1)} %constant_dynamic-slice_fusion.2), channel_id=1, source_target_pairs={{0,4},{4,0},{1,5},{5,1},{2,6},{6,2},{3,7},{7,3},{8,12},{12,8},{9,1... | collective-permute-start | bytes 1179656 | tf_op jit(solution)/shard_map/ppermute | solution.py:27
  33.6 1.3 collective-permute-done
  35.1 35.6 %all_to_all.35 = f32[96,4,256]{2,1,0:T(4,128)S(1)} all-to-all(f32[96,4,256]{2,1,0:T(4,128)S(1)} %reshape.45), channel_id=1, replica_groups=mesh['z'=12,'y'=8,'c'=2,'x'=4] {'z','y'}, dimensions={0} | all-to-all | bytes 786432 | tf_op jit(solution)/shard_map/all_to_all | solution.py:38
  71.6 7.3 %all-to-all-start.2 = ((f32[96,4,256]{2,1,0:T(4,128)}), f32[96,4,256]{2,1,0:T(4,128)S(1)}, u32[]{:S(2)}, u32[]{:S(2)}) async-start(f32[96,4,256]{2,1,0:T(4,128)} %broadcast_in_dim.6), calls=%async_computation.2 | async-start | bytes 786432 | tf_op jit(solution)/shard_map/all_to_all | solution.py:23
  79.1 20.2 %all-to-all-done.2 = f32[96,4,256]{2,1,0:T(4,128)S(1)} async-done(((f32[96,4,256]{2,1,0:T(4,128)}), f32[96,4,256]{2,1,0:T(4,128)S(1)}, u32[]{:S(2)}, u32[]{:S(2)}) %all-to-all-start.2) | async-done | bytes 393248 | tf_op jit(solution)/shard_map/all_to_all | solution.py:23
  99.4 6.5 %all_gather.19.ranged_ref = f32[768,256]{1,0:T(8,128)S(1)} all-gather(f32[384,256]{1,0:T(8,128)S(1)} %reshape.46), channel_id=1, replica_groups=mesh['z'=12,'y'=8,'c'=2,'x'=4] {'c'}, dimensions={0}, use_global_device_ids=true | all-gather | bytes 1179648 | tf_op jit(solution)/shard_map/all_gather | solution.py:246
  106.0 2.5 %shard_map.60 = f32[4,148,256]{2,1,0:T(8,128)} custom-call(s32[3]{0:T(128)S(1)} %pad_add_fusion.1.at_ref, f32[768,256]{1,0:T(8,128)S(1)} %all_gather.19.ranged_ref, bf16[20,768]{1,0:T(8,128)(2,1)S(1)} %bitcast.30, f32[16,768]{1,0:T(8,128)S(1)} %copy-done.1), custom_call_target="tpu_custom_call" | custom-call | flops 100000000 | bytes 4000000 | tf_op jit(solution)/shard_map/pallas_call | solution.py:195
  108.5 3.5 %all-to-all-start.3 = ((f32[4,148,256]{2,1,0:T(8,128)}), f32[4,148,256]{2,1,0:T(8,128)S(1)}, u32[]{:S(2)}, u32[]{:S(2)}) async-start(f32[4,148,256]{2,1,0:T(8,128)} %shard_map.60), calls=%async_computation.3 | async-start | bytes 1245184 | tf_op jit(solution)/shard_map/all_to_all | solution.py:250
  112.0 10.2 %all-to-all-done.3 = f32[4,148,256]{2,1,0:T(8,128)S(1)} async-done(((f32[4,148,256]{2,1,0:T(8,128)}), f32[4,148,256]{2,1,0:T(8,128)S(1)}, u32[]{:S(2)}, u32[]{:S(2)}) %all-to-all-start.3) | async-done | bytes 606240 | tf_op jit(solution)/shard_map/all_to_all | solution.py:250
  122.8 2.9 %all-gather = f32[320,256]{1,0:T(8,128)S(1)} all-gather(f32[160,256]{1,0:T(8,128)S(1)} %pad_maximum_fusion.1), channel_id=2, replica_groups=mesh['z'=12,'y'=8,'c'=2,'x'=4] {'c'}, dimensions={0}, use_global_device_ids=true | all-gather | bytes 491520 | tf_op jit(solution)/shard_map/all_gather | solution.py:256
  126.3 3.3 %all-to-all-start.4 = ((f32[8,4,256]{2,1,0:T(4,128)}), f32[8,4,256]{2,1,0:T(4,128)S(1)}, u32[]{:S(2)}, u32[]{:S(2)}) async-start(f32[8,4,256]{2,1,0:T(4,128)} %reshape.49), calls=%async_computation.4 | async-start | bytes 65536 | tf_op jit(solution)/shard_map/all_to_all | solution.py:38
  130.3 7.7 %shard_map.62 = f32[256,256]{1,0:T(8,128)S(1)} custom-call(f32[2,160,256]{2,1,0:T(8,128)S(1)} %bitcast.27, f32[32,256]{1,0:T(8,128)S(1)} %bitcast.31), custom_call_target="tpu_custom_call" | custom-call | flops 100000000 | bytes 30000000 | tf_op jit(solution)/shard_map/pallas_call | solution.py:107
  138.6 3.7 %all-to-all-start.5 = ((f32[12,4,256]{2,1,0:T(4,128)}), f32[12,4,256]{2,1,0:T(4,128)S(1)}, u32[]{:S(2)}, u32[]{:S(2)}) async-start(f32[12,4,256]{2,1,0:T(4,128)} %broadcast_in_dim.7), calls=%async_computation.5 | async-start | bytes 98304 | tf_op jit(solution)/shard_map/all_to_all | solution.py:23
  142.3 2.7 %shard_map.61 = bf16[32,2304]{1,0:T(8,128)(2,1)} custom-call(s32[2]{0:T(128)} %pad_add_fusion.at_ref, bf16[2304,768]{1,0:T(8,128)(2,1)} %all-gather.4.cloned.1.call-done.plane_hbm, f32[4,256]{1,0:T(4,128)} %copy-done.2), custom_call_target="tpu_custom_call" | custom-call | flops 100000000 | bytes 30000000 | tf_op jit(solution)/shard_map/pallas_call | solution.py:218
  145.1 2.2 %collective-permute-start.1 = (bf16[32,2304]{1,0:T(8,128)(2,1)}, bf16[32,2304]{1,0:T(8,128)(2,1)S(1)}, u32[]{:S(2)}, u32[]{:S(2)}) collective-permute-start(bf16[32,2304]{1,0:T(8,128)(2,1)} %shard_map.61), channel_id=1, source_target_pairs={{0,1},{4,5},{8,9},{12,13},{16,17},{20,21},{24,25},{28,29},{32,33},... | collective-permute-start | bytes 442376 | tf_op jit(solution)/shard_map/ppermute | solution.py:270
  147.3 1.3 collective-permute-start.2
  155.1 9.7 %all-to-all-start.6 = ((f32[32,4,256]{2,1,0:T(4,128)}), f32[32,4,256]{2,1,0:T(4,128)S(1)}, u32[]{:S(2)}, u32[]{:S(2)}) async-start(f32[32,4,256]{2,1,0:T(4,128)} %broadcast_in_dim.8), calls=%async_computation.6 | async-start | bytes 262144 | tf_op jit(solution)/shard_map/all_to_all | solution.py:23
  164.7 2.7 %fusion.16 = f32[32,768]{1,0:T(8,128)S(1)} fusion(bf16[32,2304]{1,0:T(8,128)(2,1)S(1)} %add_add_fusion, bf16[2304,768]{1,0:T(8,128)(2,1)} %all-gather.4.cloned.1.call-done.plane_hbm), kind=kOutput, calls=%fused_computation.34 | convolution fusion | flops 113246208 | bytes 3784704 | tf_op jit(solution)/shard_map/dot_general | solution.py:272
  167.5 6.4 %all-to-all-done.6 = f32[32,4,256]{2,1,0:T(4,128)S(1)} async-done(((f32[32,4,256]{2,1,0:T(4,128)}), f32[32,4,256]{2,1,0:T(4,128)S(1)}, u32[]{:S(2)}, u32[]{:S(2)}) %all-to-all-start.6) | async-done | bytes 131104 | tf_op jit(solution)/shard_map/all_to_all | solution.py:23
  174.0 9.6 %all-gather.1 = f32[352,256]{1,0:T(8,128)S(1)} all-gather(f32[176,256]{1,0:T(8,128)S(1)} %pad_maximum_fusion), channel_id=3, replica_groups=mesh['z'=12,'y'=8,'c'=2,'x'=4] {'c'}, dimensions={0}, use_global_device_ids=true | all-gather | bytes 540672 | tf_op jit(solution)/shard_map/all_gather | solution.py:276
  (55 shorter events, 13.6 us)
Async XLA Ops:
  7.2 135.1 %all-gather.4.cloned.1.call-start = ((), (), s32[]{:S(2)}) async-start(), calls=%async_computation.7 | async-start | bytes 3575808 | tf_op jit(solution)/shard_map/all_gather | solution.py:238
  10.8 9.9 %all-to-all-start = ((f32[4,36,256]{2,1,0:T(8,128)}), f32[4,36,256]{2,1,0:T(8,128)S(1)}, u32[]{:S(2)}, u32[]{:S(2)}) async-start(f32[4,36,256]{2,1,0:T(8,128)} %shard_map.59), calls=%async_computation | async-start | bytes 327680 | tf_op jit(solution)/shard_map/all_to_all | solution.py:240
  21.5 84.5 %copy-start = (bf16[768,20]{0,1:T(8,128)(2,1)S(1)}, bf16[768,20]{0,1:T(8,128)(2,1)}, u32[]{:S(2)}) copy-start(bf16[768,20]{0,1:T(8,128)(2,1)} %param.4) | copy-start | bytes 92164
  21.5 84.5 %copy-start.1 = (f32[16,768]{1,0:T(8,128)S(1)}, f32[16,768]{1,0:T(8,128)}, u32[]{:S(2)}) copy-start(f32[16,768]{1,0:T(8,128)} %factor_ref.1) | copy-start | bytes 147460
  21.5 13.4 %collective-permute-start = (f32[384,256]{1,0:T(8,128)S(1)}, f32[384,256]{1,0:T(8,128)S(1)}, u32[]{:S(2)}, u32[]{:S(2)}) collective-permute-start(f32[384,256]{1,0:T(8,128)S(1)} %constant_dynamic-slice_fusion.2), channel_id=1, source_target_pairs={{0,4},{4,0},{1,5},{5,1},{2,6},{6,2},{3,7},{7,3},{8,12},{12,8},{9,1... | collective-permute-start | bytes 1179656 | tf_op jit(solution)/shard_map/ppermute | solution.py:27
  71.6 27.6 %all-to-all-start.2 = ((f32[96,4,256]{2,1,0:T(4,128)}), f32[96,4,256]{2,1,0:T(4,128)S(1)}, u32[]{:S(2)}, u32[]{:S(2)}) async-start(f32[96,4,256]{2,1,0:T(4,128)} %broadcast_in_dim.6), calls=%async_computation.2 | async-start | bytes 786432 | tf_op jit(solution)/shard_map/all_to_all | solution.py:23
  108.5 13.7 %all-to-all-start.3 = ((f32[4,148,256]{2,1,0:T(8,128)}), f32[4,148,256]{2,1,0:T(8,128)S(1)}, u32[]{:S(2)}, u32[]{:S(2)}) async-start(f32[4,148,256]{2,1,0:T(8,128)} %shard_map.60), calls=%async_computation.3 | async-start | bytes 1245184 | tf_op jit(solution)/shard_map/all_to_all | solution.py:250
  126.3 11.6 %all-to-all-start.4 = ((f32[8,4,256]{2,1,0:T(4,128)}), f32[8,4,256]{2,1,0:T(4,128)S(1)}, u32[]{:S(2)}, u32[]{:S(2)}) async-start(f32[8,4,256]{2,1,0:T(4,128)} %reshape.49), calls=%async_computation.4 | async-start | bytes 65536 | tf_op jit(solution)/shard_map/all_to_all | solution.py:38
  138.0 4.4 %copy-start.2 = (f32[4,256]{1,0:T(4,128)}, f32[4,256]{1,0:T(4,128)S(1)}, u32[]{:S(2)}) copy-start(f32[4,256]{1,0:T(4,128)S(1)} %reduce_sum.48.after_ref) | copy-start | bytes 12292
  138.6 13.0 %all-to-all-start.5 = ((f32[12,4,256]{2,1,0:T(4,128)}), f32[12,4,256]{2,1,0:T(4,128)S(1)}, u32[]{:S(2)}, u32[]{:S(2)}) async-start(f32[12,4,256]{2,1,0:T(4,128)} %broadcast_in_dim.7), calls=%async_computation.5 | async-start | bytes 98304 | tf_op jit(solution)/shard_map/all_to_all | solution.py:23
  145.1 6.6 %collective-permute-start.1 = (bf16[32,2304]{1,0:T(8,128)(2,1)}, bf16[32,2304]{1,0:T(8,128)(2,1)S(1)}, u32[]{:S(2)}, u32[]{:S(2)}) collective-permute-start(bf16[32,2304]{1,0:T(8,128)(2,1)} %shard_map.61), channel_id=1, source_target_pairs={{0,1},{4,5},{8,9},{12,13},{16,17},{20,21},{24,25},{28,29},{32,33},... | collective-permute-start | bytes 442376 | tf_op jit(solution)/shard_map/ppermute | solution.py:270
  147.3 4.4 %collective-permute-start.2 = (bf16[32,2304]{1,0:T(8,128)(2,1)}, bf16[32,2304]{1,0:T(8,128)(2,1)S(1)}, u32[]{:S(2)}, u32[]{:S(2)}) collective-permute-start(bf16[32,2304]{1,0:T(8,128)(2,1)} %shard_map.61), channel_id=1, source_target_pairs={{0,2},{4,6},{8,10},{12,14},{16,18},{20,22},{24,26},{28,30},{32,34}... | collective-permute-start | bytes 442376 | tf_op jit(solution)/shard_map/ppermute | solution.py:270
  148.6 3.7 %collective-permute-start.3 = (bf16[32,2304]{1,0:T(8,128)(2,1)}, bf16[32,2304]{1,0:T(8,128)(2,1)S(1)}, u32[]{:S(2)}, u32[]{:S(2)}) collective-permute-start(bf16[32,2304]{1,0:T(8,128)(2,1)} %shard_map.61), channel_id=1, source_target_pairs={{0,3},{4,7},{8,11},{12,15},{16,19},{20,23},{24,27},{28,31},{32,35}... | collective-permute-start | bytes 442376 | tf_op jit(solution)/shard_map/ppermute | solution.py:270
  155.1 18.8 %all-to-all-start.6 = ((f32[32,4,256]{2,1,0:T(4,128)}), f32[32,4,256]{2,1,0:T(4,128)S(1)}, u32[]{:S(2)}, u32[]{:S(2)}) async-start(f32[32,4,256]{2,1,0:T(4,128)} %broadcast_in_dim.8), calls=%async_computation.6 | async-start | bytes 262144 | tf_op jit(solution)/shard_map/all_to_all | solution.py:23
Sparse Core Ops, SparseCore 0:
  11.7 128.6 all-gather.3

commit v9 on v8

--- a/solution.py
+++ b/solution.py
@@ -115,27 +115,7 @@
     )(both, after)
 
 
-def strip_kernel(grad_hbm, strip_ref, grad_ref, sem):
-    copy = pltpu.make_async_copy(grad_hbm, grad_ref, sem)
-    copy.start()
-    copy.wait()
-    grad = grad_ref[...].astype(F32)
-    strip_ref[...] = jnp.concatenate([grad, jnp.zeros((strip_ref.shape[0] - grad.shape[0], grad.shape[1]), F32)], axis=0).astype(BF16)
-
-
-def padded(grad):
-    return pl.pallas_call(
-        strip_kernel,
-        out_shape=jax.ShapeDtypeStruct((24, grad.shape[1]), BF16),
-        in_specs=[pl.BlockSpec(memory_space=pl.ANY)],
-        out_specs=pl.BlockSpec(memory_space=pltpu.VMEM),
-        scratch_shapes=[pltpu.VMEM(grad.shape, BF16), pltpu.SemaphoreType.DMA],
-        compiler_params=pltpu.CompilerParams(vmem_limit_bytes=56 << 20),
-        cost_estimate=pl.CostEstimate(flops=10**5, bytes_accessed=10**5, transcendentals=0),
-    )(grad)
-
-
-def front_kernel(grad_hbm, factor_hbm, sketch_hbm, small_ref, grad_ref, factor_ref, sketch_ref, sems):
+def front_kernel(grad_hbm, factor_hbm, sketch_hbm, small_ref, strip_ref, grad_ref, factor_ref, sketch_ref, sems):
     pairs = ((grad_hbm, grad_ref), (factor_hbm, factor_ref), (sketch_hbm, sketch_ref))
     copies = [pltpu.make_async_copy(src, dst, sems.at[i]) for i, (src, dst) in enumerate(pairs)]
     for copy in copies:
@@ -143,6 +123,7 @@
     wide, rows = grad_ref.shape[0], factor_ref.shape[0]
     copies[0].wait()
     grad = grad_ref[...]
+    strip_ref[...] = jnp.concatenate([grad.astype(F32), jnp.zeros((strip_ref.shape[0] - wide, grad.shape[1]), F32)], axis=0).astype(BF16)
     copies[1].wait()
     pieces = jnp.concatenate(split3(factor_ref[...]), axis=0)
     copies[2].wait()
@@ -160,9 +141,9 @@
     whole = pl.BlockSpec(memory_space=pltpu.VMEM)
     return pl.pallas_call(
         front_kernel,
-        out_shape=jax.ShapeDtypeStruct((NX, wide + rows, cols), F32),
+        out_shape=(jax.ShapeDtypeStruct((NX, wide + rows, cols), F32), jax.ShapeDtypeStruct((24, grad.shape[1]), BF16)),
         in_specs=[pl.BlockSpec(memory_space=pl.ANY)] * 3,
-        out_specs=whole,
+        out_specs=(whole, whole),
         scratch_shapes=[pltpu.VMEM(v.shape, v.dtype) for v in (grad, factor, sketch_ids)] + [pltpu.SemaphoreType.DMA((3,))],
         compiler_params=pltpu.CompilerParams(vmem_limit_bytes=56 << 20),
         cost_estimate=pl.CostEstimate(flops=10**8, bytes_accessed=4 * 10**6, transcendentals=0),
@@ -233,8 +214,7 @@
     offset = rows * (((z % (NZ // NX)) * NY + y) * NC + c)
     mine = (x == owner).astype(F32)
 
-    strip = padded(gradient.T)
-    small = front(gradient.T, factor, sketch_ids)
+    small, strip = front(gradient.T, factor, sketch_ids)
     plane = lax.all_gather(strip, ("z", "y"), axis=0, tiled=True)
     grad32 = gradient.astype(F32)
     small = jnp.sum(lax.all_to_all(small, "x", 0, 0), axis=0)
@@ -258,6 +238,7 @@
     inverse = inverse_factor(both, core)
     core = core_y = scatter(core, "y", NY)
     range_basis = dot(own_rows, inverse, 1, 1)
+    core = after(jnp.sum(spread(core, "z", NZ), axis=0), range_basis)
 
     pair = 2 * rows
     picked = pick(jnp.stack([offset - rows * c, (x == owner).astype(jnp.int32)]), plane, core_y, pair)
@@ -268,7 +249,6 @@
             src = (d // (NY * NC)) // (NZ // NX)
             pairs.append((d * NX + src, d * NX + (src + k) % NX))
         total = total + lax.ppermute(picked, ALL, pairs)
-    core = after(jnp.sum(spread(core, "z", NZ), axis=0), total)
     outer_sum = lax.dot_general(total, plane, (((1,), (0,)), ((), ())), preferred_element_type=F32)
 
     core = join(spread(core, ("x", "y"), NX * NY))

time: 194 us -> 188 us (0.969)
  blocking collectives: 54.6 us -> 50.3 us
  waiting for transfers between devices: 43.8 us -> 46.3 us
    all_gather x1, blocking collectives: 9.64 us -> 4.91 us  [shards(): lax.all_gather(jnp.concatenate([core] + [other[:, k:k + R] for k in range...]
    all_to_all x3, starting transfers between devices: 20.7 us -> 18.2 us  [spread(): return lax.all_to_all(jnp.broadcast_to(v[None], (n,) + v.shape), axis, 0, 0)]
  transfers between devices with their start and end apart: 11 -> 11, of which waited for: 7 -> 7; matrix products, arithmetic and copies ran while one was open for 5% -> 4% of each run, Pallas kernels for 8% -> 7%
where the time goes in v9:
time: 188 us; the launch traced here: 187 us
  blocking collectives  50.3 us (27%)
  starting transfers between devices  48.6 us (26%)
  waiting for transfers between devices  46.3 us (25%)
  Pallas kernels  15 us (8%)
  between operations  15 us (8%)
  matrix products  5.77 us (3%)
  local copies, waits for them, and re-layouts  3.82 us (2%)
  other arithmetic  2.47 us (1%)
    all_to_all x1, blocking collectives, scatter(): lax.all_to_all(v.reshape(n, v.shape[0] // n, v.shape[1]), axis, 0, 0)  36.2 us
    all_to_all x3, waiting for transfers between devices, spread(): return lax.all_to_all(jnp.broadcast_to(v[None], (n,) + v.shape), axis, 0, 0)  28.3 us
    all_to_all x3, starting transfers between devices, spread(): return lax.all_to_all(jnp.broadcast_to(v[None], (n,) + v.shape), axis, 0, 0)  18.2 us
    ppermute x1, starting transfers between devices, swap_core(): return lax.ppermute(v, 'c', [(0, 1), (1, 0)])  12 us
    all_to_all x1, waiting for transfers between devices, shards(): lax.all_to_all(middle(at, ranged, gradient.T, factor), 'x', 0, 0)  10.2 us
    pallas_call x1, Pallas kernels, inverse_factor(): pl.pallas_call(inverse_kernel, out_shape=jax.ShapeDtypeStruct((R, R), F32...  7.66 us
    ppermute x3, starting transfers between devices, shards(): total = total + lax.ppermute(picked, ALL, pairs)  6.62 us
    all_gather x1, blocking collectives, shards(): ranged = lax.all_gather(piece, 'c', axis=0, tiled=True)  6.27 us
  transfers between devices with their start and end apart: 11, of which 7 were waited for; matrix products, arithmetic and copies ran while one was open for 4% of the time, Pallas kernels for 7%

profile of v9, /device:TPU:1, one launch (start us, length us, event | category | flops | bytes accessed | tf_op | source)
XLA Modules:
  0.0 187.4 jit_solution(1712948418638884010)
XLA Ops:
  7.2 2.1 %shard_map.58 = (f32[4,36,256]{2,1,0:T(8,128)}, bf16[24,768]{1,0:T(8,128)(2,1)}) custom-call(bf16[20,768]{1,0:T(8,128)(2,1)} %bitcast.27, f32[16,768]{1,0:T(8,128)} %factor_ref.1, s32[768,256]{1,0:T(8,128)} %sketch_hbm.1), custom_call_target="tpu_custom_call" | custom-call | flops 100000000 | bytes 4000000 | tf_op jit(solution)/shard_map/pallas_call | solution.py:142
  9.4 4.9 %all-to-all-start = ((f32[4,36,256]{2,1,0:T(8,128)}), f32[4,36,256]{2,1,0:T(8,128)S(1)}, u32[]{:S(2)}, u32[]{:S(2)}) async-start(f32[4,36,256]{2,1,0:T(8,128)} %get-tuple-element.6), calls=%async_computation | async-start | bytes 327680 | tf_op jit(solution)/shard_map/all_to_all | solution.py:220
  15.1 4.1 %all-to-all-done = f32[4,36,256]{2,1,0:T(8,128)S(1)} async-done(((f32[4,36,256]{2,1,0:T(8,128)}), f32[4,36,256]{2,1,0:T(8,128)S(1)}, u32[]{:S(2)}, u32[]{:S(2)}) %all-to-all-start) | async-done | bytes 147488 | tf_op jit(solution)/shard_map/all_to_all | solution.py:220
  20.1 12.0 %collective-permute-start = (f32[384,256]{1,0:T(8,128)S(1)}, f32[384,256]{1,0:T(8,128)S(1)}, u32[]{:S(2)}, u32[]{:S(2)}) collective-permute-start(f32[384,256]{1,0:T(8,128)S(1)} %constant_dynamic-slice_fusion.2), channel_id=1, source_target_pairs={{0,4},{4,0},{1,5},{5,1},{2,6},{6,2},{3,7},{7,3},{8,12},{12,8},{9,1... | collective-permute-start | bytes 1179656 | tf_op jit(solution)/shard_map/ppermute | solution.py:27
  32.2 1.3 collective-permute-done
  33.7 36.2 %all_to_all.35 = f32[96,4,256]{2,1,0:T(4,128)S(1)} all-to-all(f32[96,4,256]{2,1,0:T(4,128)S(1)} %reshape.45), channel_id=1, replica_groups=mesh['z'=12,'y'=8,'c'=2,'x'=4] {'z','y'}, dimensions={0} | all-to-all | bytes 786432 | tf_op jit(solution)/shard_map/all_to_all | solution.py:38
  70.9 7.0 %all-to-all-start.2 = ((f32[96,4,256]{2,1,0:T(4,128)}), f32[96,4,256]{2,1,0:T(4,128)S(1)}, u32[]{:S(2)}, u32[]{:S(2)}) async-start(f32[96,4,256]{2,1,0:T(4,128)} %broadcast_in_dim.6), calls=%async_computation.2 | async-start | bytes 786432 | tf_op jit(solution)/shard_map/all_to_all | solution.py:23
  78.0 20.5 %all-to-all-done.2 = f32[96,4,256]{2,1,0:T(4,128)S(1)} async-done(((f32[96,4,256]{2,1,0:T(4,128)}), f32[96,4,256]{2,1,0:T(4,128)S(1)}, u32[]{:S(2)}, u32[]{:S(2)}) %all-to-all-start.2) | async-done | bytes 393248 | tf_op jit(solution)/shard_map/all_to_all | solution.py:23
  98.6 6.3 %all_gather.19.ranged_ref = f32[768,256]{1,0:T(8,128)S(1)} all-gather(f32[384,256]{1,0:T(8,128)S(1)} %reshape.46), channel_id=1, replica_groups=mesh['z'=12,'y'=8,'c'=2,'x'=4] {'c'}, dimensions={0}, use_global_device_ids=true | all-gather | bytes 1179648 | tf_op jit(solution)/shard_map/all_gather | solution.py:226
  104.9 2.5 %shard_map.59 = f32[4,148,256]{2,1,0:T(8,128)} custom-call(s32[3]{0:T(128)S(1)} %pad_add_fusion.1.at_ref, f32[768,256]{1,0:T(8,128)S(1)} %all_gather.19.ranged_ref, bf16[20,768]{1,0:T(8,128)(2,1)S(1)} %bitcast.28, f32[16,768]{1,0:T(8,128)S(1)} %copy-done), custom_call_target="tpu_custom_call" | custom-call | flops 100000000 | bytes 4000000 | tf_op jit(solution)/shard_map/pallas_call | solution.py:176
  107.4 3.5 %all-to-all-start.3 = ((f32[4,148,256]{2,1,0:T(8,128)}), f32[4,148,256]{2,1,0:T(8,128)S(1)}, u32[]{:S(2)}, u32[]{:S(2)}) async-start(f32[4,148,256]{2,1,0:T(8,128)} %shard_map.59), calls=%async_computation.3 | async-start | bytes 1245184 | tf_op jit(solution)/shard_map/all_to_all | solution.py:230
  110.9 10.2 %all-to-all-done.3 = f32[4,148,256]{2,1,0:T(8,128)S(1)} async-done(((f32[4,148,256]{2,1,0:T(8,128)}), f32[4,148,256]{2,1,0:T(8,128)S(1)}, u32[]{:S(2)}, u32[]{:S(2)}) %all-to-all-start.3) | async-done | bytes 606240 | tf_op jit(solution)/shard_map/all_to_all | solution.py:230
  121.7 2.9 %all-gather = f32[320,256]{1,0:T(8,128)S(1)} all-gather(f32[160,256]{1,0:T(8,128)S(1)} %pad_maximum_fusion.1), channel_id=2, replica_groups=mesh['z'=12,'y'=8,'c'=2,'x'=4] {'c'}, dimensions={0}, use_global_device_ids=true | all-gather | bytes 491520 | tf_op jit(solution)/shard_map/all_gather | solution.py:236
  125.2 3.3 %all-to-all-start.4 = ((f32[8,4,256]{2,1,0:T(4,128)}), f32[8,4,256]{2,1,0:T(4,128)S(1)}, u32[]{:S(2)}, u32[]{:S(2)}) async-start(f32[8,4,256]{2,1,0:T(4,128)} %reshape.49), calls=%async_computation.4 | async-start | bytes 65536 | tf_op jit(solution)/shard_map/all_to_all | solution.py:38
  128.6 7.7 %shard_map.61 = f32[256,256]{1,0:T(8,128)S(1)} custom-call(f32[2,160,256]{2,1,0:T(8,128)S(1)} %bitcast.26, f32[32,256]{1,0:T(8,128)S(1)} %bitcast.29), custom_call_target="tpu_custom_call" | custom-call | flops 100000000 | bytes 30000000 | tf_op jit(solution)/shard_map/pallas_call | solution.py:107
  136.9 3.7 %all-to-all-start.5 = ((f32[12,4,256]{2,1,0:T(4,128)}), f32[12,4,256]{2,1,0:T(4,128)S(1)}, u32[]{:S(2)}, u32[]{:S(2)}) async-start(f32[12,4,256]{2,1,0:T(4,128)} %broadcast_in_dim.7), calls=%async_computation.5 | async-start | bytes 98304 | tf_op jit(solution)/shard_map/all_to_all | solution.py:23
  142.2 7.8 %all-to-all-done.5 = f32[12,4,256]{2,1,0:T(4,128)S(1)} async-done(((f32[12,4,256]{2,1,0:T(4,128)}), f32[12,4,256]{2,1,0:T(4,128)S(1)}, u32[]{:S(2)}, u32[]{:S(2)}) %all-to-all-start.5) | async-done | bytes 49184 | tf_op jit(solution)/shard_map/all_to_all | solution.py:23
  150.7 7.6 %all-to-all-start.6 = ((f32[32,4,256]{2,1,0:T(4,128)}), f32[32,4,256]{2,1,0:T(4,128)S(1)}, u32[]{:S(2)}, u32[]{:S(2)}) async-start(f32[32,4,256]{2,1,0:T(4,128)} %broadcast_in_dim.8), calls=%async_computation.6 | async-start | bytes 262144 | tf_op jit(solution)/shard_map/all_to_all | solution.py:23
  158.9 2.7 %shard_map.60 = bf16[32,2304]{1,0:T(8,128)(2,1)} custom-call(s32[2]{0:T(128)} %pad_add_fusion.at_ref, bf16[2304,768]{1,0:T(8,128)(2,1)} %all-gather.4.cloned.1.call-done.plane_hbm, f32[4,256]{1,0:T(4,128)} %copy-done.2), custom_call_target="tpu_custom_call" | custom-call | flops 100000000 | bytes 30000000 | tf_op jit(solution)/shard_map/pallas_call | solution.py:199
  161.6 3.1 %collective-permute-start.1 = (bf16[32,2304]{1,0:T(8,128)(2,1)}, bf16[32,2304]{1,0:T(8,128)(2,1)S(1)}, u32[]{:S(2)}, u32[]{:S(2)}) collective-permute-start(bf16[32,2304]{1,0:T(8,128)(2,1)} %shard_map.60), channel_id=1, source_target_pairs={{0,1},{4,5},{8,9},{12,13},{16,17},{20,21},{24,25},{28,29},{32,33},... | collective-permute-start | bytes 442376 | tf_op jit(solution)/shard_map/ppermute | solution.py:251
  164.8 2.2 %collective-permute-start.2 = (bf16[32,2304]{1,0:T(8,128)(2,1)}, bf16[32,2304]{1,0:T(8,128)(2,1)S(1)}, u32[]{:S(2)}, u32[]{:S(2)}) collective-permute-start(bf16[32,2304]{1,0:T(8,128)(2,1)} %shard_map.60), channel_id=1, source_target_pairs={{0,2},{4,6},{8,10},{12,14},{16,18},{20,22},{24,26},{28,30},{32,34}... | collective-permute-start | bytes 442376 | tf_op jit(solution)/shard_map/ppermute | solution.py:251
  168.3 2.0 %collective-permute-done.2 = bf16[32,2304]{1,0:T(8,128)(2,1)S(1)} collective-permute-done((bf16[32,2304]{1,0:T(8,128)(2,1)}, bf16[32,2304]{1,0:T(8,128)(2,1)S(1)}, u32[]{:S(2)}, u32[]{:S(2)}) %collective-permute-start.2) | collective-permute-done | bytes 147488 | tf_op jit(solution)/shard_map/ppermute | solution.py:251
  170.6 2.8 %fusion = f32[32,768]{1,0:T(8,128)S(1)} fusion(bf16[2304,768]{1,0:T(8,128)(2,1)} %all-gather.4.cloned.1.call-done.plane_hbm, bf16[32,2304]{1,0:T(8,128)(2,1)S(1)} %collective-permute-done.3, bf16[32,2304]{1,0:T(8,128)(2,1)S(1)} %collective-permute-done.2, bf16[32,2304]{1,0:T(8,128)(2,1)} %shard_map.60, bf16[32,2304]{1,0:T(8,128)(2,1)S(1)} %collective-permute-done.1), kind=kOutput, calls=%fused_computation.4 | convolution fusion | flops 113467392 | bytes 4227072 | tf_op jit(solution)/shard_map/dot_general | solution.py:252
  173.4 4.9 %all-gather.1 = f32[352,256]{1,0:T(8,128)S(1)} all-gather(f32[176,256]{1,0:T(8,128)S(1)} %pad_maximum_fusion), channel_id=3, replica_groups=mesh['z'=12,'y'=8,'c'=2,'x'=4] {'c'}, dimensions={0}, use_global_device_ids=true | all-gather | bytes 540672 | tf_op jit(solution)/shard_map/all_gather | solution.py:256
  (55 shorter events, 11.0 us)
Async XLA Ops:
  7.2 151.7 %all-gather.4.cloned.1.call-start = ((), (), s32[]{:S(2)}) async-start(), calls=%async_computation.7 | async-start | bytes 3575808 | tf_op jit(solution)/shard_map/all_gather | solution.py:218
  9.4 9.9 %all-to-all-start = ((f32[4,36,256]{2,1,0:T(8,128)}), f32[4,36,256]{2,1,0:T(8,128)S(1)}, u32[]{:S(2)}, u32[]{:S(2)}) async-start(f32[4,36,256]{2,1,0:T(8,128)} %get-tuple-element.6), calls=%async_computation | async-start | bytes 327680 | tf_op jit(solution)/shard_map/all_to_all | solution.py:220
  20.1 84.8 %copy-start = (f32[16,768]{1,0:T(8,128)S(1)}, f32[16,768]{1,0:T(8,128)}, u32[]{:S(2)}) copy-start(f32[16,768]{1,0:T(8,128)} %factor_ref.1) | copy-start | bytes 147460
  20.1 84.8 %copy-start.1 = (bf16[768,20]{0,1:T(8,128)(2,1)S(1)}, bf16[768,20]{0,1:T(8,128)(2,1)}, u32[]{:S(2)}) copy-start(bf16[768,20]{0,1:T(8,128)(2,1)} %param.4) | copy-start | bytes 92164
  20.1 13.4 %collective-permute-start = (f32[384,256]{1,0:T(8,128)S(1)}, f32[384,256]{1,0:T(8,128)S(1)}, u32[]{:S(2)}, u32[]{:S(2)}) collective-permute-start(f32[384,256]{1,0:T(8,128)S(1)} %constant_dynamic-slice_fusion.2), channel_id=1, source_target_pairs={{0,4},{4,0},{1,5},{5,1},{2,6},{6,2},{3,7},{7,3},{8,12},{12,8},{9,1... | collective-permute-start | bytes 1179656 | tf_op jit(solution)/shard_map/ppermute | solution.py:27
  70.9 27.6 %all-to-all-start.2 = ((f32[96,4,256]{2,1,0:T(4,128)}), f32[96,4,256]{2,1,0:T(4,128)S(1)}, u32[]{:S(2)}, u32[]{:S(2)}) async-start(f32[96,4,256]{2,1,0:T(4,128)} %broadcast_in_dim.6), calls=%async_computation.2 | async-start | bytes 786432 | tf_op jit(solution)/shard_map/all_to_all | solution.py:23
  107.4 13.7 %all-to-all-start.3 = ((f32[4,148,256]{2,1,0:T(8,128)}), f32[4,148,256]{2,1,0:T(8,128)S(1)}, u32[]{:S(2)}, u32[]{:S(2)}) async-start(f32[4,148,256]{2,1,0:T(8,128)} %shard_map.59), calls=%async_computation.3 | async-start | bytes 1245184 | tf_op jit(solution)/shard_map/all_to_all | solution.py:230
  125.2 11.0 %all-to-all-start.4 = ((f32[8,4,256]{2,1,0:T(4,128)}), f32[8,4,256]{2,1,0:T(4,128)S(1)}, u32[]{:S(2)}, u32[]{:S(2)}) async-start(f32[8,4,256]{2,1,0:T(4,128)} %reshape.49), calls=%async_computation.4 | async-start | bytes 65536 | tf_op jit(solution)/shard_map/all_to_all | solution.py:38
  136.3 22.6 %copy-start.2 = (f32[4,256]{1,0:T(4,128)}, f32[4,256]{1,0:T(4,128)S(1)}, u32[]{:S(2)}) copy-start(f32[4,256]{1,0:T(4,128)S(1)} %reduce_sum.48.after_ref) | copy-start | bytes 12292
  136.9 13.1 %all-to-all-start.5 = ((f32[12,4,256]{2,1,0:T(4,128)}), f32[12,4,256]{2,1,0:T(4,128)S(1)}, u32[]{:S(2)}, u32[]{:S(2)}) async-start(f32[12,4,256]{2,1,0:T(4,128)} %broadcast_in_dim.7), calls=%async_computation.5 | async-start | bytes 98304 | tf_op jit(solution)/shard_map/all_to_all | solution.py:23
  140.9 32.5 %copy-start.3 = (f32[16,256]{1,0:T(8,128)}, f32[16,256]{1,0:T(8,128)S(1)}, u32[]{:S(2)}) copy-start(f32[16,256]{1,0:T(8,128)S(1)} %fusion.15) | copy-start | bytes 49156
  150.7 17.5 %all-to-all-start.6 = ((f32[32,4,256]{2,1,0:T(4,128)}), f32[32,4,256]{2,1,0:T(4,128)S(1)}, u32[]{:S(2)}, u32[]{:S(2)}) async-start(f32[32,4,256]{2,1,0:T(4,128)} %broadcast_in_dim.8), calls=%async_computation.6 | async-start | bytes 262144 | tf_op jit(solution)/shard_map/all_to_all | solution.py:23
  161.6 6.7 %collective-permute-start.1 = (bf16[32,2304]{1,0:T(8,128)(2,1)}, bf16[32,2304]{1,0:T(8,128)(2,1)S(1)}, u32[]{:S(2)}, u32[]{:S(2)}) collective-permute-start(bf16[32,2304]{1,0:T(8,128)(2,1)} %shard_map.60), channel_id=1, source_target_pairs={{0,1},{4,5},{8,9},{12,13},{16,17},{20,21},{24,25},{28,29},{32,33},... | collective-permute-start | bytes 442376 | tf_op jit(solution)/shard_map/ppermute | solution.py:251
  164.8 5.6 %collective-permute-start.2 = (bf16[32,2304]{1,0:T(8,128)(2,1)}, bf16[32,2304]{1,0:T(8,128)(2,1)S(1)}, u32[]{:S(2)}, u32[]{:S(2)}) collective-permute-start(bf16[32,2304]{1,0:T(8,128)(2,1)} %shard_map.60), channel_id=1, source_target_pairs={{0,2},{4,6},{8,10},{12,14},{16,18},{20,22},{24,26},{28,30},{32,34}... | collective-permute-start | bytes 442376 | tf_op jit(solution)/shard_map/ppermute | solution.py:251
  166.9 3.7 %collective-permute-start.3 = (bf16[32,2304]{1,0:T(8,128)(2,1)}, bf16[32,2304]{1,0:T(8,128)(2,1)S(1)}, u32[]{:S(2)}, u32[]{:S(2)}) collective-permute-start(bf16[32,2304]{1,0:T(8,128)(2,1)} %shard_map.60), channel_id=1, source_target_pairs={{0,3},{4,7},{8,11},{12,15},{16,19},{20,23},{24,27},{28,31},{32,35}... | collective-permute-start | bytes 442376 | tf_op jit(solution)/shard_map/ppermute | solution.py:251
Sparse Core Ops, SparseCore 0:
  11.7 129.1 all-gather.3

commit v10 on v6

--- a/solution.py
+++ b/solution.py
@@ -214,10 +214,10 @@
     inverse = inverse_factor(both, core)
     core = core_y = scatter(core, "y", NY)
     range_basis = dot(own_rows, inverse, 1, 1)
-    core = jnp.sum(spread(core, "z", NZ), axis=0)
+    core = after(jnp.sum(spread(core, "z", NZ), axis=0), range_basis)
 
     pair = 2 * rows
-    start = offset - rows * c + nothing(core)
+    start = offset - rows * c + nothing(range_basis)
     block = lax.dynamic_slice(plane, (0, start // LANES * LANES), (plane.shape[0], LANES))
     place = (lax.broadcasted_iota(jnp.int32, (LANES, pair), 0) == start % LANES + lax.broadcasted_iota(jnp.int32, (LANES, pair), 1))
     place = (place & (x == owner)).astype(BF16)
@@ -230,11 +230,14 @@
             pairs.append((d * NX + src, d * NX + (src + k) % NX))
         total = total + lax.ppermute(picked, ALL, pairs)
     outer_sum = lax.dot_general(total, plane, (((1,), (0,)), ((), ())), preferred_element_type=F32)
-    factor_new = decay_rate * factor + scatter_core(outer_sum, c)
 
     core = join(spread(core, ("x", "y"), NX * NY))
-    core = after(core, picked)
-    core = lax.all_gather(core, "c", axis=0, tiled=True)
+    other = lax.dynamic_slice_in_dim(outer_sum, (1 - c) * rows, rows, 0)
+    both = lax.all_gather(jnp.concatenate([core] + [other[:, k:k + R] for k in range(0, cols, R)], axis=0), "c", axis=0, tiled=False)
+    core = both[:, :128].reshape(R, R)
+    other = lax.dynamic_index_in_dim(both[:, 128:], 1 - c, 0, keepdims=False)
+    other = jnp.concatenate([other[k:k + rows] for k in range(0, other.shape[0], rows)], axis=1)
+    factor_new = decay_rate * factor + (lax.dynamic_slice_in_dim(outer_sum, c * rows, rows, 0) + other)
 
     projected_core = dot(dot(inverse, core, 1, 0), inverse, 1, 1) / B
     return (factor_new, range_basis, projected_core)

time: 188 us -> 186 us (0.989)
  starting transfers between devices: 50.8 us -> 48.6 us
    ppermute x2 -> x1, starting transfers between devices: 14.3 us -> 12 us  [swap_core(): return lax.ppermute(v, 'c', [(0, 1), (1, 0)])]
  transfers between devices with their start and end apart: 12 -> 11, of which waited for: 5 -> 8; matrix products, arithmetic and copies ran while one was open for 6% -> 4% of each run, Pallas kernels for 5% -> 6%
where the time goes in v10:
time: 186 us; the launch traced here: 185 us
  blocking collectives  50.4 us (27%)
  starting transfers between devices  48.6 us (26%)
  waiting for transfers between devices  46.2 us (25%)
  between operations  15 us (8%)
  Pallas kernels  12.3 us (7%)
  matrix products  7.08 us (4%)
  local copies, waits for them, and re-layouts  3.73 us (2%)
  other arithmetic  1.88 us (1%)
    all_to_all x1, blocking collectives, scatter(): lax.all_to_all(v.reshape(n, v.shape[0] // n, v.shape[1]), axis, 0, 0)  36.3 us
    all_to_all x3, waiting for transfers between devices, spread(): return lax.all_to_all(jnp.broadcast_to(v[None], (n,) + v.shape), axis, 0, 0)  29.4 us
    all_to_all x3, starting transfers between devices, spread(): return lax.all_to_all(jnp.broadcast_to(v[None], (n,) + v.shape), axis, 0, 0)  18.2 us
    ppermute x1, starting transfers between devices, swap_core(): return lax.ppermute(v, 'c', [(0, 1), (1, 0)])  12 us
    all_to_all x1, waiting for transfers between devices, shards(): lax.all_to_all(middle(at, ranged, gradient.T, factor), 'x', 0, 0)  10.2 us
    pallas_call x1, Pallas kernels, inverse_factor(): pl.pallas_call(inverse_kernel, out_shape=jax.ShapeDtypeStruct((R, R), F32...  7.66 us
    ppermute x3, starting transfers between devices, shards(): total = total + lax.ppermute(picked, ALL, pairs)  6.63 us
    all_gather x1, blocking collectives, shards(): ranged = lax.all_gather(piece, 'c', axis=0, tiled=True)  6.32 us
  transfers between devices with their start and end apart: 11, of which 8 were waited for; matrix products, arithmetic and copies ran while one was open for 4% of the time, Pallas kernels for 6%

profile of v10, /device:TPU:1, one launch (start us, length us, event | category | flops | bytes accessed | tf_op | source)
XLA Modules:
  0.0 185.2 jit_solution(171642902766404513)
XLA Ops:
  7.2 2.1 %shard_map.58 = (f32[4,36,256]{2,1,0:T(8,128)}, bf16[24,768]{1,0:T(8,128)(2,1)}) custom-call(bf16[20,768]{1,0:T(8,128)(2,1)} %bitcast.26, f32[16,768]{1,0:T(8,128)} %factor_ref.1, s32[768,256]{1,0:T(8,128)} %sketch_hbm.1), custom_call_target="tpu_custom_call" | custom-call | flops 100000000 | bytes 4000000 | tf_op jit(solution)/shard_map/pallas_call | solution.py:142
  9.4 4.9 %all-to-all-start = ((f32[4,36,256]{2,1,0:T(8,128)}), f32[4,36,256]{2,1,0:T(8,128)S(1)}, u32[]{:S(2)}, u32[]{:S(2)}) async-start(f32[4,36,256]{2,1,0:T(8,128)} %get-tuple-element.5), calls=%async_computation | async-start | bytes 327680 | tf_op jit(solution)/shard_map/all_to_all | solution.py:196
  15.1 4.1 %all-to-all-done = f32[4,36,256]{2,1,0:T(8,128)S(1)} async-done(((f32[4,36,256]{2,1,0:T(8,128)}), f32[4,36,256]{2,1,0:T(8,128)S(1)}, u32[]{:S(2)}, u32[]{:S(2)}) %all-to-all-start) | async-done | bytes 147488 | tf_op jit(solution)/shard_map/all_to_all | solution.py:196
  20.2 12.0 %collective-permute-start = (f32[384,256]{1,0:T(8,128)S(1)}, f32[384,256]{1,0:T(8,128)S(1)}, u32[]{:S(2)}, u32[]{:S(2)}) collective-permute-start(f32[384,256]{1,0:T(8,128)S(1)} %constant_dynamic-slice_fusion.2), channel_id=1, source_target_pairs={{0,4},{4,0},{1,5},{5,1},{2,6},{6,2},{3,7},{7,3},{8,12},{12,8},{9,1... | collective-permute-start | bytes 1179656 | tf_op jit(solution)/shard_map/ppermute | solution.py:27
  32.2 1.3 collective-permute-done
  33.7 36.3 %all_to_all.35 = f32[96,4,256]{2,1,0:T(4,128)S(1)} all-to-all(f32[96,4,256]{2,1,0:T(4,128)S(1)} %reshape.44), channel_id=1, replica_groups=mesh['z'=12,'y'=8,'c'=2,'x'=4] {'z','y'}, dimensions={0} | all-to-all | bytes 786432 | tf_op jit(solution)/shard_map/all_to_all | solution.py:38
  71.0 7.0 %all-to-all-start.2 = ((f32[96,4,256]{2,1,0:T(4,128)}), f32[96,4,256]{2,1,0:T(4,128)S(1)}, u32[]{:S(2)}, u32[]{:S(2)}) async-start(f32[96,4,256]{2,1,0:T(4,128)} %broadcast_in_dim.6), calls=%async_computation.2 | async-start | bytes 786432 | tf_op jit(solution)/shard_map/all_to_all | solution.py:23
  78.1 20.4 %all-to-all-done.2 = f32[96,4,256]{2,1,0:T(4,128)S(1)} async-done(((f32[96,4,256]{2,1,0:T(4,128)}), f32[96,4,256]{2,1,0:T(4,128)S(1)}, u32[]{:S(2)}, u32[]{:S(2)}) %all-to-all-start.2) | async-done | bytes 393248 | tf_op jit(solution)/shard_map/all_to_all | solution.py:23
  98.7 6.3 %all_gather.18.ranged_ref = f32[768,256]{1,0:T(8,128)S(1)} all-gather(f32[384,256]{1,0:T(8,128)S(1)} %reshape.45), channel_id=1, replica_groups=mesh['z'=12,'y'=8,'c'=2,'x'=4] {'c'}, dimensions={0}, use_global_device_ids=true | all-gather | bytes 1179648 | tf_op jit(solution)/shard_map/all_gather | solution.py:202
  105.0 2.5 %shard_map.59 = f32[4,148,256]{2,1,0:T(8,128)} custom-call(s32[3]{0:T(128)S(1)} %pad_add_fusion.at_ref, f32[768,256]{1,0:T(8,128)S(1)} %all_gather.18.ranged_ref, bf16[20,768]{1,0:T(8,128)(2,1)S(1)} %bitcast.27, f32[16,768]{1,0:T(8,128)S(1)} %copy-done), custom_call_target="tpu_custom_call" | custom-call | flops 100000000 | bytes 4000000 | tf_op jit(solution)/shard_map/pallas_call | solution.py:176
  107.6 3.5 %all-to-all-start.3 = ((f32[4,148,256]{2,1,0:T(8,128)}), f32[4,148,256]{2,1,0:T(8,128)S(1)}, u32[]{:S(2)}, u32[]{:S(2)}) async-start(f32[4,148,256]{2,1,0:T(8,128)} %shard_map.59), calls=%async_computation.3 | async-start | bytes 1245184 | tf_op jit(solution)/shard_map/all_to_all | solution.py:206
  111.0 10.2 %all-to-all-done.3 = f32[4,148,256]{2,1,0:T(8,128)S(1)} async-done(((f32[4,148,256]{2,1,0:T(8,128)}), f32[4,148,256]{2,1,0:T(8,128)S(1)}, u32[]{:S(2)}, u32[]{:S(2)}) %all-to-all-start.3) | async-done | bytes 606240 | tf_op jit(solution)/shard_map/all_to_all | solution.py:206
  121.8 2.9 %all-gather = f32[320,256]{1,0:T(8,128)S(1)} all-gather(f32[160,256]{1,0:T(8,128)S(1)} %pad_maximum_fusion.1), channel_id=2, replica_groups=mesh['z'=12,'y'=8,'c'=2,'x'=4] {'c'}, dimensions={0}, use_global_device_ids=true | all-gather | bytes 491520 | tf_op jit(solution)/shard_map/all_gather | solution.py:212
  125.4 3.3 %all-to-all-start.4 = ((f32[8,4,256]{2,1,0:T(4,128)}), f32[8,4,256]{2,1,0:T(4,128)S(1)}, u32[]{:S(2)}, u32[]{:S(2)}) async-start(f32[8,4,256]{2,1,0:T(4,128)} %reshape.48), calls=%async_computation.4 | async-start | bytes 65536 | tf_op jit(solution)/shard_map/all_to_all | solution.py:38
  128.7 7.7 %shard_map.60 = f32[256,256]{1,0:T(8,128)S(1)} custom-call(f32[2,160,256]{2,1,0:T(8,128)S(1)} %bitcast.25, f32[32,256]{1,0:T(8,128)S(1)} %bitcast.28), custom_call_target="tpu_custom_call" | custom-call | flops 100000000 | bytes 30000000 | tf_op jit(solution)/shard_map/pallas_call | solution.py:107
  137.1 3.7 %all-to-all-start.5 = ((f32[12,4,256]{2,1,0:T(4,128)}), f32[12,4,256]{2,1,0:T(4,128)S(1)}, u32[]{:S(2)}, u32[]{:S(2)}) async-start(f32[12,4,256]{2,1,0:T(4,128)} %broadcast_in_dim.7), calls=%async_computation.5 | async-start | bytes 98304 | tf_op jit(solution)/shard_map/all_to_all | solution.py:23
  142.3 7.9 %all-to-all-done.5 = f32[12,4,256]{2,1,0:T(4,128)S(1)} async-done(((f32[12,4,256]{2,1,0:T(4,128)}), f32[12,4,256]{2,1,0:T(4,128)S(1)}, u32[]{:S(2)}, u32[]{:S(2)}) %all-to-all-start.5) | async-done | bytes 49184 | tf_op jit(solution)/shard_map/all_to_all | solution.py:23
  150.9 7.5 %all-to-all-start.6 = ((f32[32,4,256]{2,1,0:T(4,128)}), f32[32,4,256]{2,1,0:T(4,128)S(1)}, u32[]{:S(2)}, u32[]{:S(2)}) async-start(f32[32,4,256]{2,1,0:T(4,128)} %broadcast_in_dim.8), calls=%async_computation.6 | async-start | bytes 262144 | tf_op jit(solution)/shard_map/all_to_all | solution.py:23
  158.4 1.4 convolution_convert_fusion
  159.8 3.2 %collective-permute-start.1 = (bf16[32,2304]{1,0:T(8,128)(2,1)S(1)}, bf16[32,2304]{1,0:T(8,128)(2,1)S(1)}, u32[]{:S(2)}, u32[]{:S(2)}) collective-permute-start(bf16[32,2304]{1,0:T(8,128)(2,1)S(1)} %convolution_convert_fusion), channel_id=1, source_target_pairs={{0,1},{4,5},{8,9},{12,13},{16,17},{20,21},{24,25},{28,29},{32,33},... | collective-permute-start | bytes 442376 | tf_op jit(solution)/shard_map/ppermute | solution.py:231
  163.0 2.2 %collective-permute-start.2 = (bf16[32,2304]{1,0:T(8,128)(2,1)S(1)}, bf16[32,2304]{1,0:T(8,128)(2,1)S(1)}, u32[]{:S(2)}, u32[]{:S(2)}) collective-permute-start(bf16[32,2304]{1,0:T(8,128)(2,1)S(1)} %convolution_convert_fusion), channel_id=1, source_target_pairs={{0,2},{4,6},{8,10},{12,14},{16,18},{20,22},{24,26},{28,30},{32,34}... | collective-permute-start | bytes 442376 | tf_op jit(solution)/shard_map/ppermute | solution.py:231
  165.2 1.3 collective-permute-start.3
  168.6 2.7 %fusion.1 = f32[32,768]{1,0:T(8,128)S(1)} fusion(bf16[2304,768]{1,0:T(8,128)(2,1)} %all-gather.4.cloned.1.call-done, bf16[32,2304]{1,0:T(8,128)(2,1)S(1)} %collective-permute-done.3, bf16[32,2304]{1,0:T(8,128)(2,1)S(1)} %collective-permute-done.2, bf16[32,2304]{1,0:T(8,128)(2,1)S(1)} %convolution_convert_fusion, bf16[32,2304]{1,0:T(8,128)(2,1)S(1)} %collective-permute-done.1), kind=kOutput, calls=%fused_computation.6 | convolution fusion | flops 113467392 | bytes 4227072 | tf_op jit(solution)/shard_map/dot_general | solution.py:232
  171.3 4.9 %all-gather.1 = f32[352,256]{1,0:T(8,128)S(1)} all-gather(f32[176,256]{1,0:T(8,128)S(1)} %pad_maximum_fusion), channel_id=3, replica_groups=mesh['z'=12,'y'=8,'c'=2,'x'=4] {'c'}, dimensions={0}, use_global_device_ids=true | all-gather | bytes 540672 | tf_op jit(solution)/shard_map/all_gather | solution.py:236
  (53 shorter events, 10.8 us)
Async XLA Ops:
  7.2 151.2 %all-gather.4.cloned.1.call-start = ((), (), s32[]{:S(2)}) async-start(), calls=%async_computation.7 | async-start | bytes 3575808 | tf_op jit(solution)/shard_map/all_gather | solution.py:194
  9.4 9.9 %all-to-all-start = ((f32[4,36,256]{2,1,0:T(8,128)}), f32[4,36,256]{2,1,0:T(8,128)S(1)}, u32[]{:S(2)}, u32[]{:S(2)}) async-start(f32[4,36,256]{2,1,0:T(8,128)} %get-tuple-element.5), calls=%async_computation | async-start | bytes 327680 | tf_op jit(solution)/shard_map/all_to_all | solution.py:196
  20.1 84.9 %copy-start = (f32[16,768]{1,0:T(8,128)S(1)}, f32[16,768]{1,0:T(8,128)}, u32[]{:S(2)}) copy-start(f32[16,768]{1,0:T(8,128)} %factor_ref.1) | copy-start | bytes 147460
  20.1 84.9 %copy-start.1 = (bf16[768,20]{0,1:T(8,128)(2,1)S(1)}, bf16[768,20]{0,1:T(8,128)(2,1)}, u32[]{:S(2)}) copy-start(bf16[768,20]{0,1:T(8,128)(2,1)} %param.4) | copy-start | bytes 92164
  20.2 13.4 %collective-permute-start = (f32[384,256]{1,0:T(8,128)S(1)}, f32[384,256]{1,0:T(8,128)S(1)}, u32[]{:S(2)}, u32[]{:S(2)}) collective-permute-start(f32[384,256]{1,0:T(8,128)S(1)} %constant_dynamic-slice_fusion.2), channel_id=1, source_target_pairs={{0,4},{4,0},{1,5},{5,1},{2,6},{6,2},{3,7},{7,3},{8,12},{12,8},{9,1... | collective-permute-start | bytes 1179656 | tf_op jit(solution)/shard_map/ppermute | solution.py:27
  71.0 27.6 %all-to-all-start.2 = ((f32[96,4,256]{2,1,0:T(4,128)}), f32[96,4,256]{2,1,0:T(4,128)S(1)}, u32[]{:S(2)}, u32[]{:S(2)}) async-start(f32[96,4,256]{2,1,0:T(4,128)} %broadcast_in_dim.6), calls=%async_computation.2 | async-start | bytes 786432 | tf_op jit(solution)/shard_map/all_to_all | solution.py:23
  107.6 13.7 %all-to-all-start.3 = ((f32[4,148,256]{2,1,0:T(8,128)}), f32[4,148,256]{2,1,0:T(8,128)S(1)}, u32[]{:S(2)}, u32[]{:S(2)}) async-start(f32[4,148,256]{2,1,0:T(8,128)} %shard_map.59), calls=%async_computation.3 | async-start | bytes 1245184 | tf_op jit(solution)/shard_map/all_to_all | solution.py:206
  125.4 11.0 %all-to-all-start.4 = ((f32[8,4,256]{2,1,0:T(4,128)}), f32[8,4,256]{2,1,0:T(4,128)S(1)}, u32[]{:S(2)}, u32[]{:S(2)}) async-start(f32[8,4,256]{2,1,0:T(4,128)} %reshape.48), calls=%async_computation.4 | async-start | bytes 65536 | tf_op jit(solution)/shard_map/all_to_all | solution.py:38
  137.1 13.1 %all-to-all-start.5 = ((f32[12,4,256]{2,1,0:T(4,128)}), f32[12,4,256]{2,1,0:T(4,128)S(1)}, u32[]{:S(2)}, u32[]{:S(2)}) async-start(f32[12,4,256]{2,1,0:T(4,128)} %broadcast_in_dim.7), calls=%async_computation.5 | async-start | bytes 98304 | tf_op jit(solution)/shard_map/all_to_all | solution.py:23
  141.0 35.2 %copy-start.2 = (f32[16,256]{1,0:T(8,128)}, f32[16,256]{1,0:T(8,128)S(1)}, u32[]{:S(2)}) copy-start(f32[16,256]{1,0:T(8,128)S(1)} %fusion.21) | copy-start | bytes 49156
  150.9 16.6 %all-to-all-start.6 = ((f32[32,4,256]{2,1,0:T(4,128)}), f32[32,4,256]{2,1,0:T(4,128)S(1)}, u32[]{:S(2)}, u32[]{:S(2)}) async-start(f32[32,4,256]{2,1,0:T(4,128)} %broadcast_in_dim.8), calls=%async_computation.6 | async-start | bytes 262144 | tf_op jit(solution)/shard_map/all_to_all | solution.py:23
  159.8 7.8 %collective-permute-start.1 = (bf16[32,2304]{1,0:T(8,128)(2,1)S(1)}, bf16[32,2304]{1,0:T(8,128)(2,1)S(1)}, u32[]{:S(2)}, u32[]{:S(2)}) collective-permute-start(bf16[32,2304]{1,0:T(8,128)(2,1)S(1)} %convolution_convert_fusion), channel_id=1, source_target_pairs={{0,1},{4,5},{8,9},{12,13},{16,17},{20,21},{24,25},{28,29},{32,33},... | collective-permute-start | bytes 442376 | tf_op jit(solution)/shard_map/ppermute | solution.py:231
  163.0 5.4 %collective-permute-start.2 = (bf16[32,2304]{1,0:T(8,128)(2,1)S(1)}, bf16[32,2304]{1,0:T(8,128)(2,1)S(1)}, u32[]{:S(2)}, u32[]{:S(2)}) collective-permute-start(bf16[32,2304]{1,0:T(8,128)(2,1)S(1)} %convolution_convert_fusion), channel_id=1, source_target_pairs={{0,2},{4,6},{8,10},{12,14},{16,18},{20,22},{24,26},{28,30},{32,34}... | collective-permute-start | bytes 442376 | tf_op jit(solution)/shard_map/ppermute | solution.py:231
  165.2 3.5 %collective-permute-start.3 = (bf16[32,2304]{1,0:T(8,128)(2,1)S(1)}, bf16[32,2304]{1,0:T(8,128)(2,1)S(1)}, u32[]{:S(2)}, u32[]{:S(2)}) collective-permute-start(bf16[32,2304]{1,0:T(8,128)(2,1)S(1)} %convolution_convert_fusion), channel_id=1, source_target_pairs={{0,3},{4,7},{8,11},{12,15},{16,19},{20,23},{24,27},{28,31},{32,35}... | collective-permute-start | bytes 442376 | tf_op jit(solution)/shard_map/ppermute | solution.py:231
Sparse Core Ops, SparseCore 0:
  11.7 129.5 all-gather.3
